TPU v7x, 32 devices: a whole 2x2x4 slice. The times are simulated.
32 devices in a mesh: grp: 4 (over z), vox: 8 (over y, x, core).
Axes of the slice: x: 2, y: 2, z: 4, core: 2. Of those that a mesh axis runs over, the one named last changes fastest.
Arguments:
- log_modulus: float32 [96, 65536], P('grp', 'vox'), may hold values from -3 to 3
- basis: bfloat16 [1024, 128], replicated, may hold values from -0.1875 to 0.1875
- sensitivity: bfloat16 [8192, 128], P('vox'), may hold values from -0.5 to 0.5
- obs_block: int32 [8192, 1], P('vox'), may hold values from 0 to 63; in each aligned block of 1024 rows (0 to 1023, 1024 to 2047, ...) at most 32 rows name the same one
- observed: float32 [8192], P('vox'), may hold values from -9 to 9
- noise_scale: float32 [8192], P('vox'), may hold values from 0.5 to 2
- perturbation: float32 [96, 8192], P('grp', 'vox'), may hold values from -6 to 6
Outputs:
- updated: float32 [96, 65536], P('grp', 'vox')
Inputs may be any that keep to these rules, and one draw needn't show every extreme that they name: `obs_block`: among the observations of one index of vox (aligned blocks of 1024 rows), no voxel block is read by more than 32 of them, and in every draw some block is read by exactly 32.
All inputs are finite; a program needn't handle non-finite values.
Results may differ from a plain program's by a relative error of at most 0.011.
Values may be sent and summed in bfloat16 or wider, within the bound.
No kernel may reach another device: no remote copies, remote signals or barrier semaphores. Data moves between devices by JAX's collectives and lax.ppermute only.
A program may use at most 64 MiB of HBM per device.

v0:
```python
import math

import jax
import jax.numpy as jnp
from jax import lax
from jax.sharding import PartitionSpec as P


def innovations(predicted, perturb, observed, noise_scale, scale_root):
    centre = jnp.mean(predicted, axis=0)
    scaled = ((predicted - centre) / (noise_scale * scale_root)).astype(jnp.bfloat16)
    misfit = ((observed - predicted) / noise_scale + perturb).astype(jnp.bfloat16)
    return (scaled, misfit)


def pair_sums(scaled, misfit):
    contract = (((1,), (1,)), ((), ()))
    gram_part = lax.dot_general(scaled, scaled, contract, preferred_element_type=jnp.float32)
    cross_part = lax.dot_general(scaled, misfit, contract, preferred_element_type=jnp.float32)
    misfit_wide = misfit.astype(jnp.float32)
    return (gram_part, cross_part, jnp.sum(misfit_wide * misfit_wide))


def on_device(log_modulus, basis, sensitivity, obs_block, observed, noise_scale, perturbation):
    n_vox = lax.axis_size("vox")
    n_grp = lax.axis_size("grp")
    j_dev, vox_dev = log_modulus.shape
    block_vox, feature_width = basis.shape
    blocks_dev = vox_dev // block_vox
    block_count = blocks_dev * n_vox
    obs_dev = sensitivity.shape[0]
    block_slots = max(2, 2 * obs_dev // block_count)
    members = j_dev * n_grp
    scale_root = math.sqrt(members - 1)
    compliance = jnp.exp(-log_modulus).astype(jnp.bfloat16)
    features = jnp.dot(
        compliance.reshape(j_dev * blocks_dev, block_vox), basis, preferred_element_type=jnp.float32
    )
    features = features.astype(jnp.bfloat16).reshape(j_dev, blocks_dev, feature_width)
    by_block = jnp.transpose(features, (1, 0, 2))
    blocks = obs_block[:, 0]
    positions = lax.iota(jnp.int32, obs_dev)
    earlier = (blocks[:, None] == blocks[None, :]) & (positions[None, :] < positions[:, None])
    row_rank = jnp.sum(earlier.astype(jnp.int32), axis=1)
    slot_index = blocks * block_slots + row_rank
    outgoing = (
        jnp.zeros((block_count * block_slots, feature_width), jnp.bfloat16)
        .at[slot_index]
        .set(sensitivity)
    )
    outgoing = outgoing.reshape(n_vox, blocks_dev, block_slots, feature_width)
    answers = jnp.einsum(
        "vbcf,bjf->vbcj",
        lax.all_to_all(outgoing, "vox", split_axis=0, concat_axis=0, tiled=True),
        by_block,
        preferred_element_type=jnp.float32,
    )
    returned = lax.all_to_all(answers, "vox", split_axis=0, concat_axis=0, tiled=True)
    predicted = jnp.transpose(returned.reshape(block_count * block_slots, j_dev)[slot_index])
    all_pred, all_pert = (
        lax.all_gather(predicted, "grp", axis=0, tiled=True),
        lax.all_gather(perturbation, "grp", axis=0, tiled=True),
    )
    scaled, misfit = innovations(all_pred, all_pert, observed, noise_scale, scale_root)
    partials = pair_sums(scaled, misfit)
    gram_total, cross_total, misfit_sq = lax.psum((partials[0], partials[1], partials[2]), "vox")
    damping = misfit_sq / (members * obs_dev * n_vox)
    system = gram_total + damping * jnp.eye(members, dtype=jnp.float32)
    factor = jnp.linalg.cholesky(system)
    halfway = lax.linalg.triangular_solve(factor, cross_total, left_side=True, lower=True)
    weights = lax.linalg.triangular_solve(
        factor, halfway, left_side=True, lower=True, transpose_a=True
    )
    weights_low = weights.astype(jnp.bfloat16)
    regrouped_rows = lax.all_to_all(
        log_modulus.astype(jnp.bfloat16), "grp", split_axis=1, concat_axis=0, tiled=True
    ).astype(log_modulus.dtype)
    anomaly = regrouped_rows.astype(jnp.bfloat16)
    mixture = lax.dot_general(
        weights_low, anomaly, (((0,), (0,)), ((), ())), preferred_element_type=jnp.float32
    )
    renewed = regrouped_rows + mixture / scale_root
    return lax.all_to_all(
        renewed.astype(jnp.bfloat16), "grp", split_axis=0, concat_axis=1, tiled=True
    ).astype(renewed.dtype)


def solution(mesh):
    in_specs = (
        P("grp", "vox"),
        P(),
        P("vox", None),
        P("vox", None),
        P("vox"),
        P("vox"),
        P("grp", "vox"),
    )
    out_specs = P("grp", "vox")
    return jax.shard_map(
        on_device, mesh=mesh, in_specs=in_specs, out_specs=out_specs, check_vma=False
    )
```

profile of v0, /device:TPU:0, one launch (start us, length us, event | category | flops | bytes accessed | tf_op | source)
XLA Modules:
  0.0 127.7 jit_solution(2524602034773025464)
XLA Ops:
  0.0 1.3 %convert_reduce_fusion = s32[1024]{0:T(1024)S(1)} fusion(s32[1024]{0:T(1024)} %bitcast.63), kind=kLoop, calls=%fused_computation.2 | loop fusion | flops 5241856 | bytes 8192 | tf_op jit(solution)/shard_map/reduce_sum | solution.py:44
  1.3 0.7 compare_select_fusion
  2.0 4.3 %scatter_custom_fusion = bf16[2048,128]{1,0:T(8,128)(2,1)} fusion(s32[1024]{0:T(1024)S(1)} %bitcast.61, bf16[1024,128]{1,0:T(8,128)(2,1)} %param.9, bf16[]{:T(256)} %constant.55.clone.1), kind=kCustom, calls=%fused_computation.19 | custom fusion | bytes 524800 | tf_op jit(solution)/shard_map/scatter | solution.py:49
  6.4 5.2 %all-to-all-start.1 = ((bf16[8,8,32,128]{3,2,1,0:T(8,128)(2,1)}), bf16[8,8,32,128]{3,2,1,0:T(8,128)(2,1)S(1)}, u32[]{:S(2)}, u32[]{:S(2)}) async-start(bf16[8,8,32,128]{3,2,1,0:T(8,128)(2,1)} %bitcast.9), calls=%async_computation.1 | async-start | bytes 1048576 | tf_op jit(solution)/shard_map/all_to_all | solution.py:54
  12.1 9.1 %all-to-all-done.1 = bf16[8,8,32,128]{3,2,1,0:T(8,128)(2,1)S(1)} async-done(((bf16[8,8,32,128]{3,2,1,0:T(8,128)(2,1)}), bf16[8,8,32,128]{3,2,1,0:T(8,128)(2,1)S(1)}, u32[]{:S(2)}, u32[]{:S(2)}) %all-to-all-start.1) | async-done | bytes 524320 | tf_op jit(solution)/shard_map/all_to_all | solution.py:54
  21.3 0.8 convolution_bitcast_fusion
  22.2 1.0 reshape.63
  23.2 3.4 %all-to-all-start.2 = ((f32[8,1,6144]{2,1,0:T(1,128)}), f32[8,1,6144]{2,1,0:T(1,128)S(1)}, u32[]{:S(2)}, u32[]{:S(2)}) async-start(f32[8,1,6144]{2,1,0:T(1,128)} %reshape.63), calls=%async_computation.2 | async-start | bytes 393216 | tf_op jit(solution)/shard_map/all_to_all | solution.py:58
  26.6 0.8 copy.52
  27.4 15.0 %all_gather.7 = f32[96,1024]{1,0:T(8,128)S(1)} all-gather(f32[24,1024]{1,0:T(8,128)S(1)} %copy-done.2), channel_id=1, replica_groups=mesh['grp'=4,'vox'=8] {'grp'}, dimensions={0}, use_global_device_ids=true | all-gather | bytes 491520 | tf_op jit(solution)/shard_map/all_gather | solution.py:62
  42.4 5.4 %all-to-all-start = ((bf16[24,4,2048]{2,0,1:T(8,128)(2,1)}), bf16[24,4,2048]{2,0,1:T(8,128)(2,1)S(1)}, u32[]{:S(2)}, u32[]{:S(2)}) async-start(bf16[24,4,2048]{2,0,1:T(8,128)(2,1)} %bitcast.52), calls=%async_computation | async-start | bytes 786432 | tf_op jit(solution)/shard_map/all_to_all | solution.py:75
  47.8 0.6 broadcast.94
  48.4 1.1 reduce.6
  49.8 0.4 copy.40
  50.1 2.8 %gather_fusion = f32[1024,24]{1,0:T(8,128)S(1)} fusion(f32[2048,24]{1,0:T(8,128)S(1)} %bitcast.54, s32[1024]{0:T(1024)S(1)} %broadcast_clamp_fusion), kind=kCustom, calls=%fused_computation | custom fusion | bytes 200704 | tf_op jit(solution)/shard_map/gather | solution.py:59
  53.1 15.7 %all_gather.6 = f32[96,1024]{1,0:T(8,128)S(1)} all-gather(f32[24,1024]{1,0:T(8,128)S(1)} %copy.36), channel_id=1, replica_groups=mesh['grp'=4,'vox'=8] {'grp'}, dimensions={0}, use_global_device_ids=true | all-gather | bytes 491520 | tf_op jit(solution)/shard_map/all_gather | solution.py:61
  68.9 0.8 multiply_reduce_fusion
  70.1 23.9 %all-reduce.2 = (f32[96,96]{1,0:T(8,128)S(1)}, f32[96,96]{1,0:T(8,128)S(1)}, f32[]{:T(128)}) all-reduce(f32[96,96]{1,0:T(8,128)S(1)} %fusion.16, f32[96,96]{1,0:T(8,128)S(1)} %fusion.15, f32[]{:T(128)} %get-tuple-element.8), channel_id=1, replica_groups=mesh['grp'=4,'vox'=8] {'vox'}, use_global_device_ids=true, to_apply=%region_8.9 | all-reduce | flops 18433 | bytes 147464 | tf_op jit(solution)/shard_map/psum | solution.py:66
  94.6 8.8 %cholesky.16 = f32[96,96]{1,0:T(8,128)S(1)} custom-call(f32[96,96]{1,0:T(8,128)S(1)} %fusion.12), custom_call_target="Cholesky" | custom-call | tf_op jit(solution)/shard_map/jit(cholesky)/cholesky | solution.py:69
  103.5 0.7 compare_reduce_fusion
  104.2 0.7 fusion.7
  104.9 7.4 %custom-call.8 = f32[1,96,96]{1,2,0:T(8,128)S(1)} custom-call(f32[1,96,96]{2,1,0:T(8,128)S(1)} %fusion.7), custom_call_target="InvertDiagBlocksLowerTriangular" | custom-call | tf_op jit(solution)/shard_map/triangular_solve | solution.py:71
  113.0 13.7 %all_to_all.42 = bf16[4,24,2048]{2,1,0:T(8,128)(2,1)S(1)} all-to-all(bf16[4,24,2048]{2,1,0:T(8,128)(2,1)S(1)} %bitcast.59), channel_id=1, replica_groups=mesh['grp'=4,'vox'=8] {'grp'}, dimensions={0} | all-to-all | bytes 786432 | tf_op jit(solution)/shard_map/all_to_all | solution.py:83
  126.8 0.9 copy.43
  (32 shorter events, 2.4 us)
Async XLA Ops:
  0.0 11.9 %copy-start = (bf16[1024,128]{1,0:T(8,128)(2,1)S(1)}, bf16[1024,128]{1,0:T(8,128)(2,1)}, u32[]{:S(2)}) copy-start(bf16[1024,128]{1,0:T(8,128)(2,1)} %param.8) | copy-start | bytes 786436
  0.0 11.6 %copy-start.1 = (f32[24,8192]{1,0:T(8,128)S(1)}, f32[24,8192]{1,0:T(8,128)}, u32[]{:S(2)}) copy-start(f32[24,8192]{1,0:T(8,128)} %param.7) | copy-start | bytes 2359300
  6.4 14.9 %all-to-all-start.1 = ((bf16[8,8,32,128]{3,2,1,0:T(8,128)(2,1)}), bf16[8,8,32,128]{3,2,1,0:T(8,128)(2,1)S(1)}, u32[]{:S(2)}, u32[]{:S(2)}) async-start(bf16[8,8,32,128]{3,2,1,0:T(8,128)(2,1)} %bitcast.9), calls=%async_computation.1 | async-start | bytes 1048576 | tf_op jit(solution)/shard_map/all_to_all | solution.py:54
  22.1 4.4 %copy-start.3 = (f32[1024]{0:T(1024)S(1)}, f32[1024]{0:T(1024)}, u32[]{:S(2)}) copy-start(f32[1024]{0:T(1024)} %param.12) | copy-start | bytes 12292
  22.1 5.2 %copy-start.2 = (f32[24,1024]{1,0:T(8,128)S(1)}, f32[24,1024]{1,0:T(8,128)}, u32[]{:S(2)}) copy-start(f32[24,1024]{1,0:T(8,128)} %param.13) | copy-start | bytes 294916
  23.2 19.2 %all-to-all-start.2 = ((f32[8,1,6144]{2,1,0:T(1,128)}), f32[8,1,6144]{2,1,0:T(1,128)S(1)}, u32[]{:S(2)}, u32[]{:S(2)}) async-start(f32[8,1,6144]{2,1,0:T(1,128)} %reshape.63), calls=%async_computation.2 | async-start | bytes 393216 | tf_op jit(solution)/shard_map/all_to_all | solution.py:58
  42.4 70.3 %all-to-all-start = ((bf16[24,4,2048]{2,0,1:T(8,128)(2,1)}), bf16[24,4,2048]{2,0,1:T(8,128)(2,1)S(1)}, u32[]{:S(2)}, u32[]{:S(2)}) async-start(bf16[24,4,2048]{2,0,1:T(8,128)(2,1)} %bitcast.52), calls=%async_computation | async-start | bytes 786432 | tf_op jit(solution)/shard_map/all_to_all | solution.py:75
  52.9 15.9 %copy-start.4 = (f32[1024]{0:T(1024)S(1)}, f32[1024]{0:T(1024)}, u32[]{:S(2)}) copy-start(f32[1024]{0:T(1024)} %param.11) | copy-start | bytes 12292
where the time goes:
time: 128 us
  blocking collectives  68.3 us (53%)
  other arithmetic  21.8 us (17%)
  starting transfers between devices  14 us (11%)
  local copies, waits for them, and re-layouts  11.6 us (9%)
  waiting for transfers between devices  9.12 us (7%)
  matrix products  2.18 us (2%)
    psum x1, blocking collectives, on_device(): lax.psum((partials[0], partials[1], partials[2]), 'vox')  23.9 us
    all_gather x1, blocking collectives, on_device(): lax.all_gather(predicted, 'grp', axis=0, tiled=True)  15.7 us
    all_gather x1, blocking collectives, on_device(): lax.all_gather(perturbation, 'grp', axis=0, tiled=True)  15 us
    all_to_all x1, blocking collectives, on_device(): lax.all_to_all(renewed.astype(jnp.bfloat16), 'grp', split_axis=0, concat_...  13.7 us
    another operation x3, other arithmetic, on_device(): factor = jnp.linalg.cholesky(system)  9.53 us
    all_to_all x1, waiting for transfers between devices, on_device(): lax.all_to_all(outgoing, 'vox', split_axis=0, concat_axis=0, tiled=True)  9.11 us
    another operation x2, other arithmetic, on_device(): lax.linalg.triangular_solve(factor, halfway, left_side=True, lower=True,...  8.06 us
    all_to_all x1, starting transfers between devices, on_device(): lax.all_to_all(log_modulus.astype(jnp.bfloat16), 'grp', split_axis=1, con...  5.37 us
  transfers between devices with their start and end apart: 3, of which 1 were waited for; matrix products, arithmetic and copies ran while one was open for 20% of the time, Pallas kernels for 0%

commit v1 on v0

v1 whole, which is shorter than its diff:
```python
import functools
import math

import jax
import jax.numpy as jnp
from jax import lax
from jax.experimental import pallas as pl
from jax.experimental.pallas import tpu as pltpu
from jax.sharding import PartitionSpec as P

LANES = 128
SUBLANES = 8


def round_up(value, step):
    return -(-value // step) * step


def exchange(value, axis, distance):
    count = lax.axis_size(axis)
    return lax.ppermute(value, axis, [(i, i ^ distance) for i in range(count)])


def stages(count):
    bits = count.bit_length() - 1
    low, groups = 1, []
    while low < bits:
        width = min(2, bits - low)
        groups.append([step << low for step in range(1, 1 << width)])
        low += width
    return groups + ([[1]] if bits else [])


def gather_pieces(value, axis):
    stacks, offsets = [value], [[0]]
    for group in stages(lax.axis_size(axis)):
        whole = stacks[0] if len(stacks) == 1 else jnp.concatenate(stacks, axis=0)
        held = [offset for part in offsets for offset in part]
        stacks = [whole] + [exchange(whole, axis, distance) for distance in group]
        offsets = [held] + [[offset ^ distance for offset in held] for distance in group]
    return stacks, offsets


def predict_kernel(offsets, j_dev, blocks_dev, *refs):
    stack_refs = refs[: len(offsets)]
    sens_ref, key_ref, pert_ref, obs_ref, noise_ref, out_ref = refs[len(offsets) :]
    obs_dev = sens_ref.shape[0]
    rows = j_dev * blocks_dev
    tile = min(obs_dev, 2 * LANES)
    for start in range(0, obs_dev, tile):
        cols = pl.ds(start, tile)
        sens = sens_ref[cols, :]
        key = key_ref[:, cols]
        local = lax.broadcasted_iota(jnp.int32, (blocks_dev, tile), 0)
        total = jnp.zeros((j_dev, blocks_dev, tile), jnp.float32)
        for stack_ref, held in zip(stack_refs, offsets):
            for place, offset in enumerate(held):
                piece = stack_ref[pl.ds(place * rows, rows), :]
                product = lax.dot_general(
                    piece, sens, (((1,), (1,)), ((), ())), preferred_element_type=jnp.float32
                ).reshape(j_dev, blocks_dev, tile)
                wanted = (local + offset * blocks_dev == key)[None]
                total = total + jnp.where(wanted, product, 0.0)
        predicted = jnp.sum(total, axis=1)
        misfit = ((obs_ref[:, cols] - predicted) / noise_ref[:, cols] + pert_ref[:, cols]).astype(jnp.bfloat16)
        wide = misfit.astype(jnp.float32)
        out_ref[pl.ds(0, j_dev), cols] = predicted
        squares = jnp.sum(wide * wide, axis=0, keepdims=True)
        out_ref[pl.ds(j_dev, SUBLANES), cols] = jnp.broadcast_to(squares, (SUBLANES, tile))


def pair_kernel(groups, j_dev, scale_root, *refs):
    pred_refs = refs[:groups]
    pert_ref, obs_ref, noise_ref, out_ref = refs[groups:]
    members = groups * j_dev
    noise = noise_ref[...]
    own = pred_refs[0][pl.ds(0, j_dev), :]
    predicted = jnp.concatenate([ref[pl.ds(0, j_dev), :] for ref in pred_refs], axis=0)
    centre = jnp.sum(predicted, axis=0, keepdims=True) * (1.0 / members)
    scaled = ((predicted - centre) / (noise * scale_root)).astype(jnp.bfloat16)
    misfit = ((obs_ref[...] - own) / noise + pert_ref[...]).astype(jnp.bfloat16)
    contract = (((1,), (1,)), ((), ()))
    width = out_ref.shape[1]
    right = jnp.concatenate([scaled.astype(jnp.float32), misfit.astype(jnp.float32)], axis=0)
    pad = width - right.shape[0]
    if pad:
        right = jnp.concatenate([right, jnp.zeros((pad, right.shape[1]), jnp.float32)], axis=0)
    out_ref[pl.ds(0, members), :] = lax.dot_general(
        scaled, right.astype(jnp.bfloat16), contract, preferred_element_type=jnp.float32
    )
    squares = sum(ref[pl.ds(j_dev, 1), :] for ref in pred_refs)
    folded = sum(squares[:, at : at + width] for at in range(0, squares.shape[1], width))
    first = lax.broadcasted_iota(jnp.int32, (SUBLANES, width), 0) == 0
    out_ref[pl.ds(members, SUBLANES), :] = jnp.where(first, jnp.broadcast_to(folded, (SUBLANES, width)), 0.0)


def solve_kernel(members, right, count, *refs):
    part_refs, out_ref = refs[:-1], refs[-1]
    tile = (SUBLANES, LANES)
    groups = members // SUBLANES
    lane = lax.broadcasted_iota(jnp.int32, tile, 1)
    sub = lax.broadcasted_iota(jnp.int32, tile, 0)

    def load(group):
        rows = pl.ds(group * SUBLANES, SUBLANES)
        values = [ref[rows, :] for ref in part_refs]
        while len(values) > 1:
            values = [a + b for a, b in zip(values[::2], values[1::2])] + values[len(values) // 2 * 2 :]
        return values[0]

    damping = jnp.sum(load(groups), keepdims=True) * (1.0 / count)
    damping = jnp.broadcast_to(damping, tile)
    matrix = []
    for group in range(groups):
        matrix.append(load(group) + jnp.where(lane == sub + group * SUBLANES, damping, 0.0))

    def column(value, at):
        return jnp.broadcast_to(value[:, at : at + 1], tile)

    for block in range(groups):
        base = block * SUBLANES
        rows = [jnp.broadcast_to(matrix[block][i : i + 1, :], tile) for i in range(SUBLANES)]
        pivot = {(i, j): column(rows[i], base + j) for i in range(SUBLANES) for j in range(i, SUBLANES)}
        inverse = []
        for k in range(SUBLANES):
            inverse.append(1.0 / pivot[k, k])
            for i in range(k + 1, SUBLANES):
                factor = pivot[k, i] * inverse[k]
                for j in range(i, SUBLANES):
                    pivot[i, j] = pivot[i, j] - factor * pivot[k, j]
                rows[i] = rows[i] - factor * rows[k]
        for k in range(SUBLANES - 1, -1, -1):
            rows[k] = rows[k] * inverse[k]
            for i in range(k):
                rows[i] = rows[i] - pivot[i, k] * rows[k]
        for group in range(groups):
            if group == block:
                value = rows[0]
                for i in range(1, SUBLANES):
                    value = jnp.where(sub == i, rows[i], value)
            else:
                value = matrix[group]
                for i in range(SUBLANES):
                    value = value - column(matrix[group], base + i) * rows[i]
            matrix[group] = value
    for group in range(groups):
        out_ref[pl.ds(group * SUBLANES, SUBLANES), :] = matrix[group]


def solve_weights(parts, members, j_dev, count):
    if members + j_dev <= LANES and members % SUBLANES == 0:
        solved = pl.pallas_call(
            functools.partial(solve_kernel, members, j_dev, count),
            out_shape=jax.ShapeDtypeStruct((members, LANES), jnp.float32),
        )(*parts)
        return solved[:, members : members + j_dev]
    total = functools.reduce(jnp.add, parts)
    damping = jnp.sum(total[members:]) / count
    system = total[:members, :members] + damping * jnp.eye(members, dtype=jnp.float32)
    cross = total[:members, members : members + j_dev]
    factor = jnp.linalg.cholesky(system)
    halfway = lax.linalg.triangular_solve(factor, cross, left_side=True, lower=True)
    return lax.linalg.triangular_solve(factor, halfway, left_side=True, lower=True, transpose_a=True)


def on_device(log_modulus, basis, sensitivity, obs_block, observed, noise_scale, perturbation):
    n_vox = lax.axis_size("vox")
    n_grp = lax.axis_size("grp")
    j_dev, vox_dev = log_modulus.shape
    block_vox, feature_width = basis.shape
    blocks_dev = vox_dev // block_vox
    obs_dev = sensitivity.shape[0]
    members = j_dev * n_grp
    scale_root = math.sqrt(members - 1)

    low = log_modulus.astype(jnp.bfloat16)
    compliance = jnp.exp(-log_modulus).astype(jnp.bfloat16)
    features = jnp.dot(
        compliance.reshape(j_dev * blocks_dev, block_vox), basis, preferred_element_type=jnp.float32
    ).astype(jnp.bfloat16)

    blocks = obs_block[:, 0]
    key = ((blocks // blocks_dev) ^ lax.axis_index("vox")) * blocks_dev + blocks % blocks_dev
    key = key.reshape(1, obs_dev)
    observed = observed.reshape(1, obs_dev)
    noise = noise_scale.reshape(1, obs_dev)

    stacks, offsets = gather_pieces(features, "vox")
    payload = pl.pallas_call(
        functools.partial(predict_kernel, offsets, j_dev, blocks_dev),
        out_shape=jax.ShapeDtypeStruct((j_dev + SUBLANES, obs_dev), jnp.float32),
    )(*stacks, sensitivity, key, perturbation, observed, noise)
    payloads = [payload] + [exchange(payload, "grp", distance) for distance in range(1, n_grp)]
    width = round_up(members + j_dev, LANES)
    partial_sums = pl.pallas_call(
        functools.partial(pair_kernel, n_grp, j_dev, scale_root),
        out_shape=jax.ShapeDtypeStruct((members + SUBLANES, width), jnp.float32),
    )(*payloads, perturbation, observed, noise)
    parts = [partial_sums]
    for group in reversed(stages(n_vox)):
        total = functools.reduce(jnp.add, parts)
        parts = [total] + [exchange(total, "vox", distance) for distance in group]
    weights = solve_weights(parts, members, j_dev, members * obs_dev * n_vox)
    weights_low = weights.astype(jnp.bfloat16)

    anomalies = [low] + [exchange(low, "grp", distance) for distance in range(1, n_grp)]
    mixture = sum(
        lax.dot_general(
            weights_low[place * j_dev : (place + 1) * j_dev],
            anomaly,
            (((0,), (0,)), ((), ())),
            preferred_element_type=jnp.float32,
        )
        for place, anomaly in enumerate(anomalies)
    )
    return log_modulus + mixture / scale_root


def solution(mesh):
    in_specs = (
        P("grp", "vox"),
        P(),
        P("vox", None),
        P("vox", None),
        P("vox"),
        P("vox"),
        P("grp", "vox"),
    )
    out_specs = P("grp", "vox")
    return jax.shard_map(
        on_device, mesh=mesh, in_specs=in_specs, out_specs=out_specs, check_vma=False
    )
```

time: 128 us -> 69.9 us (0.55)
  blocking collectives: 68.3 us -> 0 us
  waiting for transfers between devices: 9.12 us -> 30.2 us
  other arithmetic: 21.8 us -> 3.81 us
  Pallas kernels: 0 us -> 9.74 us
  local copies, waits for them, and re-layouts: 11.6 us -> 3.44 us
  starting transfers between devices: 14 us -> 19.5 us
    all_gather x2 -> x0, blocking collectives: 30.7 us -> none  [the longest x1 15.7 us: on_device(): lax.all_gather(predicted, 'grp', axis=0, tiled=True)]
    ppermute x0 -> x14, waiting for transfers between devices: none -> 30.2 us  [exchange(): return lax.ppermute(value, axis, [(i, i ^ distance) for i in range(count)])]
    psum x1 -> x0, blocking collectives: 23.9 us -> none  [on_device(): lax.psum((partials[0], partials[1], partials[2]), 'vox')]
    ppermute x0 -> x14, starting transfers between devices: none -> 19.5 us  [exchange(): return lax.ppermute(value, axis, [(i, i ^ distance) for i in range(count)])]
    another operation x5 -> x1, other arithmetic: 17.6 us -> 0.8 us  [the longest x3 9.53 us: on_device(): factor = jnp.linalg.cholesky(system)]
    all_to_all x3 -> x0, starting transfers between devices: 14 us -> none  [the longest x1 5.37 us: on_device(): lax.all_to_all(log_modulus.astype(jnp.bfloat16), 'grp', split_axis=1, con...]
    all_to_all x1 -> x0, blocking collectives: 13.7 us -> none  [on_device(): lax.all_to_all(renewed.astype(jnp.bfloat16), 'grp', split_axis=0, concat_...]
    pallas_call x0 -> x3, Pallas kernels: none -> 9.74 us  [the longest x1 4.81 us: solve_weights(): pl.pallas_call(functools.partial(solve_kernel, members, j_dev, count), ou...]
  transfers between devices with their start and end apart: 3 -> 14, of which waited for: 1 -> 8; matrix products, arithmetic and copies ran while one was open for 20% -> 4% of each run, Pallas kernels for 0% -> 14%
where the time goes in v1:
time: 69.9 us; the launch traced here: 69.6 us
  waiting for transfers between devices  30.2 us (43%)
  starting transfers between devices  19.5 us (28%)
  Pallas kernels  9.74 us (14%)
  other arithmetic  3.81 us (5%)
  local copies, waits for them, and re-layouts  3.44 us (5%)
  matrix products  2.69 us (4%)
    ppermute x14, waiting for transfers between devices, exchange(): return lax.ppermute(value, axis, [(i, i ^ distance) for i in range(count)])  30.2 us
    ppermute x14, starting transfers between devices, exchange(): return lax.ppermute(value, axis, [(i, i ^ distance) for i in range(count)])  19.5 us
    pallas_call x1, Pallas kernels, solve_weights(): pl.pallas_call(functools.partial(solve_kernel, members, j_dev, count), ou...  4.81 us
    unnamed x24, local copies, waits for them, and re-layouts  3.26 us
    pallas_call x1, Pallas kernels, on_device(): pl.pallas_call(functools.partial(predict_kernel, offsets, j_dev, blocks_d...  2.87 us
    dot_general x4, matrix products, on_device(): lax.dot_general(weights_low[place * j_dev:(place + 1) * j_dev], anomaly,...  2.44 us
    pallas_call x1, Pallas kernels, on_device(): pl.pallas_call(functools.partial(pair_kernel, n_grp, j_dev, scale_root),...  2.06 us
    convert_element_type x1, other arithmetic, on_device(): compliance = jnp.exp(-log_modulus).astype(jnp.bfloat16)  1.55 us
  transfers between devices with their start and end apart: 14, of which 8 were waited for; matrix products, arithmetic and copies ran while one was open for 4% of the time, Pallas kernels for 14%

profile of v1, /device:TPU:0, one launch (start us, length us, event | category | flops | bytes accessed | tf_op | source)
XLA Modules:
  0.0 69.6 jit_solution(11994837293719524811)
XLA Ops:
  0.0 1.5 %exponential_convert_fusion = (bf16[24,8192]{1,0:T(8,128)(2,1)S(1)}, bf16[24,8192]{1,0:T(8,128)(2,1)S(1)}) fusion(f32[24,8192]{1,0:T(8,128)} %param.7), kind=kLoop, calls=%fused_computation.6 | loop fusion | flops 589824 | bytes 1572864 | tf_op jit(solution)/shard_map/convert_element_type | solution.py:177
  2.0 4.0 %collective-permute-start.2 = (bf16[192,128]{1,0:T(8,128)(2,1)S(1)}, bf16[192,128]{1,0:T(8,128)(2,1)S(1)}, u32[]{:S(2)}, u32[]{:S(2)}) collective-permute-start(bf16[192,128]{1,0:T(8,128)(2,1)S(1)} %convolution_convert_fusion), channel_id=1, source_target_pairs={{0,6},{1,7},{2,4},{3,5},{4,2},{5,3},{6,0},{7,1},{8,14},{9,15},{10,... | collective-permute-start | bytes 147464 | tf_op jit(solution)/shard_map/ppermute | solution.py:21
  6.6 4.0 %collective-permute-start.13 = (bf16[24,8192]{1,0:T(8,128)(2,1)S(1)}, bf16[24,8192]{1,0:T(8,128)(2,1)S(1)}, u32[]{:S(2)}, u32[]{:S(2)}) collective-permute-start(bf16[24,8192]{1,0:T(8,128)(2,1)S(1)} %get-tuple-element.6), channel_id=1, source_target_pairs={{0,24},{8,16},{16,8},{24,0},{1,25},{9,17},{17,9},{25,1},{2,26},{10... | collective-permute-start | bytes 1179656 | tf_op jit(solution)/shard_map/ppermute | solution.py:21
  11.3 0.6 fusion.11.refs_3_
  12.2 0.7 copy-done.4
  12.9 2.9 %shard_map.73.refs_0_ = f32[32,1024]{1,0:T(8,128)} custom-call(bf16[768,128]{1,0:T(8,128)(2,1)} %copy-done.2, bf16[768,128]{1,0:T(8,128)(2,1)} %copy-done.4, bf16[1024,128]{1,0:T(8,128)(2,1)} %refs_2_.1, s32[1,1024]{1,0:T(1,128)} %fusion.11.refs_3_, f32[24,1024]{1,0:T(8,128)} %refs_4_.3, f32[1,1024]{1,0:T(1,128)} %bitcast.21, f32[1,1024]{1,0:T(1,128)} %bitcast.23), custom_call_target="tpu_custom_call" | custom-call | tf_op jit(solution)/shard_map/pallas_call | solution.py:189
  15.8 3.5 %collective-permute-start.6 = (f32[32,1024]{1,0:T(8,128)}, f32[32,1024]{1,0:T(8,128)S(1)}, u32[]{:S(2)}, u32[]{:S(2)}) collective-permute-start(f32[32,1024]{1,0:T(8,128)} %shard_map.73.refs_0_), channel_id=1, source_target_pairs={{0,24},{8,16},{16,8},{24,0},{1,25},{9,17},{17,9},{25,1},{2,26},{10... | collective-permute-start | bytes 393224 | tf_op jit(solution)/shard_map/ppermute | solution.py:21
  19.3 0.9 %collective-permute-start.4 = (f32[32,1024]{1,0:T(8,128)}, f32[32,1024]{1,0:T(8,128)S(1)}, u32[]{:S(2)}, u32[]{:S(2)}) collective-permute-start(f32[32,1024]{1,0:T(8,128)} %shard_map.73.refs_0_), channel_id=1, source_target_pairs={{0,8},{8,0},{16,24},{24,16},{1,9},{9,1},{17,25},{25,17},{2,10},{10... | collective-permute-start | bytes 393224 | tf_op jit(solution)/shard_map/ppermute | solution.py:21
  20.2 2.1 %collective-permute-start.12 = (bf16[24,8192]{1,0:T(8,128)(2,1)S(1)}, bf16[24,8192]{1,0:T(8,128)(2,1)S(1)}, u32[]{:S(2)}, u32[]{:S(2)}) collective-permute-start(bf16[24,8192]{1,0:T(8,128)(2,1)S(1)} %get-tuple-element.6), channel_id=1, source_target_pairs={{0,16},{8,24},{16,0},{24,8},{1,17},{9,25},{17,1},{25,9},{2,18},{10... | collective-permute-start | bytes 1179656 | tf_op jit(solution)/shard_map/ppermute | solution.py:21
  22.2 2.0 %collective-permute-done.6.refs_3_ = f32[32,1024]{1,0:T(8,128)S(1)} collective-permute-done((f32[32,1024]{1,0:T(8,128)}, f32[32,1024]{1,0:T(8,128)S(1)}, u32[]{:S(2)}, u32[]{:S(2)}) %collective-permute-start.6) | collective-permute-done | bytes 131104 | tf_op jit(solution)/shard_map/ppermute | solution.py:21
  24.2 22.9 %collective-permute-done.5.refs_2_ = f32[32,1024]{1,0:T(8,128)S(1)} collective-permute-done((f32[32,1024]{1,0:T(8,128)}, f32[32,1024]{1,0:T(8,128)S(1)}, u32[]{:S(2)}, u32[]{:S(2)}) %collective-permute-start.5) | collective-permute-done | bytes 131104 | tf_op jit(solution)/shard_map/ppermute | solution.py:21
  47.1 0.6 copy-done.6
  47.7 0.7 copy-done.7
  48.4 2.1 %shard_map.74 = f32[104,128]{1,0:T(8,128)} custom-call(f32[32,1024]{1,0:T(8,128)} %shard_map.73.refs_0_, f32[32,1024]{1,0:T(8,128)} %copy-done.7, f32[32,1024]{1,0:T(8,128)} %copy-done.6, f32[32,1024]{1,0:T(8,128)} %copy-done.5, f32[24,1024]{1,0:T(8,128)} %refs_4_.3, f32[1,1024]{1,0:T(1,128)} %bitcast.22, f32[1,1024]{1,0:T(1,128)} %bitcast.24), custom_call_target="tpu_custom_call" | custom-call | tf_op jit(solution)/shard_map/pallas_call | solution.py:195
  50.5 1.4 %collective-permute-done.7 = f32[104,128]{1,0:T(8,128)S(1)} collective-permute-done((f32[104,128]{1,0:T(8,128)}, f32[104,128]{1,0:T(8,128)S(1)}, u32[]{:S(2)}, u32[]{:S(2)}) %collective-permute-start.7) | collective-permute-done | bytes 53280 | tf_op jit(solution)/shard_map/ppermute | solution.py:21
  51.9 0.8 %add.48.refs_0_ = f32[104,128]{1,0:T(8,128)S(1)} add(f32[104,128]{1,0:T(8,128)} %shard_map.74, f32[104,128]{1,0:T(8,128)S(1)} %collective-permute-done.7) | non-fusion elementwise | flops 13312 | bytes 159744 | tf_op jit(solution)/shard_map/add | solution.py:201
  52.7 2.5 %collective-permute-start.10 = (f32[104,128]{1,0:T(8,128)S(1)}, f32[104,128]{1,0:T(8,128)S(1)}, u32[]{:S(2)}, u32[]{:S(2)}) collective-permute-start(f32[104,128]{1,0:T(8,128)S(1)} %add.48.refs_0_), channel_id=1, source_target_pairs={{0,6},{1,7},{2,4},{3,5},{4,2},{5,3},{6,0},{7,1},{8,14},{9,15},{10,... | collective-permute-start | bytes 159752 | tf_op jit(solution)/shard_map/ppermute | solution.py:21
  56.3 1.5 %collective-permute-done.10.refs_3_ = f32[104,128]{1,0:T(8,128)S(1)} collective-permute-done((f32[104,128]{1,0:T(8,128)S(1)}, f32[104,128]{1,0:T(8,128)S(1)}, u32[]{:S(2)}, u32[]{:S(2)}) %collective-permute-start.10) | collective-permute-done | bytes 53280 | tf_op jit(solution)/shard_map/ppermute | solution.py:21
  57.8 0.8 %collective-permute-start.11 = (bf16[24,8192]{1,0:T(8,128)(2,1)S(1)}, bf16[24,8192]{1,0:T(8,128)(2,1)S(1)}, u32[]{:S(2)}, u32[]{:S(2)}) collective-permute-start(bf16[24,8192]{1,0:T(8,128)(2,1)S(1)} %get-tuple-element.6), channel_id=1, source_target_pairs={{0,8},{8,0},{16,24},{24,16},{1,9},{9,1},{17,25},{25,17},{2,10},{10... | collective-permute-start | bytes 1179656 | tf_op jit(solution)/shard_map/ppermute | solution.py:21
  58.6 0.8 %collective-permute-done.9.refs_2_ = f32[104,128]{1,0:T(8,128)S(1)} collective-permute-done((f32[104,128]{1,0:T(8,128)S(1)}, f32[104,128]{1,0:T(8,128)S(1)}, u32[]{:S(2)}, u32[]{:S(2)}) %collective-permute-start.9) | collective-permute-done | bytes 53280 | tf_op jit(solution)/shard_map/ppermute | solution.py:21
  60.6 4.8 %shard_map.75 = f32[96,128]{1,0:T(8,128)} custom-call(f32[104,128]{1,0:T(8,128)} %copy-done.3, f32[104,128]{1,0:T(8,128)} %copy-done.10, f32[104,128]{1,0:T(8,128)} %copy-done.9, f32[104,128]{1,0:T(8,128)} %copy-done.8), custom_call_target="tpu_custom_call" | custom-call | tf_op jit(solution)/shard_map/pallas_call | solution.py:152
  65.4 0.8 %convert.3 = bf16[96,128]{1,0:T(8,128)(2,1)S(1)} convert(f32[96,128]{1,0:T(8,128)} %shard_map.75) | non-fusion elementwise | flops 12288 | bytes 73728 | tf_op jit(solution)/shard_map/convert
  67.0 0.8 %collective-permute-done.11 = bf16[24,8192]{1,0:T(8,128)(2,1)S(1)} collective-permute-done((bf16[24,8192]{1,0:T(8,128)(2,1)S(1)}, bf16[24,8192]{1,0:T(8,128)(2,1)S(1)}, u32[]{:S(2)}, u32[]{:S(2)}) %collective-permute-start.11) | collective-permute-done | bytes 393248 | tf_op jit(solution)/shard_map/ppermute | solution.py:21
  68.3 1.3 %fusion.3 = f32[24,8192]{1,0:T(8,128)} fusion(f32[24,8192]{1,0:T(8,128)S(1)} %copy-done.1, f32[24,8192]{1,0:T(8,128)S(1)} %fusion.4, f32[24,8192]{1,0:T(8,128)S(1)} %fusion.6, f32[24,8192]{1,0:T(8,128)S(1)} %fusion.8, bf16[24,8192]{1,0:T(8,128)(2,1)S(1)} %get-tuple-element.6, bf16[96,128]{1,0:T(8,128)(2,1)S(1)} %convert.3), kind=kOutput, calls=%fused_computation.4 | convolution fusion | flops 10420224 | bytes 4331520 | tf_op jit(solution)/shard_map/dot_general | solution.py:208
  (42 shorter events, 5.4 us)
Async XLA Ops:
  0.0 1.7 %copy-start = (bf16[1024,128]{1,0:T(8,128)(2,1)S(1)}, bf16[1024,128]{1,0:T(8,128)(2,1)}, u32[]{:S(2)}) copy-start(bf16[1024,128]{1,0:T(8,128)(2,1)} %param.8) | copy-start | bytes 786436
  2.0 8.6 %collective-permute-start.2 = (bf16[192,128]{1,0:T(8,128)(2,1)S(1)}, bf16[192,128]{1,0:T(8,128)(2,1)S(1)}, u32[]{:S(2)}, u32[]{:S(2)}) collective-permute-start(bf16[192,128]{1,0:T(8,128)(2,1)S(1)} %convolution_convert_fusion), channel_id=1, source_target_pairs={{0,6},{1,7},{2,4},{3,5},{4,2},{5,3},{6,0},{7,1},{8,14},{9,15},{10,... | collective-permute-start | bytes 147464 | tf_op jit(solution)/shard_map/ppermute | solution.py:21
  6.0 4.7 %collective-permute-start.1 = (bf16[192,128]{1,0:T(8,128)(2,1)S(1)}, bf16[192,128]{1,0:T(8,128)(2,1)S(1)}, u32[]{:S(2)}, u32[]{:S(2)}) collective-permute-start(bf16[192,128]{1,0:T(8,128)(2,1)S(1)} %convolution_convert_fusion), channel_id=1, source_target_pairs={{0,4},{1,5},{2,6},{3,7},{4,0},{5,1},{6,2},{7,3},{8,12},{9,13},{10,... | collective-permute-start | bytes 147464 | tf_op jit(solution)/shard_map/ppermute | solution.py:21
  6.5 4.2 %collective-permute-start = (bf16[192,128]{1,0:T(8,128)(2,1)S(1)}, bf16[192,128]{1,0:T(8,128)(2,1)S(1)}, u32[]{:S(2)}, u32[]{:S(2)}) collective-permute-start(bf16[192,128]{1,0:T(8,128)(2,1)S(1)} %convolution_convert_fusion), channel_id=1, source_target_pairs={{0,2},{1,3},{2,0},{3,1},{4,6},{5,7},{6,4},{7,5},{8,10},{9,11},{10,... | collective-permute-start | bytes 147464 | tf_op jit(solution)/shard_map/ppermute | solution.py:21
  6.6 59.6 %collective-permute-start.13 = (bf16[24,8192]{1,0:T(8,128)(2,1)S(1)}, bf16[24,8192]{1,0:T(8,128)(2,1)S(1)}, u32[]{:S(2)}, u32[]{:S(2)}) collective-permute-start(bf16[24,8192]{1,0:T(8,128)(2,1)S(1)} %get-tuple-element.6), channel_id=1, source_target_pairs={{0,24},{8,16},{16,8},{24,0},{1,25},{9,17},{17,9},{25,1},{2,26},{10... | collective-permute-start | bytes 1179656 | tf_op jit(solution)/shard_map/ppermute | solution.py:21
  10.6 0.7 copy-start.11
  10.7 1.5 %copy-start.2 = (bf16[768,128]{1,0:T(8,128)(2,1)}, bf16[768,128]{1,0:T(8,128)(2,1)S(1)}, u32[]{:S(2)}) copy-start(bf16[768,128]{1,0:T(8,128)(2,1)S(1)} %pad_maximum_fusion.refs_0_) | copy-start | bytes 589828
  10.7 1.5 %collective-permute-start.3 = (bf16[768,128]{1,0:T(8,128)(2,1)S(1)}, bf16[768,128]{1,0:T(8,128)(2,1)S(1)}, u32[]{:S(2)}, u32[]{:S(2)}) collective-permute-start(bf16[768,128]{1,0:T(8,128)(2,1)S(1)} %pad_maximum_fusion.refs_0_), channel_id=1, source_target_pairs={{0,1},{1,0},{2,3},{3,2},{4,5},{5,4},{6,7},{7,6},{8,9},{9,8},{10,11... | collective-permute-start | bytes 589832 | tf_op jit(solution)/shard_map/ppermute | solution.py:21
  12.2 0.7 copy-start.4
  15.8 8.5 %collective-permute-start.6 = (f32[32,1024]{1,0:T(8,128)}, f32[32,1024]{1,0:T(8,128)S(1)}, u32[]{:S(2)}, u32[]{:S(2)}) collective-permute-start(f32[32,1024]{1,0:T(8,128)} %shard_map.73.refs_0_), channel_id=1, source_target_pairs={{0,24},{8,16},{16,8},{24,0},{1,25},{9,17},{17,9},{25,1},{2,26},{10... | collective-permute-start | bytes 393224 | tf_op jit(solution)/shard_map/ppermute | solution.py:21
  19.3 27.8 %collective-permute-start.5 = (f32[32,1024]{1,0:T(8,128)}, f32[32,1024]{1,0:T(8,128)S(1)}, u32[]{:S(2)}, u32[]{:S(2)}) collective-permute-start(f32[32,1024]{1,0:T(8,128)} %shard_map.73.refs_0_), channel_id=1, source_target_pairs={{0,16},{8,24},{16,0},{24,8},{1,17},{9,25},{17,1},{25,9},{2,18},{10... | collective-permute-start | bytes 393224 | tf_op jit(solution)/shard_map/ppermute | solution.py:21
  19.3 27.8 %collective-permute-start.4 = (f32[32,1024]{1,0:T(8,128)}, f32[32,1024]{1,0:T(8,128)S(1)}, u32[]{:S(2)}, u32[]{:S(2)}) collective-permute-start(f32[32,1024]{1,0:T(8,128)} %shard_map.73.refs_0_), channel_id=1, source_target_pairs={{0,8},{8,0},{16,24},{24,16},{1,9},{9,1},{17,25},{25,17},{2,10},{10... | collective-permute-start | bytes 393224 | tf_op jit(solution)/shard_map/ppermute | solution.py:21
  20.2 46.5 %collective-permute-start.12 = (bf16[24,8192]{1,0:T(8,128)(2,1)S(1)}, bf16[24,8192]{1,0:T(8,128)(2,1)S(1)}, u32[]{:S(2)}, u32[]{:S(2)}) collective-permute-start(bf16[24,8192]{1,0:T(8,128)(2,1)S(1)} %get-tuple-element.6), channel_id=1, source_target_pairs={{0,16},{8,24},{16,0},{24,8},{1,17},{9,25},{17,1},{25,9},{2,18},{10... | collective-permute-start | bytes 1179656 | tf_op jit(solution)/shard_map/ppermute | solution.py:21
  24.2 22.9 %copy-start.5 = (f32[32,1024]{1,0:T(8,128)}, f32[32,1024]{1,0:T(8,128)S(1)}, u32[]{:S(2)}) copy-start(f32[32,1024]{1,0:T(8,128)S(1)} %collective-permute-done.6.refs_3_) | copy-start | bytes 393220
  47.1 0.6 copy-start.6
  47.7 0.7 copy-start.7
  50.5 1.4 %collective-permute-start.7 = (f32[104,128]{1,0:T(8,128)}, f32[104,128]{1,0:T(8,128)S(1)}, u32[]{:S(2)}, u32[]{:S(2)}) collective-permute-start(f32[104,128]{1,0:T(8,128)} %shard_map.74), channel_id=1, source_target_pairs={{0,1},{1,0},{2,3},{3,2},{4,5},{5,4},{6,7},{7,6},{8,9},{9,8},{10,11... | collective-permute-start | bytes 159752 | tf_op jit(solution)/shard_map/ppermute | solution.py:21
  52.7 7.2 %copy-start.3 = (f32[104,128]{1,0:T(8,128)}, f32[104,128]{1,0:T(8,128)S(1)}, u32[]{:S(2)}) copy-start(f32[104,128]{1,0:T(8,128)S(1)} %add.48.refs_0_) | copy-start | bytes 159748
  52.7 5.1 %collective-permute-start.10 = (f32[104,128]{1,0:T(8,128)S(1)}, f32[104,128]{1,0:T(8,128)S(1)}, u32[]{:S(2)}, u32[]{:S(2)}) collective-permute-start(f32[104,128]{1,0:T(8,128)S(1)} %add.48.refs_0_), channel_id=1, source_target_pairs={{0,6},{1,7},{2,4},{3,5},{4,2},{5,3},{6,0},{7,1},{8,14},{9,15},{10,... | collective-permute-start | bytes 159752 | tf_op jit(solution)/shard_map/ppermute | solution.py:21
  55.2 4.1 %collective-permute-start.9 = (f32[104,128]{1,0:T(8,128)S(1)}, f32[104,128]{1,0:T(8,128)S(1)}, u32[]{:S(2)}, u32[]{:S(2)}) collective-permute-start(f32[104,128]{1,0:T(8,128)S(1)} %add.48.refs_0_), channel_id=1, source_target_pairs={{0,4},{1,5},{2,6},{3,7},{4,0},{5,1},{6,2},{7,3},{8,12},{9,13},{10,... | collective-permute-start | bytes 159752 | tf_op jit(solution)/shard_map/ppermute | solution.py:21
  55.8 4.1 %collective-permute-start.8 = (f32[104,128]{1,0:T(8,128)S(1)}, f32[104,128]{1,0:T(8,128)S(1)}, u32[]{:S(2)}, u32[]{:S(2)}) collective-permute-start(f32[104,128]{1,0:T(8,128)S(1)} %add.48.refs_0_), channel_id=1, source_target_pairs={{0,2},{1,3},{2,0},{3,1},{4,6},{5,7},{6,4},{7,5},{8,10},{9,11},{10,... | collective-permute-start | bytes 159752 | tf_op jit(solution)/shard_map/ppermute | solution.py:21
  57.8 2.1 %copy-start.8 = (f32[104,128]{1,0:T(8,128)}, f32[104,128]{1,0:T(8,128)S(1)}, u32[]{:S(2)}) copy-start(f32[104,128]{1,0:T(8,128)S(1)} %collective-permute-done.10.refs_3_) | copy-start | bytes 159748
  57.8 10.0 %collective-permute-start.11 = (bf16[24,8192]{1,0:T(8,128)(2,1)S(1)}, bf16[24,8192]{1,0:T(8,128)(2,1)S(1)}, u32[]{:S(2)}, u32[]{:S(2)}) collective-permute-start(bf16[24,8192]{1,0:T(8,128)(2,1)S(1)} %get-tuple-element.6), channel_id=1, source_target_pairs={{0,8},{8,0},{16,24},{24,16},{1,9},{9,1},{17,25},{25,17},{2,10},{10... | collective-permute-start | bytes 1179656 | tf_op jit(solution)/shard_map/ppermute | solution.py:21
  67.0 1.2 %copy-start.1 = (f32[24,8192]{1,0:T(8,128)S(1)}, f32[24,8192]{1,0:T(8,128)}, u32[]{:S(2)}) copy-start(f32[24,8192]{1,0:T(8,128)} %param.7) | copy-start | bytes 2359300
  (2 other events, 1.2 us)

commit v2 on v1

v2 whole, which is shorter than its diff:
```python
import functools
import math

import jax
import jax.numpy as jnp
from jax import lax
from jax.experimental import pallas as pl
from jax.experimental.pallas import tpu as pltpu
from jax.sharding import PartitionSpec as P


LANES = 128
SUBLANES = 8


IN_VMEM = pl.BlockSpec(memory_space=pltpu.VMEM)
PIECE_ROWS = 32


def in_vmem(value):
    return pltpu.with_memory_space_constraint(value, pltpu.VMEM)


def in_hbm(value):
    return pltpu.with_memory_space_constraint(value, pltpu.HBM)


def vmem_call(kernel, outs, *operands):
    return pl.pallas_call(
        kernel,
        in_specs=[IN_VMEM] * len(operands),
        out_specs=[IN_VMEM] * len(outs),
        out_shape=[pltpu.VMEM(shape, dtype) for shape, dtype in outs],
    )(*map(in_vmem, operands))


def round_up(value, step):
    return -(-value // step) * step


def exchange(value, axis, distance):
    count = lax.axis_size(axis)
    return lax.ppermute(value, axis, [(i, i ^ distance) for i in range(count)])


def stages(count):
    bits = count.bit_length() - 1
    low, groups = 1, []
    while low < bits:
        width = min(2, bits - low)
        groups.append([step << low for step in range(1, 1 << width)])
        low += width
    return groups + ([[1]] if bits else [])


def gather_pieces(value, axis):
    stacks, offsets = [value], [[0]]
    for group in stages(lax.axis_size(axis)):
        whole = stacks[0] if len(stacks) == 1 else jnp.concatenate(stacks, axis=0)
        held = [offset for part in offsets for offset in part]
        stacks = [whole] + [exchange(whole, axis, distance) for distance in group]
        offsets = [held] + [[offset ^ distance for offset in held] for distance in group]
    return stacks, offsets


def two_parts(value):
    high = value.astype(jnp.bfloat16).astype(jnp.float32)
    return high, value - high


def predict_kernel(offsets, j_dev, blocks_dev, *refs):
    stack_refs = refs[: len(offsets)]
    sens_ref, block_ref, pert_ref, obs_ref, noise_ref, sent_ref, misfit_ref = refs[len(offsets) :]
    obs_dev = sens_ref.shape[0]
    rows = j_dev * blocks_dev
    tile = min(obs_dev, 2 * LANES)
    means, folded = [], jnp.zeros((1, LANES), jnp.float32)
    for start in range(0, obs_dev, tile):
        cols = pl.ds(start, tile)
        sens = sens_ref[cols, :]
        local = block_ref[:, cols] - lax.broadcasted_iota(jnp.int32, (blocks_dev, tile), 0)
        total = jnp.zeros((j_dev, blocks_dev, tile), jnp.float32)
        for stack_ref, held in zip(stack_refs, offsets):
            for place, offset in enumerate(held):
                piece = stack_ref[pl.ds(place * rows, rows), :]
                product = lax.dot_general(
                    piece, sens, (((1,), (1,)), ((), ())), preferred_element_type=jnp.float32
                ).reshape(j_dev, blocks_dev, tile)
                first_block = (lax.axis_index("vox") ^ offset) * blocks_dev
                total = total + jnp.where((local == first_block)[None], product, 0.0)
        predicted = jnp.sum(total, axis=1)
        misfit = ((obs_ref[:, cols] - predicted) / noise_ref[:, cols] + pert_ref[:, cols]).astype(jnp.bfloat16)
        misfit_ref[:, cols] = misfit
        mean = jnp.sum(predicted, axis=0, keepdims=True) * (1.0 / j_dev)
        sent_ref[:, cols] = (predicted - mean).astype(jnp.bfloat16)
        wide = misfit.astype(jnp.float32)
        squares = jnp.sum(wide * wide, axis=0, keepdims=True)
        for at in range(0, tile, LANES):
            means.append(mean[:, at : at + LANES])
            folded = folded + squares[:, at : at + LANES]
    mean_high, mean_low = two_parts(jnp.concatenate(means, axis=0))
    square_high, square_low = two_parts(folded)
    extra = [mean_high, mean_low, square_high, square_low]
    spare = j_dev - sum(part.shape[0] for part in extra)
    extra.append(jnp.zeros((spare, LANES), jnp.float32))
    sent_ref[:, pl.ds(obs_dev, LANES)] = jnp.concatenate(extra, axis=0).astype(jnp.bfloat16)


def pair_kernel(groups, j_dev, scale_root, *refs):
    sent_refs = refs[:groups]
    misfit_ref, noise_ref, out_ref = refs[groups:]
    members = groups * j_dev
    obs_dev = noise_ref.shape[1]
    strips = obs_dev // LANES
    means, squares = [], jnp.zeros((1, LANES), jnp.float32)
    for ref in sent_refs:
        extra = ref[:, pl.ds(obs_dev, LANES)].astype(jnp.float32)
        mean = extra[:strips] + extra[strips : 2 * strips]
        means.append(jnp.concatenate([mean[i : i + 1] for i in range(strips)], axis=1))
        squares = squares + extra[2 * strips : 2 * strips + 1] + extra[2 * strips + 1 : 2 * strips + 2]
    centre = sum(means) * (1.0 / groups)
    shrink = 1.0 / (noise_ref[...] * scale_root)
    scaled = jnp.concatenate(
        [
            (ref[:, pl.ds(0, obs_dev)].astype(jnp.float32) + (mean - centre)) * shrink
            for ref, mean in zip(sent_refs, means)
        ],
        axis=0,
    )
    width = out_ref.shape[1]
    right = [scaled, misfit_ref[...].astype(jnp.float32)]
    pad = width - members - j_dev
    if pad:
        right.append(jnp.zeros((pad, obs_dev), jnp.float32))
    out_ref[pl.ds(0, members), :] = lax.dot_general(
        scaled.astype(jnp.bfloat16),
        jnp.concatenate(right, axis=0).astype(jnp.bfloat16),
        (((1,), (1,)), ((), ())),
        preferred_element_type=jnp.float32,
    )
    first = lax.broadcasted_iota(jnp.int32, (SUBLANES, LANES), 0) == 0
    tail = jnp.where(first, jnp.broadcast_to(squares, (SUBLANES, LANES)), 0.0)
    if width > LANES:
        tail = jnp.concatenate([tail, jnp.zeros((SUBLANES, width - LANES), jnp.float32)], axis=1)
    out_ref[pl.ds(members, SUBLANES), :] = tail


def solve_turned(members, j_dev, count, part_refs):
    tile = (SUBLANES, LANES)
    groups = members // SUBLANES
    lane = lax.broadcasted_iota(jnp.int32, tile, 1)
    sub = lax.broadcasted_iota(jnp.int32, tile, 0)

    def load(group):
        rows = pl.ds(group * SUBLANES, SUBLANES)
        values = [ref[rows, :] for ref in part_refs]
        while len(values) > 1:
            values = [a + b for a, b in zip(values[::2], values[1::2])] + values[len(values) // 2 * 2 :]
        return values[0]

    damping = jnp.sum(load(groups), keepdims=True) * (1.0 / count)
    damping = jnp.broadcast_to(damping, tile)
    matrix = []
    for group in range(groups):
        matrix.append(load(group) + jnp.where(lane == sub + group * SUBLANES, damping, 0.0))

    def column(value, at):
        return jnp.broadcast_to(value[:, at : at + 1], tile)

    for block in range(groups):
        base = block * SUBLANES
        rows = [jnp.broadcast_to(matrix[block][i : i + 1, :], tile) for i in range(SUBLANES)]
        pivot = {(i, j): column(rows[i], base + j) for i in range(SUBLANES) for j in range(i, SUBLANES)}
        inverse = []
        for k in range(SUBLANES):
            inverse.append(1.0 / pivot[k, k])
            for i in range(k + 1, SUBLANES):
                factor = pivot[k, i] * inverse[k]
                for j in range(i, SUBLANES):
                    pivot[i, j] = pivot[i, j] - factor * pivot[k, j]
                rows[i] = rows[i] - factor * rows[k]
        for k in range(SUBLANES - 1, -1, -1):
            rows[k] = rows[k] * inverse[k]
            for i in range(k):
                rows[i] = rows[i] - pivot[i, k] * rows[k]
        for group in range(groups):
            if group == block:
                value = rows[0]
                for i in range(1, SUBLANES):
                    value = jnp.where(sub == i, rows[i], value)
            else:
                value = matrix[group]
                for i in range(SUBLANES):
                    value = value - column(matrix[group], base + i) * rows[i]
            matrix[group] = value
    padded = []
    for start in range(0, groups, j_dev // SUBLANES):
        padded += matrix[start : start + j_dev // SUBLANES]
        padded += [jnp.zeros(tile, jnp.float32)] * ((PIECE_ROWS - j_dev) // SUBLANES)
    padded += [jnp.zeros(tile, jnp.float32)] * (-len(padded) % (LANES // SUBLANES))
    turned = jnp.transpose(jnp.concatenate(padded, axis=0))
    return turned[members : members + j_dev, : members // j_dev * PIECE_ROWS].astype(jnp.bfloat16)


def solve_plain(parts, members, j_dev, count):
    total = functools.reduce(jnp.add, parts)
    damping = jnp.sum(total[members:]) / count
    system = total[:members, :members] + damping * jnp.eye(members, dtype=jnp.float32)
    cross = total[:members, members : members + j_dev]
    factor = jnp.linalg.cholesky(system)
    halfway = lax.linalg.triangular_solve(factor, cross, left_side=True, lower=True)
    weights = lax.linalg.triangular_solve(factor, halfway, left_side=True, lower=True, transpose_a=True)
    return weights.astype(jnp.bfloat16)


def mix(weights, anomalies):
    stack = []
    for anomaly in anomalies:
        stack += [anomaly, jnp.zeros((PIECE_ROWS - anomaly.shape[0], anomaly.shape[1]), jnp.bfloat16)]
    return lax.dot_general(
        weights, jnp.concatenate(stack, axis=0), (((1,), (0,)), ((), ())), preferred_element_type=jnp.float32
    )


def weigh_kernel(members, j_dev, count, scale_root, shares, parts, *refs):
    part_refs, refs = refs[:parts], refs[parts:]
    fetched = 1 + sum(shares)
    hbm_refs, (weights_ref, mixed_ref), refs = refs[:fetched], refs[fetched : fetched + 2], refs[fetched + 2 :]
    local_refs, semaphores = refs[:fetched], refs[fetched]
    fetches = [
        pltpu.make_async_copy(far, near, semaphores.at[number])
        for number, (far, near) in enumerate(zip(hbm_refs, local_refs))
    ]
    for fetch in fetches:
        fetch.start()
    weights = solve_turned(members, j_dev, count, part_refs)
    weights_ref[...] = weights
    for fetch in fetches:
        fetch.wait()
    log_ref, piece_refs = local_refs[0], local_refs[1:]
    vox_dev = mixed_ref.shape[1]
    tile = min(vox_dev, SUBLANES * LANES)
    for start in range(0, vox_dev, tile):
        cols = pl.ds(start, tile)
        own = log_ref[:, cols]
        anomalies, at = [own.astype(jnp.bfloat16)], 0
        for share in shares:
            anomalies.append(functools.reduce(jnp.add, [ref[:, cols] for ref in piece_refs[at : at + share]]))
            at += share
        mixed_ref[:, cols] = own + mix(weights, anomalies) * (1.0 / scale_root)


def finish_kernel(scale_root, weights_ref, mixed_ref, last_ref, out_hbm, out_ref, semaphores):
    vox_dev = mixed_ref.shape[1]
    tile = vox_dev // semaphores.shape[0]
    weights = weights_ref[...]
    weights = weights[:, weights.shape[1] - PIECE_ROWS :]
    copies = []
    for number in range(semaphores.shape[0]):
        cols = pl.ds(number * tile, tile)
        out_ref[:, cols] = mixed_ref[:, cols] + mix(weights, [last_ref[:, cols]]) * (1.0 / scale_root)
        copy = pltpu.make_async_copy(out_ref.at[:, cols], out_hbm.at[:, cols], semaphores.at[number])
        copy.start()
        copies.append(copy)
    for copy in copies:
        copy.wait()


def weigh(parts, log_modulus, pieces, members, count, scale_root):
    j_dev, vox_dev = log_modulus.shape
    flat = [piece for share in pieces for piece in share]
    return pl.pallas_call(
        functools.partial(
            weigh_kernel, members, j_dev, count, scale_root, [len(share) for share in pieces], len(parts)
        ),
        in_specs=[IN_VMEM] * len(parts) + [pl.BlockSpec(memory_space=pl.ANY)] * (1 + len(flat)),
        out_specs=[IN_VMEM] * 2,
        out_shape=[
            pltpu.VMEM((j_dev, members // j_dev * PIECE_ROWS), jnp.bfloat16),
            pltpu.VMEM((j_dev, vox_dev), jnp.float32),
        ],
        scratch_shapes=[pltpu.VMEM((j_dev, vox_dev), jnp.float32)]
        + [pltpu.VMEM((j_dev, vox_dev), jnp.bfloat16)] * len(flat)
        + [pltpu.SemaphoreType.DMA((1 + len(flat),))],
    )(*map(in_vmem, parts), log_modulus, *flat)


def finish(weights, mixed, last, scale_root):
    j_dev, vox_dev = mixed.shape
    return pl.pallas_call(
        functools.partial(finish_kernel, scale_root),
        in_specs=[IN_VMEM] * 3,
        out_specs=pl.BlockSpec(memory_space=pl.ANY),
        out_shape=jax.ShapeDtypeStruct((j_dev, vox_dev), jnp.float32),
        scratch_shapes=[
            pltpu.VMEM((j_dev, vox_dev), jnp.float32),
            pltpu.SemaphoreType.DMA((vox_dev // min(vox_dev, SUBLANES * LANES),)),
        ],
    )(*map(in_vmem, [weights, mixed, last]))


def pairs_exchange(value, axis, pairs):
    return lax.ppermute(value, axis, pairs)


def on_device(log_modulus, basis, sensitivity, obs_block, observed, noise_scale, perturbation):
    n_vox = lax.axis_size("vox")
    n_grp = lax.axis_size("grp")
    j_dev, vox_dev = log_modulus.shape
    block_vox, _ = basis.shape
    blocks_dev = vox_dev // block_vox
    obs_dev = sensitivity.shape[0]
    members = j_dev * n_grp
    scale_root = math.sqrt(members - 1)

    low = log_modulus.astype(jnp.bfloat16)
    compliance = jnp.exp(-log_modulus).astype(jnp.bfloat16)
    features = jnp.dot(
        compliance.reshape(j_dev * blocks_dev, block_vox), basis, preferred_element_type=jnp.float32
    ).astype(jnp.bfloat16)

    block = obs_block.reshape(1, obs_dev)
    observed = observed.reshape(1, obs_dev)
    noise = noise_scale.reshape(1, obs_dev)
    stacks, offsets = gather_pieces(features, "vox")
    line = n_grp == 4
    if line:
        near = in_hbm(exchange(low, "grp", 1))
        middle = in_hbm(pairs_exchange(low, "grp", [(1, 2), (2, 1)]))
    sent, misfit = vmem_call(
        functools.partial(predict_kernel, offsets, j_dev, blocks_dev),
        [((j_dev, obs_dev + LANES), jnp.bfloat16), ((j_dev, obs_dev), jnp.bfloat16)],
        *stacks,
        sensitivity,
        block,
        perturbation,
        observed,
        noise,
    )
    payloads = [sent] + [exchange(sent, "grp", distance) for distance in range(1, n_grp)]
    if line:
        ends = [(1, 0), (2, 3)]
        near_far = in_hbm(pairs_exchange(near, "grp", [(1, 2), (2, 1)]))
        middle_far = in_hbm(pairs_exchange(middle, "grp", ends))
    width = round_up(members + j_dev, LANES)
    (partial_sums,) = vmem_call(
        functools.partial(pair_kernel, n_grp, j_dev, scale_root),
        [((members + SUBLANES, width), jnp.float32)],
        *payloads,
        misfit,
        noise,
    )
    parts = [partial_sums]
    for group in reversed(stages(n_vox)):
        total = functools.reduce(jnp.add, parts)
        parts = [total] + [exchange(total, "vox", distance) for distance in group]
    count = members * obs_dev * n_vox
    if line:
        far = pairs_exchange(near_far, "grp", ends)
        weights, mixed = weigh(
            parts, log_modulus, [[near], [near_far, middle_far], [middle]], members, count, scale_root
        )
        return finish(weights, mixed, far, scale_root)
    weights = solve_plain(parts, members, j_dev, count)
    mixture = jnp.zeros_like(log_modulus)
    for distance in range(n_grp):
        anomaly = exchange(low, "grp", distance) if distance else low
        own_weights = weights[distance * j_dev : (distance + 1) * j_dev]
        mixture += lax.dot_general(
            own_weights, anomaly, (((0,), (0,)), ((), ())), preferred_element_type=jnp.float32
        )
    return log_modulus + mixture / scale_root


def solution(mesh):
    in_specs = (
        P("grp", "vox"),
        P(),
        P("vox", None),
        P("vox", None),
        P("vox"),
        P("vox"),
        P("grp", "vox"),
    )
    out_specs = P("grp", "vox")

    return jax.shard_map(on_device, mesh=mesh, in_specs=in_specs, out_specs=out_specs, check_vma=False)
```

time: 69.9 us -> 58.8 us (0.84)
  waiting for transfers between devices: 30.2 us -> 26.1 us
  local copies, waits for them, and re-layouts: 3.44 us -> 0.22 us
  starting transfers between devices: 19.5 us -> 22.6 us
  matrix products: 2.69 us -> 0.26 us
  other arithmetic: 3.81 us -> 1.57 us
  Pallas kernels: 9.74 us -> 7.61 us
    ppermute x0 -> x4, starting transfers between devices: none -> 4.65 us  [pairs_exchange(): return lax.ppermute(value, axis, pairs)]
    ppermute x14 -> x12, waiting for transfers between devices: 30.2 us -> 26.1 us  [exchange(): return lax.ppermute(value, axis, [(i, i ^ distance) for i in range(count)])]
    unnamed x24 -> x16, local copies, waits for them, and re-layouts: 3.26 us -> 0.04 us
    dot_general x4 -> x0, matrix products: 2.44 us -> none  [on_device(): lax.dot_general(weights_low[place * j_dev:(place + 1) * j_dev], anomaly,...]
    pallas_call x3 -> x4, Pallas kernels: 9.74 us -> 7.61 us  [the longest x1 5.19 us: weigh(): pl.pallas_call(functools.partial(weigh_kernel, members, j_dev, count, sca...]
    ppermute x14 -> x12, starting transfers between devices: 19.5 us -> 17.9 us  [exchange(): return lax.ppermute(value, axis, [(i, i ^ distance) for i in range(count)])]
    add x1, other arithmetic: 0.82 us -> 0.01 us  [on_device(): total = functools.reduce(jnp.add, parts)]
    another operation x1 -> x0, other arithmetic: 0.8 us -> none
  transfers between devices with their start and end apart: 14 -> 16, of which waited for: 8 -> 10; matrix products, arithmetic and copies ran while one was open for 4% -> 1% of each run, Pallas kernels for 14% -> 11%
where the time goes in v2:
time: 58.8 us; the launch traced here: 58.5 us
  waiting for transfers between devices  26.1 us (44%)
  starting transfers between devices  22.6 us (38%)
  Pallas kernels  7.61 us (13%)
  other arithmetic  1.57 us (3%)
    ppermute x12, waiting for transfers between devices, exchange(): return lax.ppermute(value, axis, [(i, i ^ distance) for i in range(count)])  26.1 us
    ppermute x12, starting transfers between devices, exchange(): return lax.ppermute(value, axis, [(i, i ^ distance) for i in range(count)])  17.9 us
    pallas_call x1, Pallas kernels, weigh(): pl.pallas_call(functools.partial(weigh_kernel, members, j_dev, count, sca...  5.19 us
    ppermute x4, starting transfers between devices, pairs_exchange(): return lax.ppermute(value, axis, pairs)  4.65 us
    convert_element_type x1, other arithmetic, on_device(): low = log_modulus.astype(jnp.bfloat16)  1.54 us
    pallas_call x2, Pallas kernels, vmem_call(): pl.pallas_call(kernel, in_specs=[IN_VMEM] * len(operands), out_specs=[IN_...  1.26 us
  transfers between devices with their start and end apart: 16, of which 10 were waited for; matrix products, arithmetic and copies ran while one was open for 1% of the time, Pallas kernels for 11%

profile of v2, /device:TPU:0, one launch (start us, length us, event | category | flops | bytes accessed | tf_op | source)
XLA Modules:
  0.0 58.5 jit_solution(11369459290876047161)
XLA Ops:
  0.0 1.5 %fusion = (bf16[24,8192]{1,0:T(8,128)(2,1)S(1)}, bf16[24,8192]{1,0:T(8,128)(2,1)S(1)}) fusion(f32[24,8192]{1,0:T(8,128)} %refs_4_.3), kind=kLoop, calls=%fused_computation.3 | loop fusion | flops 589824 | bytes 1572864 | tf_op jit(solution)/shard_map/convert_element_type | solution.py:316
  1.6 3.1 %collective-permute-start.11 = (bf16[24,8192]{1,0:T(8,128)(2,1)S(1)}, bf16[24,8192]{1,0:T(8,128)(2,1)S(1)}, u32[]{:S(2)}, u32[]{:S(2)}) collective-permute-start(bf16[24,8192]{1,0:T(8,128)(2,1)S(1)} %get-tuple-element.13), channel_id=1, source_target_pairs={{0,8},{8,0},{16,24},{24,16},{1,9},{9,1},{17,25},{25,17},{2,10},{10... | collective-permute-start | bytes 1179656 | tf_op jit(solution)/shard_map/ppermute | solution.py:43
  4.7 0.7 %collective-permute-start.13 = (bf16[24,8192]{1,0:T(8,128)(2,1)S(1)}, bf16[24,8192]{1,0:T(8,128)(2,1)S(1)}, u32[]{:S(2)}, u32[]{:S(2)}) collective-permute-start(bf16[24,8192]{1,0:T(8,128)(2,1)S(1)} %get-tuple-element.13), channel_id=1, source_target_pairs={{8,16},{16,8},{9,17},{17,9},{10,18},{18,10},{11,19},{19,11},{12,20... | collective-permute-start | bytes 1179656 | tf_op jit(solution)/shard_map/ppermute | solution.py:303
  5.3 8.4 %collective-permute-done.11.refs_5_ = bf16[24,8192]{1,0:T(8,128)(2,1)S(1)} collective-permute-done((bf16[24,8192]{1,0:T(8,128)(2,1)S(1)}, bf16[24,8192]{1,0:T(8,128)(2,1)S(1)}, u32[]{:S(2)}, u32[]{:S(2)}) %collective-permute-start.11) | collective-permute-done | bytes 393248 | tf_op jit(solution)/shard_map/ppermute | solution.py:43
  13.8 1.4 %collective-permute-start.12 = (bf16[24,8192]{1,0:T(8,128)(2,1)S(1)}, bf16[24,8192]{1,0:T(8,128)(2,1)}, u32[]{:S(2)}, u32[]{:S(2)}) collective-permute-start(bf16[24,8192]{1,0:T(8,128)(2,1)S(1)} %collective-permute-done.11.refs_5_), channel_id=1, source_target_pairs={{8,16},{16,8},{9,17},{17,9},{10,18},{18,10},{11,19},{19,11},{12,20... | collective-permute-start | bytes 1179656 | tf_op jit(solution)/shard_map/ppermute | solution.py:303
  15.7 2.7 %collective-permute-start.2 = (bf16[192,128]{1,0:T(8,128)(2,1)S(1)}, bf16[192,128]{1,0:T(8,128)(2,1)S(1)}, u32[]{:S(2)}, u32[]{:S(2)}) collective-permute-start(bf16[192,128]{1,0:T(8,128)(2,1)S(1)} %convolution_convert_fusion), channel_id=1, source_target_pairs={{0,6},{1,7},{2,4},{3,5},{4,2},{5,3},{6,0},{7,1},{8,14},{9,15},{10,... | collective-permute-start | bytes 147464 | tf_op jit(solution)/shard_map/ppermute | solution.py:43
  19.2 1.3 %collective-permute-start.14 = (bf16[24,8192]{1,0:T(8,128)(2,1)S(1)}, bf16[24,8192]{1,0:T(8,128)(2,1)}, u32[]{:S(2)}, u32[]{:S(2)}) collective-permute-start(bf16[24,8192]{1,0:T(8,128)(2,1)S(1)} %collective-permute-done.13.refs_8_), channel_id=1, source_target_pairs={{8,0},{16,24},{9,1},{17,25},{10,2},{18,26},{11,3},{19,27},{12,4},{... | collective-permute-start | bytes 1179656 | tf_op jit(solution)/shard_map/ppermute | solution.py:303
  20.5 1.3 %collective-permute-start.15 = (bf16[24,8192]{1,0:T(8,128)(2,1)}, bf16[24,8192]{1,0:T(8,128)(2,1)S(1)}, u32[]{:S(2)}, u32[]{:S(2)}) collective-permute-start(bf16[24,8192]{1,0:T(8,128)(2,1)} %collective-permute-done.12.refs_6_), channel_id=1, source_target_pairs={{8,0},{16,24},{9,1},{17,25},{10,2},{18,26},{11,3},{19,27},{12,4},{... | collective-permute-start | bytes 1179656 | tf_op jit(solution)/shard_map/ppermute | solution.py:303
  21.9 0.6 %collective-permute-done.1 = bf16[192,128]{1,0:T(8,128)(2,1)S(1)} collective-permute-done((bf16[192,128]{1,0:T(8,128)(2,1)S(1)}, bf16[192,128]{1,0:T(8,128)(2,1)S(1)}, u32[]{:S(2)}, u32[]{:S(2)}) %collective-permute-start.1) | collective-permute-done | bytes 49184 | tf_op jit(solution)/shard_map/ppermute | solution.py:43
  23.1 1.4 %collective-permute-done.3.refs_1_ = bf16[768,128]{1,0:T(8,128)(2,1)S(1)} collective-permute-done((bf16[768,128]{1,0:T(8,128)(2,1)S(1)}, bf16[768,128]{1,0:T(8,128)(2,1)S(1)}, u32[]{:S(2)}, u32[]{:S(2)}) %collective-permute-start.3) | collective-permute-done | bytes 196640 | tf_op jit(solution)/shard_map/ppermute | solution.py:43
  24.5 1.0 %shard_map.73 = (bf16[24,1152]{1,0:T(8,128)(2,1)S(1)}, bf16[24,1024]{1,0:T(8,128)(2,1)S(1)}) custom-call(bf16[768,128]{1,0:T(8,128)(2,1)S(1)} %pad_maximum_fusion.refs_0_, bf16[768,128]{1,0:T(8,128)(2,1)S(1)} %collective-permute-done.3.refs_1_, bf16[1024,128]{1,0:T(8,128)(2,1)S(1)} %copy-done.1, s32[1,1024]{1,0:T(1,128)S(1)} %bitcast.7, ...), custom_call_target="tpu_custom_call" | custom-call | tf_op jit(solution)/shard_map/pallas_call | solution.py:29
  25.6 3.7 %collective-permute-start.6 = (bf16[24,1152]{1,0:T(8,128)(2,1)S(1)}, bf16[24,1152]{1,0:T(8,128)(2,1)S(1)}, u32[]{:S(2)}, u32[]{:S(2)}) collective-permute-start(bf16[24,1152]{1,0:T(8,128)(2,1)S(1)} %get-tuple-element.9.refs_0_), channel_id=1, source_target_pairs={{0,24},{8,16},{16,8},{24,0},{1,25},{9,17},{17,9},{25,1},{2,26},{10... | collective-permute-start | bytes 165896 | tf_op jit(solution)/shard_map/ppermute | solution.py:43
  29.2 3.8 %collective-permute-start.5 = (bf16[24,1152]{1,0:T(8,128)(2,1)S(1)}, bf16[24,1152]{1,0:T(8,128)(2,1)S(1)}, u32[]{:S(2)}, u32[]{:S(2)}) collective-permute-start(bf16[24,1152]{1,0:T(8,128)(2,1)S(1)} %get-tuple-element.9.refs_0_), channel_id=1, source_target_pairs={{0,16},{8,24},{16,0},{24,8},{1,17},{9,25},{17,1},{25,9},{2,18},{10... | collective-permute-start | bytes 165896 | tf_op jit(solution)/shard_map/ppermute | solution.py:43
  33.1 3.6 %collective-permute-done.5.refs_2_ = bf16[24,1152]{1,0:T(8,128)(2,1)S(1)} collective-permute-done((bf16[24,1152]{1,0:T(8,128)(2,1)S(1)}, bf16[24,1152]{1,0:T(8,128)(2,1)S(1)}, u32[]{:S(2)}, u32[]{:S(2)}) %collective-permute-start.5) | collective-permute-done | bytes 55328 | tf_op jit(solution)/shard_map/ppermute | solution.py:43
  36.8 6.7 %collective-permute-done.4.refs_1_ = bf16[24,1152]{1,0:T(8,128)(2,1)S(1)} collective-permute-done((bf16[24,1152]{1,0:T(8,128)(2,1)S(1)}, bf16[24,1152]{1,0:T(8,128)(2,1)S(1)}, u32[]{:S(2)}, u32[]{:S(2)}) %collective-permute-start.4) | collective-permute-done | bytes 55328 | tf_op jit(solution)/shard_map/ppermute | solution.py:43
  43.8 1.2 %collective-permute-done.7 = f32[104,128]{1,0:T(8,128)S(1)} collective-permute-done((f32[104,128]{1,0:T(8,128)S(1)}, f32[104,128]{1,0:T(8,128)S(1)}, u32[]{:S(2)}, u32[]{:S(2)}) %collective-permute-start.7) | collective-permute-done | bytes 53280 | tf_op jit(solution)/shard_map/ppermute | solution.py:43
  45.0 2.5 %collective-permute-start.10 = (f32[104,128]{1,0:T(8,128)S(1)}, f32[104,128]{1,0:T(8,128)S(1)}, u32[]{:S(2)}, u32[]{:S(2)}) collective-permute-start(f32[104,128]{1,0:T(8,128)S(1)} %add.3.refs_0_), channel_id=1, source_target_pairs={{0,6},{1,7},{2,4},{3,5},{4,2},{5,3},{6,0},{7,1},{8,14},{9,15},{10,... | collective-permute-start | bytes 159752 | tf_op jit(solution)/shard_map/ppermute | solution.py:43
  47.5 0.5 collective-permute-start.9
  48.0 0.5 collective-permute-start.8
  48.6 1.6 %collective-permute-done.10.refs_3_ = f32[104,128]{1,0:T(8,128)S(1)} collective-permute-done((f32[104,128]{1,0:T(8,128)S(1)}, f32[104,128]{1,0:T(8,128)S(1)}, u32[]{:S(2)}, u32[]{:S(2)}) %collective-permute-start.10) | collective-permute-done | bytes 53280 | tf_op jit(solution)/shard_map/ppermute | solution.py:43
  50.1 1.5 %collective-permute-done.9.refs_2_ = f32[104,128]{1,0:T(8,128)S(1)} collective-permute-done((f32[104,128]{1,0:T(8,128)S(1)}, f32[104,128]{1,0:T(8,128)S(1)}, u32[]{:S(2)}, u32[]{:S(2)}) %collective-permute-start.9) | collective-permute-done | bytes 53280 | tf_op jit(solution)/shard_map/ppermute | solution.py:43
  51.6 0.5 collective-permute-done.8.refs_1_
  52.2 5.2 %shard_map.75 = (bf16[24,128]{1,0:T(8,128)(2,1)S(1)}, f32[24,8192]{1,0:T(8,128)S(1)}) custom-call(f32[104,128]{1,0:T(8,128)S(1)} %add.3.refs_0_, f32[104,128]{1,0:T(8,128)S(1)} %collective-permute-done.8.refs_1_, f32[104,128]{1,0:T(8,128)S(1)} %collective-permute-done.9.refs_2_, f32[104,128]{1,0:T(8,128)S(1)} %collective-permute-done.10.refs_3_, ...), custom_call_target="tpu_custom_call" | custom-call | tf_op jit(solution)/shard_map/pallas_call | solution.py:272
  57.4 1.2 %shard_map.76 = f32[24,8192]{1,0:T(8,128)} custom-call(bf16[24,128]{1,0:T(8,128)(2,1)S(1)} %get-tuple-element.11.weights_ref, f32[24,8192]{1,0:T(8,128)S(1)} %get-tuple-element.12.mixed_ref, bf16[24,8192]{1,0:T(8,128)(2,1)S(1)} %collective-permute-done.15.last_ref), custom_call_target="tpu_custom_call" | custom-call | tf_op jit(solution)/shard_map/pallas_call | solution.py:290
  (33 shorter events, 2.4 us)
Async XLA Ops:
  0.0 15.4 %copy-start = (bf16[1024,128]{1,0:T(8,128)(2,1)S(1)}, bf16[1024,128]{1,0:T(8,128)(2,1)}, u32[]{:S(2)}) copy-start(bf16[1024,128]{1,0:T(8,128)(2,1)} %param.8) | copy-start | bytes 786436
  1.6 12.2 %collective-permute-start.11 = (bf16[24,8192]{1,0:T(8,128)(2,1)S(1)}, bf16[24,8192]{1,0:T(8,128)(2,1)S(1)}, u32[]{:S(2)}, u32[]{:S(2)}) collective-permute-start(bf16[24,8192]{1,0:T(8,128)(2,1)S(1)} %get-tuple-element.13), channel_id=1, source_target_pairs={{0,8},{8,0},{16,24},{24,16},{1,9},{9,1},{17,25},{25,17},{2,10},{10... | collective-permute-start | bytes 1179656 | tf_op jit(solution)/shard_map/ppermute | solution.py:43
  4.7 14.6 %collective-permute-start.13 = (bf16[24,8192]{1,0:T(8,128)(2,1)S(1)}, bf16[24,8192]{1,0:T(8,128)(2,1)S(1)}, u32[]{:S(2)}, u32[]{:S(2)}) collective-permute-start(bf16[24,8192]{1,0:T(8,128)(2,1)S(1)} %get-tuple-element.13), channel_id=1, source_target_pairs={{8,16},{16,8},{9,17},{17,9},{10,18},{18,10},{11,19},{19,11},{12,20... | collective-permute-start | bytes 1179656 | tf_op jit(solution)/shard_map/ppermute | solution.py:303
  13.8 1.6 %copy-start.6 = (bf16[24,8192]{1,0:T(8,128)(2,1)}, bf16[24,8192]{1,0:T(8,128)(2,1)S(1)}, u32[]{:S(2)}) copy-start(bf16[24,8192]{1,0:T(8,128)(2,1)S(1)} %collective-permute-done.11.refs_5_) | copy-start | bytes 1179652
  13.8 6.8 %collective-permute-start.12 = (bf16[24,8192]{1,0:T(8,128)(2,1)S(1)}, bf16[24,8192]{1,0:T(8,128)(2,1)}, u32[]{:S(2)}, u32[]{:S(2)}) collective-permute-start(bf16[24,8192]{1,0:T(8,128)(2,1)S(1)} %collective-permute-done.11.refs_5_), channel_id=1, source_target_pairs={{8,16},{16,8},{9,17},{17,9},{10,18},{18,10},{11,19},{19,11},{12,20... | collective-permute-start | bytes 1179656 | tf_op jit(solution)/shard_map/ppermute | solution.py:303
  15.7 8.8 %copy-start.1 = (bf16[1024,128]{1,0:T(8,128)(2,1)S(1)}, bf16[1024,128]{1,0:T(8,128)(2,1)}, u32[]{:S(2)}) copy-start(bf16[1024,128]{1,0:T(8,128)(2,1)} %refs_2_.1) | copy-start | bytes 786436
  15.7 8.8 %copy-start.2 = (f32[24,1024]{1,0:T(8,128)S(1)}, f32[24,1024]{1,0:T(8,128)}, u32[]{:S(2)}) copy-start(f32[24,1024]{1,0:T(8,128)} %refs_4_.2) | copy-start | bytes 294916
  15.7 6.2 %collective-permute-start.2 = (bf16[192,128]{1,0:T(8,128)(2,1)S(1)}, bf16[192,128]{1,0:T(8,128)(2,1)S(1)}, u32[]{:S(2)}, u32[]{:S(2)}) collective-permute-start(bf16[192,128]{1,0:T(8,128)(2,1)S(1)} %convolution_convert_fusion), channel_id=1, source_target_pairs={{0,6},{1,7},{2,4},{3,5},{4,2},{5,3},{6,0},{7,1},{8,14},{9,15},{10,... | collective-permute-start | bytes 147464 | tf_op jit(solution)/shard_map/ppermute | solution.py:43
  18.4 4.1 %collective-permute-start.1 = (bf16[192,128]{1,0:T(8,128)(2,1)S(1)}, bf16[192,128]{1,0:T(8,128)(2,1)S(1)}, u32[]{:S(2)}, u32[]{:S(2)}) collective-permute-start(bf16[192,128]{1,0:T(8,128)(2,1)S(1)} %convolution_convert_fusion), channel_id=1, source_target_pairs={{0,4},{1,5},{2,6},{3,7},{4,0},{5,1},{6,2},{7,3},{8,12},{9,13},{10,... | collective-permute-start | bytes 147464 | tf_op jit(solution)/shard_map/ppermute | solution.py:43
  18.9 4.1 %collective-permute-start = (bf16[192,128]{1,0:T(8,128)(2,1)S(1)}, bf16[192,128]{1,0:T(8,128)(2,1)S(1)}, u32[]{:S(2)}, u32[]{:S(2)}) collective-permute-start(bf16[192,128]{1,0:T(8,128)(2,1)S(1)} %convolution_convert_fusion), channel_id=1, source_target_pairs={{0,2},{1,3},{2,0},{3,1},{4,6},{5,7},{6,4},{7,5},{8,10},{9,11},{10,... | collective-permute-start | bytes 147464 | tf_op jit(solution)/shard_map/ppermute | solution.py:43
  19.2 6.3 %copy-start.7 = (bf16[24,8192]{1,0:T(8,128)(2,1)}, bf16[24,8192]{1,0:T(8,128)(2,1)S(1)}, u32[]{:S(2)}) copy-start(bf16[24,8192]{1,0:T(8,128)(2,1)S(1)} %collective-permute-done.13.refs_8_) | copy-start | bytes 1179652
  19.2 32.9 %collective-permute-start.14 = (bf16[24,8192]{1,0:T(8,128)(2,1)S(1)}, bf16[24,8192]{1,0:T(8,128)(2,1)}, u32[]{:S(2)}, u32[]{:S(2)}) collective-permute-start(bf16[24,8192]{1,0:T(8,128)(2,1)S(1)} %collective-permute-done.13.refs_8_), channel_id=1, source_target_pairs={{8,0},{16,24},{9,1},{17,25},{10,2},{18,26},{11,3},{19,27},{12,4},{... | collective-permute-start | bytes 1179656 | tf_op jit(solution)/shard_map/ppermute | solution.py:303
  20.5 36.8 %collective-permute-start.15 = (bf16[24,8192]{1,0:T(8,128)(2,1)}, bf16[24,8192]{1,0:T(8,128)(2,1)S(1)}, u32[]{:S(2)}, u32[]{:S(2)}) collective-permute-start(bf16[24,8192]{1,0:T(8,128)(2,1)} %collective-permute-done.12.refs_6_), channel_id=1, source_target_pairs={{8,0},{16,24},{9,1},{17,25},{10,2},{18,26},{11,3},{19,27},{12,4},{... | collective-permute-start | bytes 1179656 | tf_op jit(solution)/shard_map/ppermute | solution.py:303
  23.0 1.5 %copy-start.4 = (s32[1024,1]{0,1:T(1,128)S(1)}, s32[1024,1]{0,1:T(1,128)}, u32[]{:S(2)}) copy-start(s32[1024,1]{0,1:T(1,128)} %param.10) | copy-start | bytes 12292
  23.0 1.6 %copy-start.5 = (f32[1024]{0:T(1024)S(1)}, f32[1024]{0:T(1024)}, u32[]{:S(2)}) copy-start(f32[1024]{0:T(1024)} %param.11) | copy-start | bytes 12292
  23.0 1.5 %copy-start.3 = (f32[1024]{0:T(1024)S(1)}, f32[1024]{0:T(1024)}, u32[]{:S(2)}) copy-start(f32[1024]{0:T(1024)} %param.12) | copy-start | bytes 12292
  23.0 1.5 %collective-permute-start.3 = (bf16[768,128]{1,0:T(8,128)(2,1)S(1)}, bf16[768,128]{1,0:T(8,128)(2,1)S(1)}, u32[]{:S(2)}, u32[]{:S(2)}) collective-permute-start(bf16[768,128]{1,0:T(8,128)(2,1)S(1)} %pad_maximum_fusion.refs_0_), channel_id=1, source_target_pairs={{0,1},{1,0},{2,3},{3,2},{4,5},{5,4},{6,7},{7,6},{8,9},{9,8},{10,11... | collective-permute-start | bytes 589832 | tf_op jit(solution)/shard_map/ppermute | solution.py:43
  25.6 7.6 %collective-permute-start.6 = (bf16[24,1152]{1,0:T(8,128)(2,1)S(1)}, bf16[24,1152]{1,0:T(8,128)(2,1)S(1)}, u32[]{:S(2)}, u32[]{:S(2)}) collective-permute-start(bf16[24,1152]{1,0:T(8,128)(2,1)S(1)} %get-tuple-element.9.refs_0_), channel_id=1, source_target_pairs={{0,24},{8,16},{16,8},{24,0},{1,25},{9,17},{17,9},{25,1},{2,26},{10... | collective-permute-start | bytes 165896 | tf_op jit(solution)/shard_map/ppermute | solution.py:43
  29.2 7.5 %collective-permute-start.5 = (bf16[24,1152]{1,0:T(8,128)(2,1)S(1)}, bf16[24,1152]{1,0:T(8,128)(2,1)S(1)}, u32[]{:S(2)}, u32[]{:S(2)}) collective-permute-start(bf16[24,1152]{1,0:T(8,128)(2,1)S(1)} %get-tuple-element.9.refs_0_), channel_id=1, source_target_pairs={{0,16},{8,24},{16,0},{24,8},{1,17},{9,25},{17,1},{25,9},{2,18},{10... | collective-permute-start | bytes 165896 | tf_op jit(solution)/shard_map/ppermute | solution.py:43
  33.0 10.4 %collective-permute-start.4 = (bf16[24,1152]{1,0:T(8,128)(2,1)S(1)}, bf16[24,1152]{1,0:T(8,128)(2,1)S(1)}, u32[]{:S(2)}, u32[]{:S(2)}) collective-permute-start(bf16[24,1152]{1,0:T(8,128)(2,1)S(1)} %get-tuple-element.9.refs_0_), channel_id=1, source_target_pairs={{0,8},{8,0},{16,24},{24,16},{1,9},{9,1},{17,25},{25,17},{2,10},{10... | collective-permute-start | bytes 165896 | tf_op jit(solution)/shard_map/ppermute | solution.py:43
  43.7 1.3 %collective-permute-start.7 = (f32[104,128]{1,0:T(8,128)S(1)}, f32[104,128]{1,0:T(8,128)S(1)}, u32[]{:S(2)}, u32[]{:S(2)}) collective-permute-start(f32[104,128]{1,0:T(8,128)S(1)} %shard_map.74), channel_id=1, source_target_pairs={{0,1},{1,0},{2,3},{3,2},{4,5},{5,4},{6,7},{7,6},{8,9},{9,8},{10,11... | collective-permute-start | bytes 159752 | tf_op jit(solution)/shard_map/ppermute | solution.py:43
  45.0 5.1 %collective-permute-start.10 = (f32[104,128]{1,0:T(8,128)S(1)}, f32[104,128]{1,0:T(8,128)S(1)}, u32[]{:S(2)}, u32[]{:S(2)}) collective-permute-start(f32[104,128]{1,0:T(8,128)S(1)} %add.3.refs_0_), channel_id=1, source_target_pairs={{0,6},{1,7},{2,4},{3,5},{4,2},{5,3},{6,0},{7,1},{8,14},{9,15},{10,... | collective-permute-start | bytes 159752 | tf_op jit(solution)/shard_map/ppermute | solution.py:43
  47.5 4.1 %collective-permute-start.9 = (f32[104,128]{1,0:T(8,128)S(1)}, f32[104,128]{1,0:T(8,128)S(1)}, u32[]{:S(2)}, u32[]{:S(2)}) collective-permute-start(f32[104,128]{1,0:T(8,128)S(1)} %add.3.refs_0_), channel_id=1, source_target_pairs={{0,4},{1,5},{2,6},{3,7},{4,0},{5,1},{6,2},{7,3},{8,12},{9,13},{10,... | collective-permute-start | bytes 159752 | tf_op jit(solution)/shard_map/ppermute | solution.py:43
  48.0 4.1 %collective-permute-start.8 = (f32[104,128]{1,0:T(8,128)S(1)}, f32[104,128]{1,0:T(8,128)S(1)}, u32[]{:S(2)}, u32[]{:S(2)}) collective-permute-start(f32[104,128]{1,0:T(8,128)S(1)} %add.3.refs_0_), channel_id=1, source_target_pairs={{0,2},{1,3},{2,0},{3,1},{4,6},{5,7},{6,4},{7,5},{8,10},{9,11},{10,... | collective-permute-start | bytes 159752 | tf_op jit(solution)/shard_map/ppermute | solution.py:43

commit v3 on v2

--- a/solution.py
+++ b/solution.py
@@ -224,9 +224,10 @@
 
 def weigh_kernel(members, j_dev, count, scale_root, shares, parts, *refs):
     part_refs, refs = refs[:parts], refs[parts:]
-    fetched = 1 + sum(shares)
-    hbm_refs, (weights_ref, mixed_ref), refs = refs[:fetched], refs[fetched : fetched + 2], refs[fetched + 2 :]
-    local_refs, semaphores = refs[:fetched], refs[fetched]
+    given = 1 + sum(shares)
+    fetched = len(refs) - given - 3
+    held_refs, (weights_ref, mixed_ref), refs = refs[:given], refs[given : given + 2], refs[given + 2 :]
+    hbm_refs, (local_refs, semaphores) = held_refs[:fetched], (list(refs[:fetched]), refs[fetched])
     fetches = [
         pltpu.make_async_copy(far, near, semaphores.at[number])
         for number, (far, near) in enumerate(zip(hbm_refs, local_refs))
@@ -237,6 +238,7 @@
     weights_ref[...] = weights
     for fetch in fetches:
         fetch.wait()
+    local_refs += held_refs[fetched:]
     log_ref, piece_refs = local_refs[0], local_refs[1:]
     vox_dev = mixed_ref.shape[1]
     tile = min(vox_dev, SUBLANES * LANES)
@@ -247,6 +249,7 @@
         for share in shares:
             anomalies.append(functools.reduce(jnp.add, [ref[:, cols] for ref in piece_refs[at : at + share]]))
             at += share
+        anomalies[2], anomalies[3] = anomalies[3], anomalies[2]
         mixed_ref[:, cols] = own + mix(weights, anomalies) * (1.0 / scale_root)
 
 
@@ -273,16 +276,16 @@
         functools.partial(
             weigh_kernel, members, j_dev, count, scale_root, [len(share) for share in pieces], len(parts)
         ),
-        in_specs=[IN_VMEM] * len(parts) + [pl.BlockSpec(memory_space=pl.ANY)] * (1 + len(flat)),
+        in_specs=[IN_VMEM] * len(parts) + [pl.BlockSpec(memory_space=pl.ANY)] * len(flat) + [IN_VMEM],
         out_specs=[IN_VMEM] * 2,
         out_shape=[
             pltpu.VMEM((j_dev, members // j_dev * PIECE_ROWS), jnp.bfloat16),
             pltpu.VMEM((j_dev, vox_dev), jnp.float32),
         ],
         scratch_shapes=[pltpu.VMEM((j_dev, vox_dev), jnp.float32)]
-        + [pltpu.VMEM((j_dev, vox_dev), jnp.bfloat16)] * len(flat)
-        + [pltpu.SemaphoreType.DMA((1 + len(flat),))],
-    )(*map(in_vmem, parts), log_modulus, *flat)
+        + [pltpu.VMEM((j_dev, vox_dev), jnp.bfloat16)] * (len(flat) - 1)
+        + [pltpu.SemaphoreType.DMA((len(flat),))],
+    )(*map(in_vmem, parts), log_modulus, *flat[:-1], in_vmem(flat[-1]))
 
 
 def finish(weights, mixed, last, scale_root):
@@ -341,7 +344,7 @@
     if line:
         ends = [(1, 0), (2, 3)]
         near_far = in_hbm(pairs_exchange(near, "grp", [(1, 2), (2, 1)]))
-        middle_far = in_hbm(pairs_exchange(middle, "grp", ends))
+        middle_far = pairs_exchange(middle, "grp", ends)
     width = round_up(members + j_dev, LANES)
     (partial_sums,) = vmem_call(
         functools.partial(pair_kernel, n_grp, j_dev, scale_root),
@@ -358,7 +361,7 @@
     if line:
         far = pairs_exchange(near_far, "grp", ends)
         weights, mixed = weigh(
-            parts, log_modulus, [[near], [near_far, middle_far], [middle]], members, count, scale_root
+            parts, log_modulus, [[near], [middle], [near_far, middle_far]], members, count, scale_root
         )
         return finish(weights, mixed, far, scale_root)
     weights = solve_plain(parts, members, j_dev, count)

time: 58.8 us -> 58.6 us (level)
  no operation moved by 1% of the time
where the time goes in v3:
time: 58.6 us; the launch traced here: 58.4 us
  waiting for transfers between devices  26.1 us (45%)
  starting transfers between devices  22.6 us (39%)
  Pallas kernels  7.49 us (13%)
  other arithmetic  1.57 us (3%)
    ppermute x12, waiting for transfers between devices, exchange(): return lax.ppermute(value, axis, [(i, i ^ distance) for i in range(count)])  26.1 us
    ppermute x12, starting transfers between devices, exchange(): return lax.ppermute(value, axis, [(i, i ^ distance) for i in range(count)])  17.9 us
    pallas_call x1, Pallas kernels, weigh(): pl.pallas_call(functools.partial(weigh_kernel, members, j_dev, count, sca...  5.06 us
    ppermute x4, starting transfers between devices, pairs_exchange(): return lax.ppermute(value, axis, pairs)  4.65 us
    convert_element_type x1, other arithmetic, on_device(): low = log_modulus.astype(jnp.bfloat16)  1.55 us
    pallas_call x2, Pallas kernels, vmem_call(): pl.pallas_call(kernel, in_specs=[IN_VMEM] * len(operands), out_specs=[IN_...  1.27 us
  transfers between devices with their start and end apart: 16, of which 10 were waited for; matrix products, arithmetic and copies ran while one was open for 1% of the time, Pallas kernels for 11%

profile of v3, /device:TPU:0, one launch (start us, length us, event | category | flops | bytes accessed | tf_op | source)
XLA Modules:
  0.0 58.4 jit_solution(7344595046848044566)
XLA Ops:
  0.0 1.5 %fusion = (bf16[24,8192]{1,0:T(8,128)(2,1)S(1)}, bf16[24,8192]{1,0:T(8,128)(2,1)S(1)}) fusion(f32[24,8192]{1,0:T(8,128)} %refs_4_.3), kind=kLoop, calls=%fused_computation.3 | loop fusion | flops 589824 | bytes 1572864 | tf_op jit(solution)/shard_map/convert_element_type | solution.py:319
  1.6 3.1 %collective-permute-start.11 = (bf16[24,8192]{1,0:T(8,128)(2,1)S(1)}, bf16[24,8192]{1,0:T(8,128)(2,1)S(1)}, u32[]{:S(2)}, u32[]{:S(2)}) collective-permute-start(bf16[24,8192]{1,0:T(8,128)(2,1)S(1)} %get-tuple-element.13), channel_id=1, source_target_pairs={{0,8},{8,0},{16,24},{24,16},{1,9},{9,1},{17,25},{25,17},{2,10},{10... | collective-permute-start | bytes 1179656 | tf_op jit(solution)/shard_map/ppermute | solution.py:43
  4.7 0.7 %collective-permute-start.12 = (bf16[24,8192]{1,0:T(8,128)(2,1)S(1)}, bf16[24,8192]{1,0:T(8,128)(2,1)S(1)}, u32[]{:S(2)}, u32[]{:S(2)}) collective-permute-start(bf16[24,8192]{1,0:T(8,128)(2,1)S(1)} %get-tuple-element.13), channel_id=1, source_target_pairs={{8,16},{16,8},{9,17},{17,9},{10,18},{18,10},{11,19},{19,11},{12,20... | collective-permute-start | bytes 1179656 | tf_op jit(solution)/shard_map/ppermute | solution.py:306
  5.4 8.4 %collective-permute-done.11.refs_5_ = bf16[24,8192]{1,0:T(8,128)(2,1)S(1)} collective-permute-done((bf16[24,8192]{1,0:T(8,128)(2,1)S(1)}, bf16[24,8192]{1,0:T(8,128)(2,1)S(1)}, u32[]{:S(2)}, u32[]{:S(2)}) %collective-permute-start.11) | collective-permute-done | bytes 393248 | tf_op jit(solution)/shard_map/ppermute | solution.py:43
  13.8 1.4 %collective-permute-start.13 = (bf16[24,8192]{1,0:T(8,128)(2,1)S(1)}, bf16[24,8192]{1,0:T(8,128)(2,1)}, u32[]{:S(2)}, u32[]{:S(2)}) collective-permute-start(bf16[24,8192]{1,0:T(8,128)(2,1)S(1)} %collective-permute-done.11.refs_5_), channel_id=1, source_target_pairs={{8,16},{16,8},{9,17},{17,9},{10,18},{18,10},{11,19},{19,11},{12,20... | collective-permute-start | bytes 1179656 | tf_op jit(solution)/shard_map/ppermute | solution.py:306
  15.7 2.7 %collective-permute-start.2 = (bf16[192,128]{1,0:T(8,128)(2,1)S(1)}, bf16[192,128]{1,0:T(8,128)(2,1)S(1)}, u32[]{:S(2)}, u32[]{:S(2)}) collective-permute-start(bf16[192,128]{1,0:T(8,128)(2,1)S(1)} %convolution_convert_fusion), channel_id=1, source_target_pairs={{0,6},{1,7},{2,4},{3,5},{4,2},{5,3},{6,0},{7,1},{8,14},{9,15},{10,... | collective-permute-start | bytes 147464 | tf_op jit(solution)/shard_map/ppermute | solution.py:43
  18.4 0.5 collective-permute-start.1
  19.2 1.3 %collective-permute-start.14 = (bf16[24,8192]{1,0:T(8,128)(2,1)S(1)}, bf16[24,8192]{1,0:T(8,128)(2,1)S(1)}, u32[]{:S(2)}, u32[]{:S(2)}) collective-permute-start(bf16[24,8192]{1,0:T(8,128)(2,1)S(1)} %collective-permute-done.12.refs_6_), channel_id=1, source_target_pairs={{8,0},{16,24},{9,1},{17,25},{10,2},{18,26},{11,3},{19,27},{12,4},{... | collective-permute-start | bytes 1179656 | tf_op jit(solution)/shard_map/ppermute | solution.py:306
  20.5 1.3 %collective-permute-start.15 = (bf16[24,8192]{1,0:T(8,128)(2,1)}, bf16[24,8192]{1,0:T(8,128)(2,1)S(1)}, u32[]{:S(2)}, u32[]{:S(2)}) collective-permute-start(bf16[24,8192]{1,0:T(8,128)(2,1)} %collective-permute-done.13.refs_7_), channel_id=1, source_target_pairs={{8,0},{16,24},{9,1},{17,25},{10,2},{18,26},{11,3},{19,27},{12,4},{... | collective-permute-start | bytes 1179656 | tf_op jit(solution)/shard_map/ppermute | solution.py:306
  21.9 0.6 %collective-permute-done.1 = bf16[192,128]{1,0:T(8,128)(2,1)S(1)} collective-permute-done((bf16[192,128]{1,0:T(8,128)(2,1)S(1)}, bf16[192,128]{1,0:T(8,128)(2,1)S(1)}, u32[]{:S(2)}, u32[]{:S(2)}) %collective-permute-start.1) | collective-permute-done | bytes 49184 | tf_op jit(solution)/shard_map/ppermute | solution.py:43
  22.5 0.5 collective-permute-done
  23.1 1.4 %collective-permute-done.3.refs_1_ = bf16[768,128]{1,0:T(8,128)(2,1)S(1)} collective-permute-done((bf16[768,128]{1,0:T(8,128)(2,1)S(1)}, bf16[768,128]{1,0:T(8,128)(2,1)S(1)}, u32[]{:S(2)}, u32[]{:S(2)}) %collective-permute-start.3) | collective-permute-done | bytes 196640 | tf_op jit(solution)/shard_map/ppermute | solution.py:43
  24.5 1.0 %shard_map.73 = (bf16[24,1152]{1,0:T(8,128)(2,1)S(1)}, bf16[24,1024]{1,0:T(8,128)(2,1)S(1)}) custom-call(bf16[768,128]{1,0:T(8,128)(2,1)S(1)} %pad_maximum_fusion.refs_0_, bf16[768,128]{1,0:T(8,128)(2,1)S(1)} %collective-permute-done.3.refs_1_, bf16[1024,128]{1,0:T(8,128)(2,1)S(1)} %copy-done.1, s32[1,1024]{1,0:T(1,128)S(1)} %bitcast.7, ...), custom_call_target="tpu_custom_call" | custom-call | tf_op jit(solution)/shard_map/pallas_call | solution.py:29
  25.6 3.7 %collective-permute-start.6 = (bf16[24,1152]{1,0:T(8,128)(2,1)S(1)}, bf16[24,1152]{1,0:T(8,128)(2,1)S(1)}, u32[]{:S(2)}, u32[]{:S(2)}) collective-permute-start(bf16[24,1152]{1,0:T(8,128)(2,1)S(1)} %get-tuple-element.9.refs_0_), channel_id=1, source_target_pairs={{0,24},{8,16},{16,8},{24,0},{1,25},{9,17},{17,9},{25,1},{2,26},{10... | collective-permute-start | bytes 165896 | tf_op jit(solution)/shard_map/ppermute | solution.py:43
  29.2 3.8 %collective-permute-start.5 = (bf16[24,1152]{1,0:T(8,128)(2,1)S(1)}, bf16[24,1152]{1,0:T(8,128)(2,1)S(1)}, u32[]{:S(2)}, u32[]{:S(2)}) collective-permute-start(bf16[24,1152]{1,0:T(8,128)(2,1)S(1)} %get-tuple-element.9.refs_0_), channel_id=1, source_target_pairs={{0,16},{8,24},{16,0},{24,8},{1,17},{9,25},{17,1},{25,9},{2,18},{10... | collective-permute-start | bytes 165896 | tf_op jit(solution)/shard_map/ppermute | solution.py:43
  33.2 3.6 %collective-permute-done.5.refs_2_ = bf16[24,1152]{1,0:T(8,128)(2,1)S(1)} collective-permute-done((bf16[24,1152]{1,0:T(8,128)(2,1)S(1)}, bf16[24,1152]{1,0:T(8,128)(2,1)S(1)}, u32[]{:S(2)}, u32[]{:S(2)}) %collective-permute-start.5) | collective-permute-done | bytes 55328 | tf_op jit(solution)/shard_map/ppermute | solution.py:43
  36.8 6.6 %collective-permute-done.4.refs_1_ = bf16[24,1152]{1,0:T(8,128)(2,1)S(1)} collective-permute-done((bf16[24,1152]{1,0:T(8,128)(2,1)S(1)}, bf16[24,1152]{1,0:T(8,128)(2,1)S(1)}, u32[]{:S(2)}, u32[]{:S(2)}) %collective-permute-start.4) | collective-permute-done | bytes 55328 | tf_op jit(solution)/shard_map/ppermute | solution.py:43
  43.8 1.2 %collective-permute-done.7 = f32[104,128]{1,0:T(8,128)S(1)} collective-permute-done((f32[104,128]{1,0:T(8,128)S(1)}, f32[104,128]{1,0:T(8,128)S(1)}, u32[]{:S(2)}, u32[]{:S(2)}) %collective-permute-start.7) | collective-permute-done | bytes 53280 | tf_op jit(solution)/shard_map/ppermute | solution.py:43
  45.0 2.5 %collective-permute-start.10 = (f32[104,128]{1,0:T(8,128)S(1)}, f32[104,128]{1,0:T(8,128)S(1)}, u32[]{:S(2)}, u32[]{:S(2)}) collective-permute-start(f32[104,128]{1,0:T(8,128)S(1)} %add.3.refs_0_), channel_id=1, source_target_pairs={{0,6},{1,7},{2,4},{3,5},{4,2},{5,3},{6,0},{7,1},{8,14},{9,15},{10,... | collective-permute-start | bytes 159752 | tf_op jit(solution)/shard_map/ppermute | solution.py:43
  48.0 0.5 collective-permute-start.8
  48.6 1.6 %collective-permute-done.10.refs_3_ = f32[104,128]{1,0:T(8,128)S(1)} collective-permute-done((f32[104,128]{1,0:T(8,128)S(1)}, f32[104,128]{1,0:T(8,128)S(1)}, u32[]{:S(2)}, u32[]{:S(2)}) %collective-permute-start.10) | collective-permute-done | bytes 53280 | tf_op jit(solution)/shard_map/ppermute | solution.py:43
  50.1 1.5 %collective-permute-done.9.refs_2_ = f32[104,128]{1,0:T(8,128)S(1)} collective-permute-done((f32[104,128]{1,0:T(8,128)S(1)}, f32[104,128]{1,0:T(8,128)S(1)}, u32[]{:S(2)}, u32[]{:S(2)}) %collective-permute-start.9) | collective-permute-done | bytes 53280 | tf_op jit(solution)/shard_map/ppermute | solution.py:43
  52.2 5.1 %shard_map.75 = (bf16[24,128]{1,0:T(8,128)(2,1)S(1)}, f32[24,8192]{1,0:T(8,128)S(1)}) custom-call(f32[104,128]{1,0:T(8,128)S(1)} %add.3.refs_0_, f32[104,128]{1,0:T(8,128)S(1)} %collective-permute-done.8.refs_1_, f32[104,128]{1,0:T(8,128)S(1)} %collective-permute-done.9.refs_2_, f32[104,128]{1,0:T(8,128)S(1)} %collective-permute-done.10.refs_3_, ...), custom_call_target="tpu_custom_call" | custom-call | tf_op jit(solution)/shard_map/pallas_call | solution.py:275
  57.2 1.2 %shard_map.76 = f32[24,8192]{1,0:T(8,128)} custom-call(bf16[24,128]{1,0:T(8,128)(2,1)S(1)} %get-tuple-element.11.weights_ref, f32[24,8192]{1,0:T(8,128)S(1)} %get-tuple-element.12.mixed_ref, bf16[24,8192]{1,0:T(8,128)(2,1)S(1)} %collective-permute-done.15.last_ref), custom_call_target="tpu_custom_call" | custom-call | tf_op jit(solution)/shard_map/pallas_call | solution.py:293
  (33 shorter events, 2.4 us)
Async XLA Ops:
  0.0 15.4 %copy-start = (bf16[1024,128]{1,0:T(8,128)(2,1)S(1)}, bf16[1024,128]{1,0:T(8,128)(2,1)}, u32[]{:S(2)}) copy-start(bf16[1024,128]{1,0:T(8,128)(2,1)} %param.8) | copy-start | bytes 786436
  1.6 12.2 %collective-permute-start.11 = (bf16[24,8192]{1,0:T(8,128)(2,1)S(1)}, bf16[24,8192]{1,0:T(8,128)(2,1)S(1)}, u32[]{:S(2)}, u32[]{:S(2)}) collective-permute-start(bf16[24,8192]{1,0:T(8,128)(2,1)S(1)} %get-tuple-element.13), channel_id=1, source_target_pairs={{0,8},{8,0},{16,24},{24,16},{1,9},{9,1},{17,25},{25,17},{2,10},{10... | collective-permute-start | bytes 1179656 | tf_op jit(solution)/shard_map/ppermute | solution.py:43
  4.7 14.6 %collective-permute-start.12 = (bf16[24,8192]{1,0:T(8,128)(2,1)S(1)}, bf16[24,8192]{1,0:T(8,128)(2,1)S(1)}, u32[]{:S(2)}, u32[]{:S(2)}) collective-permute-start(bf16[24,8192]{1,0:T(8,128)(2,1)S(1)} %get-tuple-element.13), channel_id=1, source_target_pairs={{8,16},{16,8},{9,17},{17,9},{10,18},{18,10},{11,19},{19,11},{12,20... | collective-permute-start | bytes 1179656 | tf_op jit(solution)/shard_map/ppermute | solution.py:306
  13.8 1.6 %copy-start.6 = (bf16[24,8192]{1,0:T(8,128)(2,1)}, bf16[24,8192]{1,0:T(8,128)(2,1)S(1)}, u32[]{:S(2)}) copy-start(bf16[24,8192]{1,0:T(8,128)(2,1)S(1)} %collective-permute-done.11.refs_5_) | copy-start | bytes 1179652
  13.8 6.8 %collective-permute-start.13 = (bf16[24,8192]{1,0:T(8,128)(2,1)S(1)}, bf16[24,8192]{1,0:T(8,128)(2,1)}, u32[]{:S(2)}, u32[]{:S(2)}) collective-permute-start(bf16[24,8192]{1,0:T(8,128)(2,1)S(1)} %collective-permute-done.11.refs_5_), channel_id=1, source_target_pairs={{8,16},{16,8},{9,17},{17,9},{10,18},{18,10},{11,19},{19,11},{12,20... | collective-permute-start | bytes 1179656 | tf_op jit(solution)/shard_map/ppermute | solution.py:306
  15.7 8.8 %copy-start.1 = (bf16[1024,128]{1,0:T(8,128)(2,1)S(1)}, bf16[1024,128]{1,0:T(8,128)(2,1)}, u32[]{:S(2)}) copy-start(bf16[1024,128]{1,0:T(8,128)(2,1)} %refs_2_.1) | copy-start | bytes 786436
  15.7 8.8 %copy-start.2 = (f32[24,1024]{1,0:T(8,128)S(1)}, f32[24,1024]{1,0:T(8,128)}, u32[]{:S(2)}) copy-start(f32[24,1024]{1,0:T(8,128)} %refs_4_.2) | copy-start | bytes 294916
  15.7 6.2 %collective-permute-start.2 = (bf16[192,128]{1,0:T(8,128)(2,1)S(1)}, bf16[192,128]{1,0:T(8,128)(2,1)S(1)}, u32[]{:S(2)}, u32[]{:S(2)}) collective-permute-start(bf16[192,128]{1,0:T(8,128)(2,1)S(1)} %convolution_convert_fusion), channel_id=1, source_target_pairs={{0,6},{1,7},{2,4},{3,5},{4,2},{5,3},{6,0},{7,1},{8,14},{9,15},{10,... | collective-permute-start | bytes 147464 | tf_op jit(solution)/shard_map/ppermute | solution.py:43
  18.4 4.1 %collective-permute-start.1 = (bf16[192,128]{1,0:T(8,128)(2,1)S(1)}, bf16[192,128]{1,0:T(8,128)(2,1)S(1)}, u32[]{:S(2)}, u32[]{:S(2)}) collective-permute-start(bf16[192,128]{1,0:T(8,128)(2,1)S(1)} %convolution_convert_fusion), channel_id=1, source_target_pairs={{0,4},{1,5},{2,6},{3,7},{4,0},{5,1},{6,2},{7,3},{8,12},{9,13},{10,... | collective-permute-start | bytes 147464 | tf_op jit(solution)/shard_map/ppermute | solution.py:43
  18.9 4.1 %collective-permute-start = (bf16[192,128]{1,0:T(8,128)(2,1)S(1)}, bf16[192,128]{1,0:T(8,128)(2,1)S(1)}, u32[]{:S(2)}, u32[]{:S(2)}) collective-permute-start(bf16[192,128]{1,0:T(8,128)(2,1)S(1)} %convolution_convert_fusion), channel_id=1, source_target_pairs={{0,2},{1,3},{2,0},{3,1},{4,6},{5,7},{6,4},{7,5},{8,10},{9,11},{10,... | collective-permute-start | bytes 147464 | tf_op jit(solution)/shard_map/ppermute | solution.py:43
  19.2 6.3 %copy-start.7 = (bf16[24,8192]{1,0:T(8,128)(2,1)}, bf16[24,8192]{1,0:T(8,128)(2,1)S(1)}, u32[]{:S(2)}) copy-start(bf16[24,8192]{1,0:T(8,128)(2,1)S(1)} %collective-permute-done.12.refs_6_) | copy-start | bytes 1179652
  19.2 32.9 %collective-permute-start.14 = (bf16[24,8192]{1,0:T(8,128)(2,1)S(1)}, bf16[24,8192]{1,0:T(8,128)(2,1)S(1)}, u32[]{:S(2)}, u32[]{:S(2)}) collective-permute-start(bf16[24,8192]{1,0:T(8,128)(2,1)S(1)} %collective-permute-done.12.refs_6_), channel_id=1, source_target_pairs={{8,0},{16,24},{9,1},{17,25},{10,2},{18,26},{11,3},{19,27},{12,4},{... | collective-permute-start | bytes 1179656 | tf_op jit(solution)/shard_map/ppermute | solution.py:306
  20.5 36.7 %collective-permute-start.15 = (bf16[24,8192]{1,0:T(8,128)(2,1)}, bf16[24,8192]{1,0:T(8,128)(2,1)S(1)}, u32[]{:S(2)}, u32[]{:S(2)}) collective-permute-start(bf16[24,8192]{1,0:T(8,128)(2,1)} %collective-permute-done.13.refs_7_), channel_id=1, source_target_pairs={{8,0},{16,24},{9,1},{17,25},{10,2},{18,26},{11,3},{19,27},{12,4},{... | collective-permute-start | bytes 1179656 | tf_op jit(solution)/shard_map/ppermute | solution.py:306
  23.0 1.5 %copy-start.4 = (s32[1024,1]{0,1:T(1,128)S(1)}, s32[1024,1]{0,1:T(1,128)}, u32[]{:S(2)}) copy-start(s32[1024,1]{0,1:T(1,128)} %param.10) | copy-start | bytes 12292
  23.0 1.6 %copy-start.5 = (f32[1024]{0:T(1024)S(1)}, f32[1024]{0:T(1024)}, u32[]{:S(2)}) copy-start(f32[1024]{0:T(1024)} %param.11) | copy-start | bytes 12292
  23.0 1.5 %copy-start.3 = (f32[1024]{0:T(1024)S(1)}, f32[1024]{0:T(1024)}, u32[]{:S(2)}) copy-start(f32[1024]{0:T(1024)} %param.12) | copy-start | bytes 12292
  23.0 1.5 %collective-permute-start.3 = (bf16[768,128]{1,0:T(8,128)(2,1)S(1)}, bf16[768,128]{1,0:T(8,128)(2,1)S(1)}, u32[]{:S(2)}, u32[]{:S(2)}) collective-permute-start(bf16[768,128]{1,0:T(8,128)(2,1)S(1)} %pad_maximum_fusion.refs_0_), channel_id=1, source_target_pairs={{0,1},{1,0},{2,3},{3,2},{4,5},{5,4},{6,7},{7,6},{8,9},{9,8},{10,11... | collective-permute-start | bytes 589832 | tf_op jit(solution)/shard_map/ppermute | solution.py:43
  25.6 7.6 %collective-permute-start.6 = (bf16[24,1152]{1,0:T(8,128)(2,1)S(1)}, bf16[24,1152]{1,0:T(8,128)(2,1)S(1)}, u32[]{:S(2)}, u32[]{:S(2)}) collective-permute-start(bf16[24,1152]{1,0:T(8,128)(2,1)S(1)} %get-tuple-element.9.refs_0_), channel_id=1, source_target_pairs={{0,24},{8,16},{16,8},{24,0},{1,25},{9,17},{17,9},{25,1},{2,26},{10... | collective-permute-start | bytes 165896 | tf_op jit(solution)/shard_map/ppermute | solution.py:43
  29.2 7.6 %collective-permute-start.5 = (bf16[24,1152]{1,0:T(8,128)(2,1)S(1)}, bf16[24,1152]{1,0:T(8,128)(2,1)S(1)}, u32[]{:S(2)}, u32[]{:S(2)}) collective-permute-start(bf16[24,1152]{1,0:T(8,128)(2,1)S(1)} %get-tuple-element.9.refs_0_), channel_id=1, source_target_pairs={{0,16},{8,24},{16,0},{24,8},{1,17},{9,25},{17,1},{25,9},{2,18},{10... | collective-permute-start | bytes 165896 | tf_op jit(solution)/shard_map/ppermute | solution.py:43
  33.0 10.4 %collective-permute-start.4 = (bf16[24,1152]{1,0:T(8,128)(2,1)S(1)}, bf16[24,1152]{1,0:T(8,128)(2,1)S(1)}, u32[]{:S(2)}, u32[]{:S(2)}) collective-permute-start(bf16[24,1152]{1,0:T(8,128)(2,1)S(1)} %get-tuple-element.9.refs_0_), channel_id=1, source_target_pairs={{0,8},{8,0},{16,24},{24,16},{1,9},{9,1},{17,25},{25,17},{2,10},{10... | collective-permute-start | bytes 165896 | tf_op jit(solution)/shard_map/ppermute | solution.py:43
  43.7 1.3 %collective-permute-start.7 = (f32[104,128]{1,0:T(8,128)S(1)}, f32[104,128]{1,0:T(8,128)S(1)}, u32[]{:S(2)}, u32[]{:S(2)}) collective-permute-start(f32[104,128]{1,0:T(8,128)S(1)} %shard_map.74), channel_id=1, source_target_pairs={{0,1},{1,0},{2,3},{3,2},{4,5},{5,4},{6,7},{7,6},{8,9},{9,8},{10,11... | collective-permute-start | bytes 159752 | tf_op jit(solution)/shard_map/ppermute | solution.py:43
  45.0 5.1 %collective-permute-start.10 = (f32[104,128]{1,0:T(8,128)S(1)}, f32[104,128]{1,0:T(8,128)S(1)}, u32[]{:S(2)}, u32[]{:S(2)}) collective-permute-start(f32[104,128]{1,0:T(8,128)S(1)} %add.3.refs_0_), channel_id=1, source_target_pairs={{0,6},{1,7},{2,4},{3,5},{4,2},{5,3},{6,0},{7,1},{8,14},{9,15},{10,... | collective-permute-start | bytes 159752 | tf_op jit(solution)/shard_map/ppermute | solution.py:43
  47.5 4.1 %collective-permute-start.9 = (f32[104,128]{1,0:T(8,128)S(1)}, f32[104,128]{1,0:T(8,128)S(1)}, u32[]{:S(2)}, u32[]{:S(2)}) collective-permute-start(f32[104,128]{1,0:T(8,128)S(1)} %add.3.refs_0_), channel_id=1, source_target_pairs={{0,4},{1,5},{2,6},{3,7},{4,0},{5,1},{6,2},{7,3},{8,12},{9,13},{10,... | collective-permute-start | bytes 159752 | tf_op jit(solution)/shard_map/ppermute | solution.py:43
  48.0 4.1 %collective-permute-start.8 = (f32[104,128]{1,0:T(8,128)S(1)}, f32[104,128]{1,0:T(8,128)S(1)}, u32[]{:S(2)}, u32[]{:S(2)}) collective-permute-start(f32[104,128]{1,0:T(8,128)S(1)} %add.3.refs_0_), channel_id=1, source_target_pairs={{0,2},{1,3},{2,0},{3,1},{4,6},{5,7},{6,4},{7,5},{8,10},{9,11},{10,... | collective-permute-start | bytes 159752 | tf_op jit(solution)/shard_map/ppermute | solution.py:43

commit v4 on v3

--- a/solution.py
+++ b/solution.py
@@ -10,6 +10,7 @@
 
 
 LANES = 128
+BATCHES = 1
 SUBLANES = 8
 
 
@@ -66,6 +67,55 @@
 def two_parts(value):
     high = value.astype(jnp.bfloat16).astype(jnp.float32)
     return high, value - high
+
+
+def feature_kernel(block_vox, log_hbm, basis_hbm, low_ref, feature_ref, log_ref, basis_ref, semaphores):
+    j_dev, vox_dev = log_ref.shape
+    blocks = vox_dev // block_vox
+    fetches = []
+    for block in range(blocks):
+        cols = pl.ds(block * block_vox, block_vox)
+        fetches.append(pltpu.make_async_copy(log_hbm.at[:, cols], log_ref.at[:, cols], semaphores.at[block]))
+        fetches[-1].start()
+    fetch_basis = pltpu.make_async_copy(basis_hbm, basis_ref, semaphores.at[blocks])
+    fetch_basis.start()
+    batch = max(1, blocks // BATCHES)
+    for start in range(0, blocks, batch):
+        compliance = []
+        for block in range(start, min(blocks, start + batch)):
+            fetches[block].wait()
+            cols = pl.ds(block * block_vox, block_vox)
+            value = log_ref[:, cols]
+            low_ref[:, cols] = value.astype(jnp.bfloat16)
+            compliance.append(jnp.exp(-value))
+        if start == 0:
+            fetch_basis.wait()
+        rows = len(compliance) * j_dev
+        feature_ref[pl.ds(start * j_dev, rows), :] = jnp.dot(
+            jnp.concatenate(compliance, axis=0).astype(jnp.bfloat16),
+            basis_ref[...],
+            preferred_element_type=jnp.float32,
+        ).astype(jnp.bfloat16)
+
+
+def make_features(log_modulus, basis):
+    j_dev, vox_dev = log_modulus.shape
+    block_vox, feature_width = basis.shape
+    blocks = vox_dev // block_vox
+    return pl.pallas_call(
+        functools.partial(feature_kernel, block_vox),
+        in_specs=[pl.BlockSpec(memory_space=pl.ANY)] * 2,
+        out_specs=[IN_VMEM] * 2,
+        out_shape=[
+            pltpu.VMEM((j_dev, vox_dev), jnp.bfloat16),
+            pltpu.VMEM((blocks * j_dev, feature_width), jnp.bfloat16),
+        ],
+        scratch_shapes=[
+            pltpu.VMEM((j_dev, vox_dev), jnp.float32),
+            pltpu.VMEM(basis.shape, basis.dtype),
+            pltpu.SemaphoreType.DMA((blocks + 1,)),
+        ],
+    )(log_modulus, basis)
 
 
 def predict_kernel(offsets, j_dev, blocks_dev, *refs):
@@ -78,17 +128,19 @@
     for start in range(0, obs_dev, tile):
         cols = pl.ds(start, tile)
         sens = sens_ref[cols, :]
-        local = block_ref[:, cols] - lax.broadcasted_iota(jnp.int32, (blocks_dev, tile), 0)
-        total = jnp.zeros((j_dev, blocks_dev, tile), jnp.float32)
+        block = block_ref[:, cols]
+        total = jnp.zeros((j_dev, tile), jnp.float32)
         for stack_ref, held in zip(stack_refs, offsets):
             for place, offset in enumerate(held):
                 piece = stack_ref[pl.ds(place * rows, rows), :]
                 product = lax.dot_general(
                     piece, sens, (((1,), (1,)), ((), ())), preferred_element_type=jnp.float32
-                ).reshape(j_dev, blocks_dev, tile)
+                )
                 first_block = (lax.axis_index("vox") ^ offset) * blocks_dev
-                total = total + jnp.where((local == first_block)[None], product, 0.0)
-        predicted = jnp.sum(total, axis=1)
+                for local in range(blocks_dev):
+                    wanted = jnp.broadcast_to(block == first_block + local, total.shape)
+                    total = jnp.where(wanted, product[local * j_dev : (local + 1) * j_dev], total)
+        predicted = total
         misfit = ((obs_ref[:, cols] - predicted) / noise_ref[:, cols] + pert_ref[:, cols]).astype(jnp.bfloat16)
         misfit_ref[:, cols] = misfit
         mean = jnp.sum(predicted, axis=0, keepdims=True) * (1.0 / j_dev)
@@ -316,12 +368,7 @@
     members = j_dev * n_grp
     scale_root = math.sqrt(members - 1)
 
-    low = log_modulus.astype(jnp.bfloat16)
-    compliance = jnp.exp(-log_modulus).astype(jnp.bfloat16)
-    features = jnp.dot(
-        compliance.reshape(j_dev * blocks_dev, block_vox), basis, preferred_element_type=jnp.float32
-    ).astype(jnp.bfloat16)
-
+    low, features = make_features(log_modulus, basis)
     block = obs_block.reshape(1, obs_dev)
     observed = observed.reshape(1, obs_dev)
     noise = noise_scale.reshape(1, obs_dev)

time: 58.6 us -> 60.6 us (1.034)
  waiting for transfers between devices: 26.1 us -> 30.5 us
  starting transfers between devices: 22.6 us -> 20.4 us
  Pallas kernels: 7.49 us -> 9.12 us
  other arithmetic: 1.57 us -> 0.01 us
    ppermute x12, waiting for transfers between devices: 26.1 us -> 30.5 us  [exchange(): return lax.ppermute(value, axis, [(i, i ^ distance) for i in range(count)])]
    ppermute x12, starting transfers between devices: 17.9 us -> 15.8 us  [exchange(): return lax.ppermute(value, axis, [(i, i ^ distance) for i in range(count)])]
    pallas_call x0 -> x1, Pallas kernels: none -> 1.63 us  [make_features(): pl.pallas_call(functools.partial(feature_kernel, block_vox), in_specs=[pl...]
    convert_element_type x1 -> x0, other arithmetic: 1.55 us -> none  [on_device(): low = log_modulus.astype(jnp.bfloat16)]
  transfers between devices with their start and end apart: 16 -> 16, of which waited for: 10 -> 10; matrix products, arithmetic and copies ran while one was open for 1% -> 0% of each run, Pallas kernels for 11% -> 10%
where the time goes in v4:
time: 60.6 us; the launch traced here: 60.4 us
  waiting for transfers between devices  30.5 us (50%)
  starting transfers between devices  20.4 us (34%)
  Pallas kernels  9.12 us (15%)
    ppermute x12, waiting for transfers between devices, exchange(): return lax.ppermute(value, axis, [(i, i ^ distance) for i in range(count)])  30.5 us
    ppermute x12, starting transfers between devices, exchange(): return lax.ppermute(value, axis, [(i, i ^ distance) for i in range(count)])  15.8 us
    pallas_call x1, Pallas kernels, weigh(): pl.pallas_call(functools.partial(weigh_kernel, members, j_dev, count, sca...  5.06 us
    ppermute x4, starting transfers between devices, pairs_exchange(): return lax.ppermute(value, axis, pairs)  4.65 us
    pallas_call x1, Pallas kernels, make_features(): pl.pallas_call(functools.partial(feature_kernel, block_vox), in_specs=[pl...  1.63 us
    pallas_call x2, Pallas kernels, vmem_call(): pl.pallas_call(kernel, in_specs=[IN_VMEM] * len(operands), out_specs=[IN_...  1.27 us
  transfers between devices with their start and end apart: 16, of which 10 were waited for; matrix products, arithmetic and copies ran while one was open for 0% of the time, Pallas kernels for 10%

profile of v4, /device:TPU:0, one launch (start us, length us, event | category | flops | bytes accessed | tf_op | source)
XLA Modules:
  0.0 60.4 jit_solution(14655000450238343623)
XLA Ops:
  0.0 1.6 %shard_map.73 = (bf16[24,8192]{1,0:T(8,128)(2,1)S(1)}, bf16[192,128]{1,0:T(8,128)(2,1)S(1)}) custom-call(f32[24,8192]{1,0:T(8,128)} %refs_4_.3, bf16[1024,128]{1,0:T(8,128)(2,1)} %basis_hbm.1), custom_call_target="tpu_custom_call" | custom-call | tf_op jit(solution)/shard_map/pallas_call | solution.py:105
  1.7 3.1 %collective-permute-start.11 = (bf16[24,8192]{1,0:T(8,128)(2,1)S(1)}, bf16[24,8192]{1,0:T(8,128)(2,1)S(1)}, u32[]{:S(2)}, u32[]{:S(2)}) collective-permute-start(bf16[24,8192]{1,0:T(8,128)(2,1)S(1)} %get-tuple-element.14), channel_id=1, source_target_pairs={{0,8},{8,0},{16,24},{24,16},{1,9},{9,1},{17,25},{25,17},{2,10},{10... | collective-permute-start | bytes 1179656 | tf_op jit(solution)/shard_map/ppermute | solution.py:44
  4.8 0.7 %collective-permute-start.12 = (bf16[24,8192]{1,0:T(8,128)(2,1)S(1)}, bf16[24,8192]{1,0:T(8,128)(2,1)S(1)}, u32[]{:S(2)}, u32[]{:S(2)}) collective-permute-start(bf16[24,8192]{1,0:T(8,128)(2,1)S(1)} %get-tuple-element.14), channel_id=1, source_target_pairs={{8,16},{16,8},{9,17},{17,9},{10,18},{18,10},{11,19},{19,11},{12,20... | collective-permute-start | bytes 1179656 | tf_op jit(solution)/shard_map/ppermute | solution.py:358
  5.5 8.4 %collective-permute-done.11.refs_5_ = bf16[24,8192]{1,0:T(8,128)(2,1)S(1)} collective-permute-done((bf16[24,8192]{1,0:T(8,128)(2,1)S(1)}, bf16[24,8192]{1,0:T(8,128)(2,1)S(1)}, u32[]{:S(2)}, u32[]{:S(2)}) %collective-permute-start.11) | collective-permute-done | bytes 393248 | tf_op jit(solution)/shard_map/ppermute | solution.py:44
  13.9 1.4 %collective-permute-start.13 = (bf16[24,8192]{1,0:T(8,128)(2,1)S(1)}, bf16[24,8192]{1,0:T(8,128)(2,1)}, u32[]{:S(2)}, u32[]{:S(2)}) collective-permute-start(bf16[24,8192]{1,0:T(8,128)(2,1)S(1)} %collective-permute-done.11.refs_5_), channel_id=1, source_target_pairs={{8,16},{16,8},{9,17},{17,9},{10,18},{18,10},{11,19},{19,11},{12,20... | collective-permute-start | bytes 1179656 | tf_op jit(solution)/shard_map/ppermute | solution.py:358
  15.3 2.6 %collective-permute-start.2 = (bf16[192,128]{1,0:T(8,128)(2,1)S(1)}, bf16[192,128]{1,0:T(8,128)(2,1)S(1)}, u32[]{:S(2)}, u32[]{:S(2)}) collective-permute-start(bf16[192,128]{1,0:T(8,128)(2,1)S(1)} %get-tuple-element.11), channel_id=1, source_target_pairs={{0,6},{1,7},{2,4},{3,5},{4,2},{5,3},{6,0},{7,1},{8,14},{9,15},{10,... | collective-permute-start | bytes 147464 | tf_op jit(solution)/shard_map/ppermute | solution.py:44
  18.8 3.7 %collective-permute-done = bf16[192,128]{1,0:T(8,128)(2,1)S(1)} collective-permute-done((bf16[192,128]{1,0:T(8,128)(2,1)S(1)}, bf16[192,128]{1,0:T(8,128)(2,1)S(1)}, u32[]{:S(2)}, u32[]{:S(2)}) %collective-permute-start) | collective-permute-done | bytes 49184 | tf_op jit(solution)/shard_map/ppermute | solution.py:44
  22.6 1.3 %collective-permute-start.14 = (bf16[24,8192]{1,0:T(8,128)(2,1)S(1)}, bf16[24,8192]{1,0:T(8,128)(2,1)S(1)}, u32[]{:S(2)}, u32[]{:S(2)}) collective-permute-start(bf16[24,8192]{1,0:T(8,128)(2,1)S(1)} %collective-permute-done.12.refs_6_), channel_id=1, source_target_pairs={{8,0},{16,24},{9,1},{17,25},{10,2},{18,26},{11,3},{19,27},{12,4},{... | collective-permute-start | bytes 1179656 | tf_op jit(solution)/shard_map/ppermute | solution.py:358
  23.9 1.3 %collective-permute-start.15 = (bf16[24,8192]{1,0:T(8,128)(2,1)}, bf16[24,8192]{1,0:T(8,128)(2,1)S(1)}, u32[]{:S(2)}, u32[]{:S(2)}) collective-permute-start(bf16[24,8192]{1,0:T(8,128)(2,1)} %collective-permute-done.13.refs_7_), channel_id=1, source_target_pairs={{8,0},{16,24},{9,1},{17,25},{10,2},{18,26},{11,3},{19,27},{12,4},{... | collective-permute-start | bytes 1179656 | tf_op jit(solution)/shard_map/ppermute | solution.py:358
  25.3 1.4 %collective-permute-done.3.refs_1_ = bf16[768,128]{1,0:T(8,128)(2,1)S(1)} collective-permute-done((bf16[768,128]{1,0:T(8,128)(2,1)S(1)}, bf16[768,128]{1,0:T(8,128)(2,1)S(1)}, u32[]{:S(2)}, u32[]{:S(2)}) %collective-permute-start.3) | collective-permute-done | bytes 196640 | tf_op jit(solution)/shard_map/ppermute | solution.py:44
  26.8 1.0 %shard_map.74 = (bf16[24,1152]{1,0:T(8,128)(2,1)S(1)}, bf16[24,1024]{1,0:T(8,128)(2,1)S(1)}) custom-call(bf16[768,128]{1,0:T(8,128)(2,1)S(1)} %constant_dynamic-update-slice_fusion.refs_0_, bf16[768,128]{1,0:T(8,128)(2,1)S(1)} %collective-permute-done.3.refs_1_, bf16[1024,128]{1,0:T(8,128)(2,1)S(1)} %copy-done, s32[1,1024]{1,0:T(1,128)S(1)} %bitcast.5, ...), custom_call_target="tpu_custom_call" | custom-call | tf_op jit(solution)/shard_map/pallas_call | solution.py:30
  27.8 3.7 %collective-permute-start.6 = (bf16[24,1152]{1,0:T(8,128)(2,1)S(1)}, bf16[24,1152]{1,0:T(8,128)(2,1)S(1)}, u32[]{:S(2)}, u32[]{:S(2)}) collective-permute-start(bf16[24,1152]{1,0:T(8,128)(2,1)S(1)} %get-tuple-element.12.refs_0_), channel_id=1, source_target_pairs={{0,24},{8,16},{16,8},{24,0},{1,25},{9,17},{17,9},{25,1},{2,26},{10... | collective-permute-start | bytes 165896 | tf_op jit(solution)/shard_map/ppermute | solution.py:44
  31.5 1.6 %collective-permute-start.5 = (bf16[24,1152]{1,0:T(8,128)(2,1)S(1)}, bf16[24,1152]{1,0:T(8,128)(2,1)S(1)}, u32[]{:S(2)}, u32[]{:S(2)}) collective-permute-start(bf16[24,1152]{1,0:T(8,128)(2,1)S(1)} %get-tuple-element.12.refs_0_), channel_id=1, source_target_pairs={{0,16},{8,24},{16,0},{24,8},{1,17},{9,25},{17,1},{25,9},{2,18},{10... | collective-permute-start | bytes 165896 | tf_op jit(solution)/shard_map/ppermute | solution.py:44
  33.3 0.6 collective-permute-done.6.refs_3_
  33.9 3.4 %collective-permute-done.5.refs_2_ = bf16[24,1152]{1,0:T(8,128)(2,1)S(1)} collective-permute-done((bf16[24,1152]{1,0:T(8,128)(2,1)S(1)}, bf16[24,1152]{1,0:T(8,128)(2,1)S(1)}, u32[]{:S(2)}, u32[]{:S(2)}) %collective-permute-start.5) | collective-permute-done | bytes 55328 | tf_op jit(solution)/shard_map/ppermute | solution.py:44
  37.3 9.0 %collective-permute-done.4.refs_1_ = bf16[24,1152]{1,0:T(8,128)(2,1)S(1)} collective-permute-done((bf16[24,1152]{1,0:T(8,128)(2,1)S(1)}, bf16[24,1152]{1,0:T(8,128)(2,1)S(1)}, u32[]{:S(2)}, u32[]{:S(2)}) %collective-permute-start.4) | collective-permute-done | bytes 55328 | tf_op jit(solution)/shard_map/ppermute | solution.py:44
  46.5 1.2 %collective-permute-done.7 = f32[104,128]{1,0:T(8,128)S(1)} collective-permute-done((f32[104,128]{1,0:T(8,128)S(1)}, f32[104,128]{1,0:T(8,128)S(1)}, u32[]{:S(2)}, u32[]{:S(2)}) %collective-permute-start.7) | collective-permute-done | bytes 53280 | tf_op jit(solution)/shard_map/ppermute | solution.py:44
  47.8 1.5 %collective-permute-start.10 = (f32[104,128]{1,0:T(8,128)S(1)}, f32[104,128]{1,0:T(8,128)S(1)}, u32[]{:S(2)}, u32[]{:S(2)}) collective-permute-start(f32[104,128]{1,0:T(8,128)S(1)} %add.3.refs_0_), channel_id=1, source_target_pairs={{0,6},{1,7},{2,4},{3,5},{4,2},{5,3},{6,0},{7,1},{8,14},{9,15},{10,... | collective-permute-start | bytes 159752 | tf_op jit(solution)/shard_map/ppermute | solution.py:44
  49.3 0.6 collective-permute-start.9
  49.9 1.4 %collective-permute-start.8 = (f32[104,128]{1,0:T(8,128)S(1)}, f32[104,128]{1,0:T(8,128)S(1)}, u32[]{:S(2)}, u32[]{:S(2)}) collective-permute-start(f32[104,128]{1,0:T(8,128)S(1)} %add.3.refs_0_), channel_id=1, source_target_pairs={{0,2},{1,3},{2,0},{3,1},{4,6},{5,7},{6,4},{7,5},{8,10},{9,11},{10,... | collective-permute-start | bytes 159752 | tf_op jit(solution)/shard_map/ppermute | solution.py:44
  51.3 1.5 %collective-permute-done.10.refs_3_ = f32[104,128]{1,0:T(8,128)S(1)} collective-permute-done((f32[104,128]{1,0:T(8,128)S(1)}, f32[104,128]{1,0:T(8,128)S(1)}, u32[]{:S(2)}, u32[]{:S(2)}) %collective-permute-start.10) | collective-permute-done | bytes 53280 | tf_op jit(solution)/shard_map/ppermute | solution.py:44
  52.9 0.9 %collective-permute-done.9.refs_2_ = f32[104,128]{1,0:T(8,128)S(1)} collective-permute-done((f32[104,128]{1,0:T(8,128)S(1)}, f32[104,128]{1,0:T(8,128)S(1)}, u32[]{:S(2)}, u32[]{:S(2)}) %collective-permute-start.9) | collective-permute-done | bytes 53280 | tf_op jit(solution)/shard_map/ppermute | solution.py:44
  54.1 5.1 %shard_map.76 = (bf16[24,128]{1,0:T(8,128)(2,1)S(1)}, f32[24,8192]{1,0:T(8,128)S(1)}) custom-call(f32[104,128]{1,0:T(8,128)S(1)} %add.3.refs_0_, f32[104,128]{1,0:T(8,128)S(1)} %collective-permute-done.8.refs_1_, f32[104,128]{1,0:T(8,128)S(1)} %collective-permute-done.9.refs_2_, f32[104,128]{1,0:T(8,128)S(1)} %collective-permute-done.10.refs_3_, ...), custom_call_target="tpu_custom_call" | custom-call | tf_op jit(solution)/shard_map/pallas_call | solution.py:327
  59.2 1.2 %shard_map.77 = f32[24,8192]{1,0:T(8,128)} custom-call(bf16[24,128]{1,0:T(8,128)(2,1)S(1)} %get-tuple-element.15.weights_ref, f32[24,8192]{1,0:T(8,128)S(1)} %get-tuple-element.16.mixed_ref, bf16[24,8192]{1,0:T(8,128)(2,1)S(1)} %collective-permute-done.15.last_ref), custom_call_target="tpu_custom_call" | custom-call | tf_op jit(solution)/shard_map/pallas_call | solution.py:345
  (32 shorter events, 1.9 us)
Async XLA Ops:
  1.6 25.1 %copy-start = (bf16[1024,128]{1,0:T(8,128)(2,1)S(1)}, bf16[1024,128]{1,0:T(8,128)(2,1)}, u32[]{:S(2)}) copy-start(bf16[1024,128]{1,0:T(8,128)(2,1)} %refs_2_.1) | copy-start | bytes 786436
  1.7 12.2 %collective-permute-start.11 = (bf16[24,8192]{1,0:T(8,128)(2,1)S(1)}, bf16[24,8192]{1,0:T(8,128)(2,1)S(1)}, u32[]{:S(2)}, u32[]{:S(2)}) collective-permute-start(bf16[24,8192]{1,0:T(8,128)(2,1)S(1)} %get-tuple-element.14), channel_id=1, source_target_pairs={{0,8},{8,0},{16,24},{24,16},{1,9},{9,1},{17,25},{25,17},{2,10},{10... | collective-permute-start | bytes 1179656 | tf_op jit(solution)/shard_map/ppermute | solution.py:44
  4.8 17.8 %collective-permute-start.12 = (bf16[24,8192]{1,0:T(8,128)(2,1)S(1)}, bf16[24,8192]{1,0:T(8,128)(2,1)S(1)}, u32[]{:S(2)}, u32[]{:S(2)}) collective-permute-start(bf16[24,8192]{1,0:T(8,128)(2,1)S(1)} %get-tuple-element.14), channel_id=1, source_target_pairs={{8,16},{16,8},{9,17},{17,9},{10,18},{18,10},{11,19},{19,11},{12,20... | collective-permute-start | bytes 1179656 | tf_op jit(solution)/shard_map/ppermute | solution.py:358
  13.9 13.9 %copy-start.5 = (bf16[24,8192]{1,0:T(8,128)(2,1)}, bf16[24,8192]{1,0:T(8,128)(2,1)S(1)}, u32[]{:S(2)}) copy-start(bf16[24,8192]{1,0:T(8,128)(2,1)S(1)} %collective-permute-done.11.refs_5_) | copy-start | bytes 1179652
  13.9 10.0 %collective-permute-start.13 = (bf16[24,8192]{1,0:T(8,128)(2,1)S(1)}, bf16[24,8192]{1,0:T(8,128)(2,1)}, u32[]{:S(2)}, u32[]{:S(2)}) collective-permute-start(bf16[24,8192]{1,0:T(8,128)(2,1)S(1)} %collective-permute-done.11.refs_5_), channel_id=1, source_target_pairs={{8,16},{16,8},{9,17},{17,9},{10,18},{18,10},{11,19},{19,11},{12,20... | collective-permute-start | bytes 1179656 | tf_op jit(solution)/shard_map/ppermute | solution.py:358
  15.3 9.9 %collective-permute-start.2 = (bf16[192,128]{1,0:T(8,128)(2,1)S(1)}, bf16[192,128]{1,0:T(8,128)(2,1)S(1)}, u32[]{:S(2)}, u32[]{:S(2)}) collective-permute-start(bf16[192,128]{1,0:T(8,128)(2,1)S(1)} %get-tuple-element.11), channel_id=1, source_target_pairs={{0,6},{1,7},{2,4},{3,5},{4,2},{5,3},{6,0},{7,1},{8,14},{9,15},{10,... | collective-permute-start | bytes 147464 | tf_op jit(solution)/shard_map/ppermute | solution.py:44
  17.9 4.6 %collective-permute-start.1 = (bf16[192,128]{1,0:T(8,128)(2,1)S(1)}, bf16[192,128]{1,0:T(8,128)(2,1)S(1)}, u32[]{:S(2)}, u32[]{:S(2)}) collective-permute-start(bf16[192,128]{1,0:T(8,128)(2,1)S(1)} %get-tuple-element.11), channel_id=1, source_target_pairs={{0,4},{1,5},{2,6},{3,7},{4,0},{5,1},{6,2},{7,3},{8,12},{9,13},{10,... | collective-permute-start | bytes 147464 | tf_op jit(solution)/shard_map/ppermute | solution.py:44
  18.4 4.1 %collective-permute-start = (bf16[192,128]{1,0:T(8,128)(2,1)S(1)}, bf16[192,128]{1,0:T(8,128)(2,1)S(1)}, u32[]{:S(2)}, u32[]{:S(2)}) collective-permute-start(bf16[192,128]{1,0:T(8,128)(2,1)S(1)} %get-tuple-element.11), channel_id=1, source_target_pairs={{0,2},{1,3},{2,0},{3,1},{4,6},{5,7},{6,4},{7,5},{8,10},{9,11},{10,... | collective-permute-start | bytes 147464 | tf_op jit(solution)/shard_map/ppermute | solution.py:44
  22.5 4.2 %copy-start.1 = (f32[24,1024]{1,0:T(8,128)S(1)}, f32[24,1024]{1,0:T(8,128)}, u32[]{:S(2)}) copy-start(f32[24,1024]{1,0:T(8,128)} %refs_4_.2) | copy-start | bytes 294916
  22.6 5.3 %copy-start.6 = (bf16[24,8192]{1,0:T(8,128)(2,1)}, bf16[24,8192]{1,0:T(8,128)(2,1)S(1)}, u32[]{:S(2)}) copy-start(bf16[24,8192]{1,0:T(8,128)(2,1)S(1)} %collective-permute-done.12.refs_6_) | copy-start | bytes 1179652
  22.6 31.6 %collective-permute-start.14 = (bf16[24,8192]{1,0:T(8,128)(2,1)S(1)}, bf16[24,8192]{1,0:T(8,128)(2,1)S(1)}, u32[]{:S(2)}, u32[]{:S(2)}) collective-permute-start(bf16[24,8192]{1,0:T(8,128)(2,1)S(1)} %collective-permute-done.12.refs_6_), channel_id=1, source_target_pairs={{8,0},{16,24},{9,1},{17,25},{10,2},{18,26},{11,3},{19,27},{12,4},{... | collective-permute-start | bytes 1179656 | tf_op jit(solution)/shard_map/ppermute | solution.py:358
  23.9 35.3 %collective-permute-start.15 = (bf16[24,8192]{1,0:T(8,128)(2,1)}, bf16[24,8192]{1,0:T(8,128)(2,1)S(1)}, u32[]{:S(2)}, u32[]{:S(2)}) collective-permute-start(bf16[24,8192]{1,0:T(8,128)(2,1)} %collective-permute-done.13.refs_7_), channel_id=1, source_target_pairs={{8,0},{16,24},{9,1},{17,25},{10,2},{18,26},{11,3},{19,27},{12,4},{... | collective-permute-start | bytes 1179656 | tf_op jit(solution)/shard_map/ppermute | solution.py:358
  25.2 1.6 %copy-start.3 = (s32[1024,1]{0,1:T(1,128)S(1)}, s32[1024,1]{0,1:T(1,128)}, u32[]{:S(2)}) copy-start(s32[1024,1]{0,1:T(1,128)} %param.10) | copy-start | bytes 12292
  25.2 1.6 %copy-start.4 = (f32[1024]{0:T(1024)S(1)}, f32[1024]{0:T(1024)}, u32[]{:S(2)}) copy-start(f32[1024]{0:T(1024)} %param.11) | copy-start | bytes 12292
  25.2 1.5 %copy-start.2 = (f32[1024]{0:T(1024)S(1)}, f32[1024]{0:T(1024)}, u32[]{:S(2)}) copy-start(f32[1024]{0:T(1024)} %param.12) | copy-start | bytes 12292
  25.2 1.5 %collective-permute-start.3 = (bf16[768,128]{1,0:T(8,128)(2,1)S(1)}, bf16[768,128]{1,0:T(8,128)(2,1)S(1)}, u32[]{:S(2)}, u32[]{:S(2)}) collective-permute-start(bf16[768,128]{1,0:T(8,128)(2,1)S(1)} %constant_dynamic-update-slice_fusion.refs_0_), channel_id=1, source_target_pairs={{0,1},{1,0},{2,3},{3,2},{4,5},{5,4},{6,7},{7,6},{8,9},{9,8},{10,11... | collective-permute-start | bytes 589832 | tf_op jit(solution)/shard_map/ppermute | solution.py:44
  27.8 6.0 %collective-permute-start.6 = (bf16[24,1152]{1,0:T(8,128)(2,1)S(1)}, bf16[24,1152]{1,0:T(8,128)(2,1)S(1)}, u32[]{:S(2)}, u32[]{:S(2)}) collective-permute-start(bf16[24,1152]{1,0:T(8,128)(2,1)S(1)} %get-tuple-element.12.refs_0_), channel_id=1, source_target_pairs={{0,24},{8,16},{16,8},{24,0},{1,25},{9,17},{17,9},{25,1},{2,26},{10... | collective-permute-start | bytes 165896 | tf_op jit(solution)/shard_map/ppermute | solution.py:44
  31.5 5.8 %collective-permute-start.5 = (bf16[24,1152]{1,0:T(8,128)(2,1)S(1)}, bf16[24,1152]{1,0:T(8,128)(2,1)S(1)}, u32[]{:S(2)}, u32[]{:S(2)}) collective-permute-start(bf16[24,1152]{1,0:T(8,128)(2,1)S(1)} %get-tuple-element.12.refs_0_), channel_id=1, source_target_pairs={{0,16},{8,24},{16,0},{24,8},{1,17},{9,25},{17,1},{25,9},{2,18},{10... | collective-permute-start | bytes 165896 | tf_op jit(solution)/shard_map/ppermute | solution.py:44
  33.1 13.1 %collective-permute-start.4 = (bf16[24,1152]{1,0:T(8,128)(2,1)S(1)}, bf16[24,1152]{1,0:T(8,128)(2,1)S(1)}, u32[]{:S(2)}, u32[]{:S(2)}) collective-permute-start(bf16[24,1152]{1,0:T(8,128)(2,1)S(1)} %get-tuple-element.12.refs_0_), channel_id=1, source_target_pairs={{0,8},{8,0},{16,24},{24,16},{1,9},{9,1},{17,25},{25,17},{2,10},{10... | collective-permute-start | bytes 165896 | tf_op jit(solution)/shard_map/ppermute | solution.py:44
  46.5 1.3 %collective-permute-start.7 = (f32[104,128]{1,0:T(8,128)S(1)}, f32[104,128]{1,0:T(8,128)S(1)}, u32[]{:S(2)}, u32[]{:S(2)}) collective-permute-start(f32[104,128]{1,0:T(8,128)S(1)} %shard_map.75), channel_id=1, source_target_pairs={{0,1},{1,0},{2,3},{3,2},{4,5},{5,4},{6,7},{7,6},{8,9},{9,8},{10,11... | collective-permute-start | bytes 159752 | tf_op jit(solution)/shard_map/ppermute | solution.py:44
  47.8 5.1 %collective-permute-start.10 = (f32[104,128]{1,0:T(8,128)S(1)}, f32[104,128]{1,0:T(8,128)S(1)}, u32[]{:S(2)}, u32[]{:S(2)}) collective-permute-start(f32[104,128]{1,0:T(8,128)S(1)} %add.3.refs_0_), channel_id=1, source_target_pairs={{0,6},{1,7},{2,4},{3,5},{4,2},{5,3},{6,0},{7,1},{8,14},{9,15},{10,... | collective-permute-start | bytes 159752 | tf_op jit(solution)/shard_map/ppermute | solution.py:44
  49.3 4.4 %collective-permute-start.9 = (f32[104,128]{1,0:T(8,128)S(1)}, f32[104,128]{1,0:T(8,128)S(1)}, u32[]{:S(2)}, u32[]{:S(2)}) collective-permute-start(f32[104,128]{1,0:T(8,128)S(1)} %add.3.refs_0_), channel_id=1, source_target_pairs={{0,4},{1,5},{2,6},{3,7},{4,0},{5,1},{6,2},{7,3},{8,12},{9,13},{10,... | collective-permute-start | bytes 159752 | tf_op jit(solution)/shard_map/ppermute | solution.py:44
  49.9 4.2 %collective-permute-start.8 = (f32[104,128]{1,0:T(8,128)S(1)}, f32[104,128]{1,0:T(8,128)S(1)}, u32[]{:S(2)}, u32[]{:S(2)}) collective-permute-start(f32[104,128]{1,0:T(8,128)S(1)} %add.3.refs_0_), channel_id=1, source_target_pairs={{0,2},{1,3},{2,0},{3,1},{4,6},{5,7},{6,4},{7,5},{8,10},{9,11},{10,... | collective-permute-start | bytes 159752 | tf_op jit(solution)/shard_map/ppermute | solution.py:44

commit v5 on v4

--- a/solution.py
+++ b/solution.py
@@ -389,9 +389,8 @@
     )
     payloads = [sent] + [exchange(sent, "grp", distance) for distance in range(1, n_grp)]
     if line:
-        ends = [(1, 0), (2, 3)]
         near_far = in_hbm(pairs_exchange(near, "grp", [(1, 2), (2, 1)]))
-        middle_far = pairs_exchange(middle, "grp", ends)
+        middle_far = exchange(middle, "grp", 1)
     width = round_up(members + j_dev, LANES)
     (partial_sums,) = vmem_call(
         functools.partial(pair_kernel, n_grp, j_dev, scale_root),
@@ -406,7 +405,7 @@
         parts = [total] + [exchange(total, "vox", distance) for distance in group]
     count = members * obs_dev * n_vox
     if line:
-        far = pairs_exchange(near_far, "grp", ends)
+        far = exchange(near_far, "grp", 1)
         weights, mixed = weigh(
             parts, log_modulus, [[near], [middle], [near_far, middle_far]], members, count, scale_root
         )

time: 60.6 us -> 59.3 us (0.979)
  waiting for transfers between devices: 30.5 us -> 27.9 us
  starting transfers between devices: 20.4 us -> 21.9 us
    ppermute x12 -> x14, starting transfers between devices: 15.8 us -> 19.8 us  [exchange(): return lax.ppermute(value, axis, [(i, i ^ distance) for i in range(count)])]
    ppermute x12 -> x14, waiting for transfers between devices: 30.5 us -> 27.9 us  [exchange(): return lax.ppermute(value, axis, [(i, i ^ distance) for i in range(count)])]
    ppermute x4 -> x2, starting transfers between devices: 4.65 us -> 2.07 us  [pairs_exchange(): return lax.ppermute(value, axis, pairs)]
  transfers between devices with their start and end apart: 16 -> 16, of which waited for: 10 -> 8; matrix products, arithmetic and copies ran while one was open for 0% -> 0% of each run, Pallas kernels for 10% -> 11%
where the time goes in v5:
time: 59.3 us; the launch traced here: 59.2 us
  waiting for transfers between devices  27.9 us (47%)
  starting transfers between devices  21.9 us (37%)
  Pallas kernels  9.11 us (15%)
    ppermute x14, waiting for transfers between devices, exchange(): return lax.ppermute(value, axis, [(i, i ^ distance) for i in range(count)])  27.9 us
    ppermute x14, starting transfers between devices, exchange(): return lax.ppermute(value, axis, [(i, i ^ distance) for i in range(count)])  19.8 us
    pallas_call x1, Pallas kernels, weigh(): pl.pallas_call(functools.partial(weigh_kernel, members, j_dev, count, sca...  5.06 us
    ppermute x2, starting transfers between devices, pairs_exchange(): return lax.ppermute(value, axis, pairs)  2.07 us
    pallas_call x1, Pallas kernels, make_features(): pl.pallas_call(functools.partial(feature_kernel, block_vox), in_specs=[pl...  1.63 us
    pallas_call x2, Pallas kernels, vmem_call(): pl.pallas_call(kernel, in_specs=[IN_VMEM] * len(operands), out_specs=[IN_...  1.27 us
  transfers between devices with their start and end apart: 16, of which 8 were waited for; matrix products, arithmetic and copies ran while one was open for 0% of the time, Pallas kernels for 11%

profile of v5, /device:TPU:0, one launch (start us, length us, event | category | flops | bytes accessed | tf_op | source)
XLA Modules:
  0.0 59.2 jit_solution(11278320690802439155)
XLA Ops:
  0.0 1.6 %shard_map.73 = (bf16[24,8192]{1,0:T(8,128)(2,1)S(1)}, bf16[192,128]{1,0:T(8,128)(2,1)S(1)}) custom-call(f32[24,8192]{1,0:T(8,128)} %refs_4_.3, bf16[1024,128]{1,0:T(8,128)(2,1)} %basis_hbm.1), custom_call_target="tpu_custom_call" | custom-call | tf_op jit(solution)/shard_map/pallas_call | solution.py:105
  1.7 3.1 %collective-permute-start.11 = (bf16[24,8192]{1,0:T(8,128)(2,1)S(1)}, bf16[24,8192]{1,0:T(8,128)(2,1)S(1)}, u32[]{:S(2)}, u32[]{:S(2)}) collective-permute-start(bf16[24,8192]{1,0:T(8,128)(2,1)S(1)} %get-tuple-element.14), channel_id=1, source_target_pairs={{0,8},{8,0},{16,24},{24,16},{1,9},{9,1},{17,25},{25,17},{2,10},{10... | collective-permute-start | bytes 1179656 | tf_op jit(solution)/shard_map/ppermute | solution.py:44
  4.8 0.7 %collective-permute-start.12 = (bf16[24,8192]{1,0:T(8,128)(2,1)S(1)}, bf16[24,8192]{1,0:T(8,128)(2,1)S(1)}, u32[]{:S(2)}, u32[]{:S(2)}) collective-permute-start(bf16[24,8192]{1,0:T(8,128)(2,1)S(1)} %get-tuple-element.14), channel_id=1, source_target_pairs={{8,16},{16,8},{9,17},{17,9},{10,18},{18,10},{11,19},{19,11},{12,20... | collective-permute-start | bytes 1179656 | tf_op jit(solution)/shard_map/ppermute | solution.py:358
  5.5 8.4 %collective-permute-done.11.refs_5_ = bf16[24,8192]{1,0:T(8,128)(2,1)S(1)} collective-permute-done((bf16[24,8192]{1,0:T(8,128)(2,1)S(1)}, bf16[24,8192]{1,0:T(8,128)(2,1)S(1)}, u32[]{:S(2)}, u32[]{:S(2)}) %collective-permute-start.11) | collective-permute-done | bytes 393248 | tf_op jit(solution)/shard_map/ppermute | solution.py:44
  13.9 1.4 %collective-permute-start.13 = (bf16[24,8192]{1,0:T(8,128)(2,1)S(1)}, bf16[24,8192]{1,0:T(8,128)(2,1)}, u32[]{:S(2)}, u32[]{:S(2)}) collective-permute-start(bf16[24,8192]{1,0:T(8,128)(2,1)S(1)} %collective-permute-done.11.refs_5_), channel_id=1, source_target_pairs={{8,16},{16,8},{9,17},{17,9},{10,18},{18,10},{11,19},{19,11},{12,20... | collective-permute-start | bytes 1179656 | tf_op jit(solution)/shard_map/ppermute | solution.py:358
  15.3 2.6 %collective-permute-start.2 = (bf16[192,128]{1,0:T(8,128)(2,1)S(1)}, bf16[192,128]{1,0:T(8,128)(2,1)S(1)}, u32[]{:S(2)}, u32[]{:S(2)}) collective-permute-start(bf16[192,128]{1,0:T(8,128)(2,1)S(1)} %get-tuple-element.11), channel_id=1, source_target_pairs={{0,6},{1,7},{2,4},{3,5},{4,2},{5,3},{6,0},{7,1},{8,14},{9,15},{10,... | collective-permute-start | bytes 147464 | tf_op jit(solution)/shard_map/ppermute | solution.py:44
  17.9 0.5 collective-permute-start.1
  18.8 3.7 %collective-permute-done = bf16[192,128]{1,0:T(8,128)(2,1)S(1)} collective-permute-done((bf16[192,128]{1,0:T(8,128)(2,1)S(1)}, bf16[192,128]{1,0:T(8,128)(2,1)S(1)}, u32[]{:S(2)}, u32[]{:S(2)}) %collective-permute-start) | collective-permute-done | bytes 49184 | tf_op jit(solution)/shard_map/ppermute | solution.py:44
  22.6 3.8 %collective-permute-start.14 = (bf16[24,8192]{1,0:T(8,128)(2,1)S(1)}, bf16[24,8192]{1,0:T(8,128)(2,1)S(1)}, u32[]{:S(2)}, u32[]{:S(2)}) collective-permute-start(bf16[24,8192]{1,0:T(8,128)(2,1)S(1)} %collective-permute-done.12.refs_6_), channel_id=1, source_target_pairs={{0,8},{8,0},{16,24},{24,16},{1,9},{9,1},{17,25},{25,17},{2,10},{10... | collective-permute-start | bytes 1179656 | tf_op jit(solution)/shard_map/ppermute | solution.py:44
  26.4 1.2 %collective-permute-start.15 = (bf16[24,8192]{1,0:T(8,128)(2,1)}, bf16[24,8192]{1,0:T(8,128)(2,1)S(1)}, u32[]{:S(2)}, u32[]{:S(2)}) collective-permute-start(bf16[24,8192]{1,0:T(8,128)(2,1)} %collective-permute-done.13.refs_7_), channel_id=1, source_target_pairs={{0,8},{8,0},{16,24},{24,16},{1,9},{9,1},{17,25},{25,17},{2,10},{10... | collective-permute-start | bytes 1179656 | tf_op jit(solution)/shard_map/ppermute | solution.py:44
  27.7 1.4 %collective-permute-done.3.refs_1_ = bf16[768,128]{1,0:T(8,128)(2,1)S(1)} collective-permute-done((bf16[768,128]{1,0:T(8,128)(2,1)S(1)}, bf16[768,128]{1,0:T(8,128)(2,1)S(1)}, u32[]{:S(2)}, u32[]{:S(2)}) %collective-permute-start.3) | collective-permute-done | bytes 196640 | tf_op jit(solution)/shard_map/ppermute | solution.py:44
  29.2 1.0 %shard_map.74 = (bf16[24,1152]{1,0:T(8,128)(2,1)S(1)}, bf16[24,1024]{1,0:T(8,128)(2,1)S(1)}) custom-call(bf16[768,128]{1,0:T(8,128)(2,1)S(1)} %constant_dynamic-update-slice_fusion.refs_0_, bf16[768,128]{1,0:T(8,128)(2,1)S(1)} %collective-permute-done.3.refs_1_, bf16[1024,128]{1,0:T(8,128)(2,1)S(1)} %copy-done, s32[1,1024]{1,0:T(1,128)S(1)} %bitcast.5, ...), custom_call_target="tpu_custom_call" | custom-call | tf_op jit(solution)/shard_map/pallas_call | solution.py:30
  30.2 2.5 %collective-permute-start.6 = (bf16[24,1152]{1,0:T(8,128)(2,1)S(1)}, bf16[24,1152]{1,0:T(8,128)(2,1)S(1)}, u32[]{:S(2)}, u32[]{:S(2)}) collective-permute-start(bf16[24,1152]{1,0:T(8,128)(2,1)S(1)} %get-tuple-element.12.refs_0_), channel_id=1, source_target_pairs={{0,24},{8,16},{16,8},{24,0},{1,25},{9,17},{17,9},{25,1},{2,26},{10... | collective-permute-start | bytes 165896 | tf_op jit(solution)/shard_map/ppermute | solution.py:44
  32.8 1.9 %collective-permute-start.4 = (bf16[24,1152]{1,0:T(8,128)(2,1)S(1)}, bf16[24,1152]{1,0:T(8,128)(2,1)S(1)}, u32[]{:S(2)}, u32[]{:S(2)}) collective-permute-start(bf16[24,1152]{1,0:T(8,128)(2,1)S(1)} %get-tuple-element.12.refs_0_), channel_id=1, source_target_pairs={{0,8},{8,0},{16,24},{24,16},{1,9},{9,1},{17,25},{25,17},{2,10},{10... | collective-permute-start | bytes 165896 | tf_op jit(solution)/shard_map/ppermute | solution.py:44
  34.7 10.3 %collective-permute-done.6.refs_3_ = bf16[24,1152]{1,0:T(8,128)(2,1)S(1)} collective-permute-done((bf16[24,1152]{1,0:T(8,128)(2,1)S(1)}, bf16[24,1152]{1,0:T(8,128)(2,1)S(1)}, u32[]{:S(2)}, u32[]{:S(2)}) %collective-permute-start.6) | collective-permute-done | bytes 55328 | tf_op jit(solution)/shard_map/ppermute | solution.py:44
  45.3 1.2 %collective-permute-done.7 = f32[104,128]{1,0:T(8,128)S(1)} collective-permute-done((f32[104,128]{1,0:T(8,128)S(1)}, f32[104,128]{1,0:T(8,128)S(1)}, u32[]{:S(2)}, u32[]{:S(2)}) %collective-permute-start.7) | collective-permute-done | bytes 53280 | tf_op jit(solution)/shard_map/ppermute | solution.py:44
  46.6 1.5 %collective-permute-start.10 = (f32[104,128]{1,0:T(8,128)S(1)}, f32[104,128]{1,0:T(8,128)S(1)}, u32[]{:S(2)}, u32[]{:S(2)}) collective-permute-start(f32[104,128]{1,0:T(8,128)S(1)} %add.3.refs_0_), channel_id=1, source_target_pairs={{0,6},{1,7},{2,4},{3,5},{4,2},{5,3},{6,0},{7,1},{8,14},{9,15},{10,... | collective-permute-start | bytes 159752 | tf_op jit(solution)/shard_map/ppermute | solution.py:44
  48.1 0.6 collective-permute-start.9
  48.7 1.4 %collective-permute-start.8 = (f32[104,128]{1,0:T(8,128)S(1)}, f32[104,128]{1,0:T(8,128)S(1)}, u32[]{:S(2)}, u32[]{:S(2)}) collective-permute-start(f32[104,128]{1,0:T(8,128)S(1)} %add.3.refs_0_), channel_id=1, source_target_pairs={{0,2},{1,3},{2,0},{3,1},{4,6},{5,7},{6,4},{7,5},{8,10},{9,11},{10,... | collective-permute-start | bytes 159752 | tf_op jit(solution)/shard_map/ppermute | solution.py:44
  50.1 1.5 %collective-permute-done.10.refs_3_ = f32[104,128]{1,0:T(8,128)S(1)} collective-permute-done((f32[104,128]{1,0:T(8,128)S(1)}, f32[104,128]{1,0:T(8,128)S(1)}, u32[]{:S(2)}, u32[]{:S(2)}) %collective-permute-start.10) | collective-permute-done | bytes 53280 | tf_op jit(solution)/shard_map/ppermute | solution.py:44
  51.7 0.9 %collective-permute-done.9.refs_2_ = f32[104,128]{1,0:T(8,128)S(1)} collective-permute-done((f32[104,128]{1,0:T(8,128)S(1)}, f32[104,128]{1,0:T(8,128)S(1)}, u32[]{:S(2)}, u32[]{:S(2)}) %collective-permute-start.9) | collective-permute-done | bytes 53280 | tf_op jit(solution)/shard_map/ppermute | solution.py:44
  52.5 0.4 collective-permute-done.8.refs_1_
  52.9 5.1 %shard_map.76 = (bf16[24,128]{1,0:T(8,128)(2,1)S(1)}, f32[24,8192]{1,0:T(8,128)S(1)}) custom-call(f32[104,128]{1,0:T(8,128)S(1)} %add.3.refs_0_, f32[104,128]{1,0:T(8,128)S(1)} %collective-permute-done.8.refs_1_, f32[104,128]{1,0:T(8,128)S(1)} %collective-permute-done.9.refs_2_, f32[104,128]{1,0:T(8,128)S(1)} %collective-permute-done.10.refs_3_, ...), custom_call_target="tpu_custom_call" | custom-call | tf_op jit(solution)/shard_map/pallas_call | solution.py:327
  58.0 1.2 %shard_map.77 = f32[24,8192]{1,0:T(8,128)} custom-call(bf16[24,128]{1,0:T(8,128)(2,1)S(1)} %get-tuple-element.15.weights_ref, f32[24,8192]{1,0:T(8,128)S(1)} %get-tuple-element.16.mixed_ref, bf16[24,8192]{1,0:T(8,128)(2,1)S(1)} %collective-permute-done.15.last_ref), custom_call_target="tpu_custom_call" | custom-call | tf_op jit(solution)/shard_map/pallas_call | solution.py:345
  (32 shorter events, 0.9 us)
Async XLA Ops:
  1.6 27.5 %copy-start = (bf16[1024,128]{1,0:T(8,128)(2,1)S(1)}, bf16[1024,128]{1,0:T(8,128)(2,1)}, u32[]{:S(2)}) copy-start(bf16[1024,128]{1,0:T(8,128)(2,1)} %refs_2_.1) | copy-start | bytes 786436
  1.7 12.2 %collective-permute-start.11 = (bf16[24,8192]{1,0:T(8,128)(2,1)S(1)}, bf16[24,8192]{1,0:T(8,128)(2,1)S(1)}, u32[]{:S(2)}, u32[]{:S(2)}) collective-permute-start(bf16[24,8192]{1,0:T(8,128)(2,1)S(1)} %get-tuple-element.14), channel_id=1, source_target_pairs={{0,8},{8,0},{16,24},{24,16},{1,9},{9,1},{17,25},{25,17},{2,10},{10... | collective-permute-start | bytes 1179656 | tf_op jit(solution)/shard_map/ppermute | solution.py:44
  4.8 17.8 %collective-permute-start.12 = (bf16[24,8192]{1,0:T(8,128)(2,1)S(1)}, bf16[24,8192]{1,0:T(8,128)(2,1)S(1)}, u32[]{:S(2)}, u32[]{:S(2)}) collective-permute-start(bf16[24,8192]{1,0:T(8,128)(2,1)S(1)} %get-tuple-element.14), channel_id=1, source_target_pairs={{8,16},{16,8},{9,17},{17,9},{10,18},{18,10},{11,19},{19,11},{12,20... | collective-permute-start | bytes 1179656 | tf_op jit(solution)/shard_map/ppermute | solution.py:358
  13.9 16.3 %copy-start.5 = (bf16[24,8192]{1,0:T(8,128)(2,1)}, bf16[24,8192]{1,0:T(8,128)(2,1)S(1)}, u32[]{:S(2)}) copy-start(bf16[24,8192]{1,0:T(8,128)(2,1)S(1)} %collective-permute-done.11.refs_5_) | copy-start | bytes 1179652
  13.9 12.5 %collective-permute-start.13 = (bf16[24,8192]{1,0:T(8,128)(2,1)S(1)}, bf16[24,8192]{1,0:T(8,128)(2,1)}, u32[]{:S(2)}, u32[]{:S(2)}) collective-permute-start(bf16[24,8192]{1,0:T(8,128)(2,1)S(1)} %collective-permute-done.11.refs_5_), channel_id=1, source_target_pairs={{8,16},{16,8},{9,17},{17,9},{10,18},{18,10},{11,19},{19,11},{12,20... | collective-permute-start | bytes 1179656 | tf_op jit(solution)/shard_map/ppermute | solution.py:358
  15.3 12.3 %collective-permute-start.2 = (bf16[192,128]{1,0:T(8,128)(2,1)S(1)}, bf16[192,128]{1,0:T(8,128)(2,1)S(1)}, u32[]{:S(2)}, u32[]{:S(2)}) collective-permute-start(bf16[192,128]{1,0:T(8,128)(2,1)S(1)} %get-tuple-element.11), channel_id=1, source_target_pairs={{0,6},{1,7},{2,4},{3,5},{4,2},{5,3},{6,0},{7,1},{8,14},{9,15},{10,... | collective-permute-start | bytes 147464 | tf_op jit(solution)/shard_map/ppermute | solution.py:44
  17.9 4.6 %collective-permute-start.1 = (bf16[192,128]{1,0:T(8,128)(2,1)S(1)}, bf16[192,128]{1,0:T(8,128)(2,1)S(1)}, u32[]{:S(2)}, u32[]{:S(2)}) collective-permute-start(bf16[192,128]{1,0:T(8,128)(2,1)S(1)} %get-tuple-element.11), channel_id=1, source_target_pairs={{0,4},{1,5},{2,6},{3,7},{4,0},{5,1},{6,2},{7,3},{8,12},{9,13},{10,... | collective-permute-start | bytes 147464 | tf_op jit(solution)/shard_map/ppermute | solution.py:44
  18.4 4.1 %collective-permute-start = (bf16[192,128]{1,0:T(8,128)(2,1)S(1)}, bf16[192,128]{1,0:T(8,128)(2,1)S(1)}, u32[]{:S(2)}, u32[]{:S(2)}) collective-permute-start(bf16[192,128]{1,0:T(8,128)(2,1)S(1)} %get-tuple-element.11), channel_id=1, source_target_pairs={{0,2},{1,3},{2,0},{3,1},{4,6},{5,7},{6,4},{7,5},{8,10},{9,11},{10,... | collective-permute-start | bytes 147464 | tf_op jit(solution)/shard_map/ppermute | solution.py:44
  22.5 6.7 %copy-start.1 = (f32[24,1024]{1,0:T(8,128)S(1)}, f32[24,1024]{1,0:T(8,128)}, u32[]{:S(2)}) copy-start(f32[24,1024]{1,0:T(8,128)} %refs_4_.2) | copy-start | bytes 294916
  22.6 7.7 %copy-start.6 = (bf16[24,8192]{1,0:T(8,128)(2,1)}, bf16[24,8192]{1,0:T(8,128)(2,1)S(1)}, u32[]{:S(2)}) copy-start(bf16[24,8192]{1,0:T(8,128)(2,1)S(1)} %collective-permute-done.12.refs_6_) | copy-start | bytes 1179652
  22.6 30.4 %collective-permute-start.14 = (bf16[24,8192]{1,0:T(8,128)(2,1)S(1)}, bf16[24,8192]{1,0:T(8,128)(2,1)S(1)}, u32[]{:S(2)}, u32[]{:S(2)}) collective-permute-start(bf16[24,8192]{1,0:T(8,128)(2,1)S(1)} %collective-permute-done.12.refs_6_), channel_id=1, source_target_pairs={{0,8},{8,0},{16,24},{24,16},{1,9},{9,1},{17,25},{25,17},{2,10},{10... | collective-permute-start | bytes 1179656 | tf_op jit(solution)/shard_map/ppermute | solution.py:44
  26.4 31.6 %collective-permute-start.15 = (bf16[24,8192]{1,0:T(8,128)(2,1)}, bf16[24,8192]{1,0:T(8,128)(2,1)S(1)}, u32[]{:S(2)}, u32[]{:S(2)}) collective-permute-start(bf16[24,8192]{1,0:T(8,128)(2,1)} %collective-permute-done.13.refs_7_), channel_id=1, source_target_pairs={{0,8},{8,0},{16,24},{24,16},{1,9},{9,1},{17,25},{25,17},{2,10},{10... | collective-permute-start | bytes 1179656 | tf_op jit(solution)/shard_map/ppermute | solution.py:44
  27.6 1.5 %copy-start.3 = (s32[1024,1]{0,1:T(1,128)S(1)}, s32[1024,1]{0,1:T(1,128)}, u32[]{:S(2)}) copy-start(s32[1024,1]{0,1:T(1,128)} %param.10) | copy-start | bytes 12292
  27.6 1.5 %copy-start.4 = (f32[1024]{0:T(1024)S(1)}, f32[1024]{0:T(1024)}, u32[]{:S(2)}) copy-start(f32[1024]{0:T(1024)} %param.11) | copy-start | bytes 12292
  27.6 1.5 %copy-start.2 = (f32[1024]{0:T(1024)S(1)}, f32[1024]{0:T(1024)}, u32[]{:S(2)}) copy-start(f32[1024]{0:T(1024)} %param.12) | copy-start | bytes 12292
  27.6 1.5 %collective-permute-start.3 = (bf16[768,128]{1,0:T(8,128)(2,1)S(1)}, bf16[768,128]{1,0:T(8,128)(2,1)S(1)}, u32[]{:S(2)}, u32[]{:S(2)}) collective-permute-start(bf16[768,128]{1,0:T(8,128)(2,1)S(1)} %constant_dynamic-update-slice_fusion.refs_0_), channel_id=1, source_target_pairs={{0,1},{1,0},{2,3},{3,2},{4,5},{5,4},{6,7},{7,6},{8,9},{9,8},{10,11... | collective-permute-start | bytes 589832 | tf_op jit(solution)/shard_map/ppermute | solution.py:44
  30.2 14.7 %collective-permute-start.6 = (bf16[24,1152]{1,0:T(8,128)(2,1)S(1)}, bf16[24,1152]{1,0:T(8,128)(2,1)S(1)}, u32[]{:S(2)}, u32[]{:S(2)}) collective-permute-start(bf16[24,1152]{1,0:T(8,128)(2,1)S(1)} %get-tuple-element.12.refs_0_), channel_id=1, source_target_pairs={{0,24},{8,16},{16,8},{24,0},{1,25},{9,17},{17,9},{25,1},{2,26},{10... | collective-permute-start | bytes 165896 | tf_op jit(solution)/shard_map/ppermute | solution.py:44
  32.8 12.2 %collective-permute-start.5 = (bf16[24,1152]{1,0:T(8,128)(2,1)S(1)}, bf16[24,1152]{1,0:T(8,128)(2,1)S(1)}, u32[]{:S(2)}, u32[]{:S(2)}) collective-permute-start(bf16[24,1152]{1,0:T(8,128)(2,1)S(1)} %get-tuple-element.12.refs_0_), channel_id=1, source_target_pairs={{0,16},{8,24},{16,0},{24,8},{1,17},{9,25},{17,1},{25,9},{2,18},{10... | collective-permute-start | bytes 165896 | tf_op jit(solution)/shard_map/ppermute | solution.py:44
  32.8 12.2 %collective-permute-start.4 = (bf16[24,1152]{1,0:T(8,128)(2,1)S(1)}, bf16[24,1152]{1,0:T(8,128)(2,1)S(1)}, u32[]{:S(2)}, u32[]{:S(2)}) collective-permute-start(bf16[24,1152]{1,0:T(8,128)(2,1)S(1)} %get-tuple-element.12.refs_0_), channel_id=1, source_target_pairs={{0,8},{8,0},{16,24},{24,16},{1,9},{9,1},{17,25},{25,17},{2,10},{10... | collective-permute-start | bytes 165896 | tf_op jit(solution)/shard_map/ppermute | solution.py:44
  45.2 1.3 %collective-permute-start.7 = (f32[104,128]{1,0:T(8,128)S(1)}, f32[104,128]{1,0:T(8,128)S(1)}, u32[]{:S(2)}, u32[]{:S(2)}) collective-permute-start(f32[104,128]{1,0:T(8,128)S(1)} %shard_map.75), channel_id=1, source_target_pairs={{0,1},{1,0},{2,3},{3,2},{4,5},{5,4},{6,7},{7,6},{8,9},{9,8},{10,11... | collective-permute-start | bytes 159752 | tf_op jit(solution)/shard_map/ppermute | solution.py:44
  46.6 5.1 %collective-permute-start.10 = (f32[104,128]{1,0:T(8,128)S(1)}, f32[104,128]{1,0:T(8,128)S(1)}, u32[]{:S(2)}, u32[]{:S(2)}) collective-permute-start(f32[104,128]{1,0:T(8,128)S(1)} %add.3.refs_0_), channel_id=1, source_target_pairs={{0,6},{1,7},{2,4},{3,5},{4,2},{5,3},{6,0},{7,1},{8,14},{9,15},{10,... | collective-permute-start | bytes 159752 | tf_op jit(solution)/shard_map/ppermute | solution.py:44
  48.1 4.4 %collective-permute-start.9 = (f32[104,128]{1,0:T(8,128)S(1)}, f32[104,128]{1,0:T(8,128)S(1)}, u32[]{:S(2)}, u32[]{:S(2)}) collective-permute-start(f32[104,128]{1,0:T(8,128)S(1)} %add.3.refs_0_), channel_id=1, source_target_pairs={{0,4},{1,5},{2,6},{3,7},{4,0},{5,1},{6,2},{7,3},{8,12},{9,13},{10,... | collective-permute-start | bytes 159752 | tf_op jit(solution)/shard_map/ppermute | solution.py:44
  48.7 4.2 %collective-permute-start.8 = (f32[104,128]{1,0:T(8,128)S(1)}, f32[104,128]{1,0:T(8,128)S(1)}, u32[]{:S(2)}, u32[]{:S(2)}) collective-permute-start(f32[104,128]{1,0:T(8,128)S(1)} %add.3.refs_0_), channel_id=1, source_target_pairs={{0,2},{1,3},{2,0},{3,1},{4,6},{5,7},{6,4},{7,5},{8,10},{9,11},{10,... | collective-permute-start | bytes 159752 | tf_op jit(solution)/shard_map/ppermute | solution.py:44

commit v6 on v5

--- a/solution.py
+++ b/solution.py
@@ -387,7 +387,9 @@
         observed,
         noise,
     )
-    payloads = [sent] + [exchange(sent, "grp", distance) for distance in range(1, n_grp)]
+    payloads = [sent]
+    for distance in range(1, n_grp):
+        payloads.append(exchange(sent, "grp", distance))
     if line:
         near_far = in_hbm(pairs_exchange(near, "grp", [(1, 2), (2, 1)]))
         middle_far = exchange(middle, "grp", 1)
@@ -402,7 +404,9 @@
     parts = [partial_sums]
     for group in reversed(stages(n_vox)):
         total = functools.reduce(jnp.add, parts)
-        parts = [total] + [exchange(total, "vox", distance) for distance in group]
+        parts = [total]
+        for distance in group:
+            parts.append(exchange(total, "vox", distance))
     count = members * obs_dev * n_vox
     if line:
         far = exchange(near_far, "grp", 1)

time: 59.3 us -> 59.3 us (level)
  no operation moved by 1% of the time
where the time goes in v6:
time: 59.3 us; the launch traced here: 59.2 us
  waiting for transfers between devices  27.9 us (47%)
  starting transfers between devices  21.9 us (37%)
  Pallas kernels  9.11 us (15%)
    ppermute x14, waiting for transfers between devices, exchange(): return lax.ppermute(value, axis, [(i, i ^ distance) for i in range(count)])  27.9 us
    ppermute x14, starting transfers between devices, exchange(): return lax.ppermute(value, axis, [(i, i ^ distance) for i in range(count)])  19.8 us
    pallas_call x1, Pallas kernels, weigh(): pl.pallas_call(functools.partial(weigh_kernel, members, j_dev, count, sca...  5.06 us
    ppermute x2, starting transfers between devices, pairs_exchange(): return lax.ppermute(value, axis, pairs)  2.07 us
    pallas_call x1, Pallas kernels, make_features(): pl.pallas_call(functools.partial(feature_kernel, block_vox), in_specs=[pl...  1.63 us
    pallas_call x2, Pallas kernels, vmem_call(): pl.pallas_call(kernel, in_specs=[IN_VMEM] * len(operands), out_specs=[IN_...  1.27 us
  transfers between devices with their start and end apart: 16, of which 8 were waited for; matrix products, arithmetic and copies ran while one was open for 0% of the time, Pallas kernels for 11%

profile of v6, /device:TPU:0, one launch (start us, length us, event | category | flops | bytes accessed | tf_op | source)
XLA Modules:
  0.0 59.2 jit_solution(11278320690802439155)
XLA Ops:
  0.0 1.6 %shard_map.73 = (bf16[24,8192]{1,0:T(8,128)(2,1)S(1)}, bf16[192,128]{1,0:T(8,128)(2,1)S(1)}) custom-call(f32[24,8192]{1,0:T(8,128)} %refs_4_.3, bf16[1024,128]{1,0:T(8,128)(2,1)} %basis_hbm.1), custom_call_target="tpu_custom_call" | custom-call | tf_op jit(solution)/shard_map/pallas_call | solution.py:105
  1.7 3.1 %collective-permute-start.11 = (bf16[24,8192]{1,0:T(8,128)(2,1)S(1)}, bf16[24,8192]{1,0:T(8,128)(2,1)S(1)}, u32[]{:S(2)}, u32[]{:S(2)}) collective-permute-start(bf16[24,8192]{1,0:T(8,128)(2,1)S(1)} %get-tuple-element.14), channel_id=1, source_target_pairs={{0,8},{8,0},{16,24},{24,16},{1,9},{9,1},{17,25},{25,17},{2,10},{10... | collective-permute-start | bytes 1179656 | tf_op jit(solution)/shard_map/ppermute | solution.py:44
  4.8 0.7 %collective-permute-start.12 = (bf16[24,8192]{1,0:T(8,128)(2,1)S(1)}, bf16[24,8192]{1,0:T(8,128)(2,1)S(1)}, u32[]{:S(2)}, u32[]{:S(2)}) collective-permute-start(bf16[24,8192]{1,0:T(8,128)(2,1)S(1)} %get-tuple-element.14), channel_id=1, source_target_pairs={{8,16},{16,8},{9,17},{17,9},{10,18},{18,10},{11,19},{19,11},{12,20... | collective-permute-start | bytes 1179656 | tf_op jit(solution)/shard_map/ppermute | solution.py:358
  5.5 8.4 %collective-permute-done.11.refs_5_ = bf16[24,8192]{1,0:T(8,128)(2,1)S(1)} collective-permute-done((bf16[24,8192]{1,0:T(8,128)(2,1)S(1)}, bf16[24,8192]{1,0:T(8,128)(2,1)S(1)}, u32[]{:S(2)}, u32[]{:S(2)}) %collective-permute-start.11) | collective-permute-done | bytes 393248 | tf_op jit(solution)/shard_map/ppermute | solution.py:44
  13.9 1.4 %collective-permute-start.13 = (bf16[24,8192]{1,0:T(8,128)(2,1)S(1)}, bf16[24,8192]{1,0:T(8,128)(2,1)}, u32[]{:S(2)}, u32[]{:S(2)}) collective-permute-start(bf16[24,8192]{1,0:T(8,128)(2,1)S(1)} %collective-permute-done.11.refs_5_), channel_id=1, source_target_pairs={{8,16},{16,8},{9,17},{17,9},{10,18},{18,10},{11,19},{19,11},{12,20... | collective-permute-start | bytes 1179656 | tf_op jit(solution)/shard_map/ppermute | solution.py:358
  15.3 2.6 %collective-permute-start.2 = (bf16[192,128]{1,0:T(8,128)(2,1)S(1)}, bf16[192,128]{1,0:T(8,128)(2,1)S(1)}, u32[]{:S(2)}, u32[]{:S(2)}) collective-permute-start(bf16[192,128]{1,0:T(8,128)(2,1)S(1)} %get-tuple-element.11), channel_id=1, source_target_pairs={{0,6},{1,7},{2,4},{3,5},{4,2},{5,3},{6,0},{7,1},{8,14},{9,15},{10,... | collective-permute-start | bytes 147464 | tf_op jit(solution)/shard_map/ppermute | solution.py:44
  17.9 0.5 collective-permute-start.1
  18.8 3.7 %collective-permute-done = bf16[192,128]{1,0:T(8,128)(2,1)S(1)} collective-permute-done((bf16[192,128]{1,0:T(8,128)(2,1)S(1)}, bf16[192,128]{1,0:T(8,128)(2,1)S(1)}, u32[]{:S(2)}, u32[]{:S(2)}) %collective-permute-start) | collective-permute-done | bytes 49184 | tf_op jit(solution)/shard_map/ppermute | solution.py:44
  22.6 3.8 %collective-permute-start.14 = (bf16[24,8192]{1,0:T(8,128)(2,1)S(1)}, bf16[24,8192]{1,0:T(8,128)(2,1)S(1)}, u32[]{:S(2)}, u32[]{:S(2)}) collective-permute-start(bf16[24,8192]{1,0:T(8,128)(2,1)S(1)} %collective-permute-done.12.refs_6_), channel_id=1, source_target_pairs={{0,8},{8,0},{16,24},{24,16},{1,9},{9,1},{17,25},{25,17},{2,10},{10... | collective-permute-start | bytes 1179656 | tf_op jit(solution)/shard_map/ppermute | solution.py:44
  26.4 1.2 %collective-permute-start.15 = (bf16[24,8192]{1,0:T(8,128)(2,1)}, bf16[24,8192]{1,0:T(8,128)(2,1)S(1)}, u32[]{:S(2)}, u32[]{:S(2)}) collective-permute-start(bf16[24,8192]{1,0:T(8,128)(2,1)} %collective-permute-done.13.refs_7_), channel_id=1, source_target_pairs={{0,8},{8,0},{16,24},{24,16},{1,9},{9,1},{17,25},{25,17},{2,10},{10... | collective-permute-start | bytes 1179656 | tf_op jit(solution)/shard_map/ppermute | solution.py:44
  27.7 1.4 %collective-permute-done.3.refs_1_ = bf16[768,128]{1,0:T(8,128)(2,1)S(1)} collective-permute-done((bf16[768,128]{1,0:T(8,128)(2,1)S(1)}, bf16[768,128]{1,0:T(8,128)(2,1)S(1)}, u32[]{:S(2)}, u32[]{:S(2)}) %collective-permute-start.3) | collective-permute-done | bytes 196640 | tf_op jit(solution)/shard_map/ppermute | solution.py:44
  29.2 1.0 %shard_map.74 = (bf16[24,1152]{1,0:T(8,128)(2,1)S(1)}, bf16[24,1024]{1,0:T(8,128)(2,1)S(1)}) custom-call(bf16[768,128]{1,0:T(8,128)(2,1)S(1)} %constant_dynamic-update-slice_fusion.refs_0_, bf16[768,128]{1,0:T(8,128)(2,1)S(1)} %collective-permute-done.3.refs_1_, bf16[1024,128]{1,0:T(8,128)(2,1)S(1)} %copy-done, s32[1,1024]{1,0:T(1,128)S(1)} %bitcast.5, ...), custom_call_target="tpu_custom_call" | custom-call | tf_op jit(solution)/shard_map/pallas_call | solution.py:30
  30.2 2.5 %collective-permute-start.6 = (bf16[24,1152]{1,0:T(8,128)(2,1)S(1)}, bf16[24,1152]{1,0:T(8,128)(2,1)S(1)}, u32[]{:S(2)}, u32[]{:S(2)}) collective-permute-start(bf16[24,1152]{1,0:T(8,128)(2,1)S(1)} %get-tuple-element.12.refs_0_), channel_id=1, source_target_pairs={{0,24},{8,16},{16,8},{24,0},{1,25},{9,17},{17,9},{25,1},{2,26},{10... | collective-permute-start | bytes 165896 | tf_op jit(solution)/shard_map/ppermute | solution.py:44
  32.8 1.9 %collective-permute-start.4 = (bf16[24,1152]{1,0:T(8,128)(2,1)S(1)}, bf16[24,1152]{1,0:T(8,128)(2,1)S(1)}, u32[]{:S(2)}, u32[]{:S(2)}) collective-permute-start(bf16[24,1152]{1,0:T(8,128)(2,1)S(1)} %get-tuple-element.12.refs_0_), channel_id=1, source_target_pairs={{0,8},{8,0},{16,24},{24,16},{1,9},{9,1},{17,25},{25,17},{2,10},{10... | collective-permute-start | bytes 165896 | tf_op jit(solution)/shard_map/ppermute | solution.py:44
  34.7 10.3 %collective-permute-done.6.refs_3_ = bf16[24,1152]{1,0:T(8,128)(2,1)S(1)} collective-permute-done((bf16[24,1152]{1,0:T(8,128)(2,1)S(1)}, bf16[24,1152]{1,0:T(8,128)(2,1)S(1)}, u32[]{:S(2)}, u32[]{:S(2)}) %collective-permute-start.6) | collective-permute-done | bytes 55328 | tf_op jit(solution)/shard_map/ppermute | solution.py:44
  45.3 1.2 %collective-permute-done.7 = f32[104,128]{1,0:T(8,128)S(1)} collective-permute-done((f32[104,128]{1,0:T(8,128)S(1)}, f32[104,128]{1,0:T(8,128)S(1)}, u32[]{:S(2)}, u32[]{:S(2)}) %collective-permute-start.7) | collective-permute-done | bytes 53280 | tf_op jit(solution)/shard_map/ppermute | solution.py:44
  46.6 1.5 %collective-permute-start.10 = (f32[104,128]{1,0:T(8,128)S(1)}, f32[104,128]{1,0:T(8,128)S(1)}, u32[]{:S(2)}, u32[]{:S(2)}) collective-permute-start(f32[104,128]{1,0:T(8,128)S(1)} %add.3.refs_0_), channel_id=1, source_target_pairs={{0,6},{1,7},{2,4},{3,5},{4,2},{5,3},{6,0},{7,1},{8,14},{9,15},{10,... | collective-permute-start | bytes 159752 | tf_op jit(solution)/shard_map/ppermute | solution.py:44
  48.1 0.6 collective-permute-start.9
  48.7 1.4 %collective-permute-start.8 = (f32[104,128]{1,0:T(8,128)S(1)}, f32[104,128]{1,0:T(8,128)S(1)}, u32[]{:S(2)}, u32[]{:S(2)}) collective-permute-start(f32[104,128]{1,0:T(8,128)S(1)} %add.3.refs_0_), channel_id=1, source_target_pairs={{0,2},{1,3},{2,0},{3,1},{4,6},{5,7},{6,4},{7,5},{8,10},{9,11},{10,... | collective-permute-start | bytes 159752 | tf_op jit(solution)/shard_map/ppermute | solution.py:44
  50.1 1.5 %collective-permute-done.10.refs_3_ = f32[104,128]{1,0:T(8,128)S(1)} collective-permute-done((f32[104,128]{1,0:T(8,128)S(1)}, f32[104,128]{1,0:T(8,128)S(1)}, u32[]{:S(2)}, u32[]{:S(2)}) %collective-permute-start.10) | collective-permute-done | bytes 53280 | tf_op jit(solution)/shard_map/ppermute | solution.py:44
  51.7 0.9 %collective-permute-done.9.refs_2_ = f32[104,128]{1,0:T(8,128)S(1)} collective-permute-done((f32[104,128]{1,0:T(8,128)S(1)}, f32[104,128]{1,0:T(8,128)S(1)}, u32[]{:S(2)}, u32[]{:S(2)}) %collective-permute-start.9) | collective-permute-done | bytes 53280 | tf_op jit(solution)/shard_map/ppermute | solution.py:44
  52.5 0.4 collective-permute-done.8.refs_1_
  52.9 5.1 %shard_map.76 = (bf16[24,128]{1,0:T(8,128)(2,1)S(1)}, f32[24,8192]{1,0:T(8,128)S(1)}) custom-call(f32[104,128]{1,0:T(8,128)S(1)} %add.3.refs_0_, f32[104,128]{1,0:T(8,128)S(1)} %collective-permute-done.8.refs_1_, f32[104,128]{1,0:T(8,128)S(1)} %collective-permute-done.9.refs_2_, f32[104,128]{1,0:T(8,128)S(1)} %collective-permute-done.10.refs_3_, ...), custom_call_target="tpu_custom_call" | custom-call | tf_op jit(solution)/shard_map/pallas_call | solution.py:327
  58.0 1.2 %shard_map.77 = f32[24,8192]{1,0:T(8,128)} custom-call(bf16[24,128]{1,0:T(8,128)(2,1)S(1)} %get-tuple-element.15.weights_ref, f32[24,8192]{1,0:T(8,128)S(1)} %get-tuple-element.16.mixed_ref, bf16[24,8192]{1,0:T(8,128)(2,1)S(1)} %collective-permute-done.15.last_ref), custom_call_target="tpu_custom_call" | custom-call | tf_op jit(solution)/shard_map/pallas_call | solution.py:345
  (32 shorter events, 0.9 us)
Async XLA Ops:
  1.6 27.5 %copy-start = (bf16[1024,128]{1,0:T(8,128)(2,1)S(1)}, bf16[1024,128]{1,0:T(8,128)(2,1)}, u32[]{:S(2)}) copy-start(bf16[1024,128]{1,0:T(8,128)(2,1)} %refs_2_.1) | copy-start | bytes 786436
  1.7 12.2 %collective-permute-start.11 = (bf16[24,8192]{1,0:T(8,128)(2,1)S(1)}, bf16[24,8192]{1,0:T(8,128)(2,1)S(1)}, u32[]{:S(2)}, u32[]{:S(2)}) collective-permute-start(bf16[24,8192]{1,0:T(8,128)(2,1)S(1)} %get-tuple-element.14), channel_id=1, source_target_pairs={{0,8},{8,0},{16,24},{24,16},{1,9},{9,1},{17,25},{25,17},{2,10},{10... | collective-permute-start | bytes 1179656 | tf_op jit(solution)/shard_map/ppermute | solution.py:44
  4.8 17.8 %collective-permute-start.12 = (bf16[24,8192]{1,0:T(8,128)(2,1)S(1)}, bf16[24,8192]{1,0:T(8,128)(2,1)S(1)}, u32[]{:S(2)}, u32[]{:S(2)}) collective-permute-start(bf16[24,8192]{1,0:T(8,128)(2,1)S(1)} %get-tuple-element.14), channel_id=1, source_target_pairs={{8,16},{16,8},{9,17},{17,9},{10,18},{18,10},{11,19},{19,11},{12,20... | collective-permute-start | bytes 1179656 | tf_op jit(solution)/shard_map/ppermute | solution.py:358
  13.9 16.3 %copy-start.5 = (bf16[24,8192]{1,0:T(8,128)(2,1)}, bf16[24,8192]{1,0:T(8,128)(2,1)S(1)}, u32[]{:S(2)}) copy-start(bf16[24,8192]{1,0:T(8,128)(2,1)S(1)} %collective-permute-done.11.refs_5_) | copy-start | bytes 1179652
  13.9 12.5 %collective-permute-start.13 = (bf16[24,8192]{1,0:T(8,128)(2,1)S(1)}, bf16[24,8192]{1,0:T(8,128)(2,1)}, u32[]{:S(2)}, u32[]{:S(2)}) collective-permute-start(bf16[24,8192]{1,0:T(8,128)(2,1)S(1)} %collective-permute-done.11.refs_5_), channel_id=1, source_target_pairs={{8,16},{16,8},{9,17},{17,9},{10,18},{18,10},{11,19},{19,11},{12,20... | collective-permute-start | bytes 1179656 | tf_op jit(solution)/shard_map/ppermute | solution.py:358
  15.3 12.3 %collective-permute-start.2 = (bf16[192,128]{1,0:T(8,128)(2,1)S(1)}, bf16[192,128]{1,0:T(8,128)(2,1)S(1)}, u32[]{:S(2)}, u32[]{:S(2)}) collective-permute-start(bf16[192,128]{1,0:T(8,128)(2,1)S(1)} %get-tuple-element.11), channel_id=1, source_target_pairs={{0,6},{1,7},{2,4},{3,5},{4,2},{5,3},{6,0},{7,1},{8,14},{9,15},{10,... | collective-permute-start | bytes 147464 | tf_op jit(solution)/shard_map/ppermute | solution.py:44
  17.9 4.6 %collective-permute-start.1 = (bf16[192,128]{1,0:T(8,128)(2,1)S(1)}, bf16[192,128]{1,0:T(8,128)(2,1)S(1)}, u32[]{:S(2)}, u32[]{:S(2)}) collective-permute-start(bf16[192,128]{1,0:T(8,128)(2,1)S(1)} %get-tuple-element.11), channel_id=1, source_target_pairs={{0,4},{1,5},{2,6},{3,7},{4,0},{5,1},{6,2},{7,3},{8,12},{9,13},{10,... | collective-permute-start | bytes 147464 | tf_op jit(solution)/shard_map/ppermute | solution.py:44
  18.4 4.1 %collective-permute-start = (bf16[192,128]{1,0:T(8,128)(2,1)S(1)}, bf16[192,128]{1,0:T(8,128)(2,1)S(1)}, u32[]{:S(2)}, u32[]{:S(2)}) collective-permute-start(bf16[192,128]{1,0:T(8,128)(2,1)S(1)} %get-tuple-element.11), channel_id=1, source_target_pairs={{0,2},{1,3},{2,0},{3,1},{4,6},{5,7},{6,4},{7,5},{8,10},{9,11},{10,... | collective-permute-start | bytes 147464 | tf_op jit(solution)/shard_map/ppermute | solution.py:44
  22.5 6.7 %copy-start.1 = (f32[24,1024]{1,0:T(8,128)S(1)}, f32[24,1024]{1,0:T(8,128)}, u32[]{:S(2)}) copy-start(f32[24,1024]{1,0:T(8,128)} %refs_4_.2) | copy-start | bytes 294916
  22.6 7.7 %copy-start.6 = (bf16[24,8192]{1,0:T(8,128)(2,1)}, bf16[24,8192]{1,0:T(8,128)(2,1)S(1)}, u32[]{:S(2)}) copy-start(bf16[24,8192]{1,0:T(8,128)(2,1)S(1)} %collective-permute-done.12.refs_6_) | copy-start | bytes 1179652
  22.6 30.4 %collective-permute-start.14 = (bf16[24,8192]{1,0:T(8,128)(2,1)S(1)}, bf16[24,8192]{1,0:T(8,128)(2,1)S(1)}, u32[]{:S(2)}, u32[]{:S(2)}) collective-permute-start(bf16[24,8192]{1,0:T(8,128)(2,1)S(1)} %collective-permute-done.12.refs_6_), channel_id=1, source_target_pairs={{0,8},{8,0},{16,24},{24,16},{1,9},{9,1},{17,25},{25,17},{2,10},{10... | collective-permute-start | bytes 1179656 | tf_op jit(solution)/shard_map/ppermute | solution.py:44
  26.4 31.6 %collective-permute-start.15 = (bf16[24,8192]{1,0:T(8,128)(2,1)}, bf16[24,8192]{1,0:T(8,128)(2,1)S(1)}, u32[]{:S(2)}, u32[]{:S(2)}) collective-permute-start(bf16[24,8192]{1,0:T(8,128)(2,1)} %collective-permute-done.13.refs_7_), channel_id=1, source_target_pairs={{0,8},{8,0},{16,24},{24,16},{1,9},{9,1},{17,25},{25,17},{2,10},{10... | collective-permute-start | bytes 1179656 | tf_op jit(solution)/shard_map/ppermute | solution.py:44
  27.6 1.5 %copy-start.3 = (s32[1024,1]{0,1:T(1,128)S(1)}, s32[1024,1]{0,1:T(1,128)}, u32[]{:S(2)}) copy-start(s32[1024,1]{0,1:T(1,128)} %param.10) | copy-start | bytes 12292
  27.6 1.5 %copy-start.4 = (f32[1024]{0:T(1024)S(1)}, f32[1024]{0:T(1024)}, u32[]{:S(2)}) copy-start(f32[1024]{0:T(1024)} %param.11) | copy-start | bytes 12292
  27.6 1.5 %copy-start.2 = (f32[1024]{0:T(1024)S(1)}, f32[1024]{0:T(1024)}, u32[]{:S(2)}) copy-start(f32[1024]{0:T(1024)} %param.12) | copy-start | bytes 12292
  27.6 1.5 %collective-permute-start.3 = (bf16[768,128]{1,0:T(8,128)(2,1)S(1)}, bf16[768,128]{1,0:T(8,128)(2,1)S(1)}, u32[]{:S(2)}, u32[]{:S(2)}) collective-permute-start(bf16[768,128]{1,0:T(8,128)(2,1)S(1)} %constant_dynamic-update-slice_fusion.refs_0_), channel_id=1, source_target_pairs={{0,1},{1,0},{2,3},{3,2},{4,5},{5,4},{6,7},{7,6},{8,9},{9,8},{10,11... | collective-permute-start | bytes 589832 | tf_op jit(solution)/shard_map/ppermute | solution.py:44
  30.2 14.7 %collective-permute-start.6 = (bf16[24,1152]{1,0:T(8,128)(2,1)S(1)}, bf16[24,1152]{1,0:T(8,128)(2,1)S(1)}, u32[]{:S(2)}, u32[]{:S(2)}) collective-permute-start(bf16[24,1152]{1,0:T(8,128)(2,1)S(1)} %get-tuple-element.12.refs_0_), channel_id=1, source_target_pairs={{0,24},{8,16},{16,8},{24,0},{1,25},{9,17},{17,9},{25,1},{2,26},{10... | collective-permute-start | bytes 165896 | tf_op jit(solution)/shard_map/ppermute | solution.py:44
  32.8 12.2 %collective-permute-start.5 = (bf16[24,1152]{1,0:T(8,128)(2,1)S(1)}, bf16[24,1152]{1,0:T(8,128)(2,1)S(1)}, u32[]{:S(2)}, u32[]{:S(2)}) collective-permute-start(bf16[24,1152]{1,0:T(8,128)(2,1)S(1)} %get-tuple-element.12.refs_0_), channel_id=1, source_target_pairs={{0,16},{8,24},{16,0},{24,8},{1,17},{9,25},{17,1},{25,9},{2,18},{10... | collective-permute-start | bytes 165896 | tf_op jit(solution)/shard_map/ppermute | solution.py:44
  32.8 12.2 %collective-permute-start.4 = (bf16[24,1152]{1,0:T(8,128)(2,1)S(1)}, bf16[24,1152]{1,0:T(8,128)(2,1)S(1)}, u32[]{:S(2)}, u32[]{:S(2)}) collective-permute-start(bf16[24,1152]{1,0:T(8,128)(2,1)S(1)} %get-tuple-element.12.refs_0_), channel_id=1, source_target_pairs={{0,8},{8,0},{16,24},{24,16},{1,9},{9,1},{17,25},{25,17},{2,10},{10... | collective-permute-start | bytes 165896 | tf_op jit(solution)/shard_map/ppermute | solution.py:44
  45.2 1.3 %collective-permute-start.7 = (f32[104,128]{1,0:T(8,128)S(1)}, f32[104,128]{1,0:T(8,128)S(1)}, u32[]{:S(2)}, u32[]{:S(2)}) collective-permute-start(f32[104,128]{1,0:T(8,128)S(1)} %shard_map.75), channel_id=1, source_target_pairs={{0,1},{1,0},{2,3},{3,2},{4,5},{5,4},{6,7},{7,6},{8,9},{9,8},{10,11... | collective-permute-start | bytes 159752 | tf_op jit(solution)/shard_map/ppermute | solution.py:44
  46.6 5.1 %collective-permute-start.10 = (f32[104,128]{1,0:T(8,128)S(1)}, f32[104,128]{1,0:T(8,128)S(1)}, u32[]{:S(2)}, u32[]{:S(2)}) collective-permute-start(f32[104,128]{1,0:T(8,128)S(1)} %add.3.refs_0_), channel_id=1, source_target_pairs={{0,6},{1,7},{2,4},{3,5},{4,2},{5,3},{6,0},{7,1},{8,14},{9,15},{10,... | collective-permute-start | bytes 159752 | tf_op jit(solution)/shard_map/ppermute | solution.py:44
  48.1 4.4 %collective-permute-start.9 = (f32[104,128]{1,0:T(8,128)S(1)}, f32[104,128]{1,0:T(8,128)S(1)}, u32[]{:S(2)}, u32[]{:S(2)}) collective-permute-start(f32[104,128]{1,0:T(8,128)S(1)} %add.3.refs_0_), channel_id=1, source_target_pairs={{0,4},{1,5},{2,6},{3,7},{4,0},{5,1},{6,2},{7,3},{8,12},{9,13},{10,... | collective-permute-start | bytes 159752 | tf_op jit(solution)/shard_map/ppermute | solution.py:44
  48.7 4.2 %collective-permute-start.8 = (f32[104,128]{1,0:T(8,128)S(1)}, f32[104,128]{1,0:T(8,128)S(1)}, u32[]{:S(2)}, u32[]{:S(2)}) collective-permute-start(f32[104,128]{1,0:T(8,128)S(1)} %add.3.refs_0_), channel_id=1, source_target_pairs={{0,2},{1,3},{2,0},{3,1},{4,6},{5,7},{6,4},{7,5},{8,10},{9,11},{10,... | collective-permute-start | bytes 159752 | tf_op jit(solution)/shard_map/ppermute | solution.py:44
